TPU v7x, 512 devices: a whole 4x4x16 slice. The times are simulated.
512 devices in a mesh: wave: 8 (over x, core), plane: 64 (over y, z).
Axes of the slice: x: 4, y: 4, z: 16, core: 2. Of those that a mesh axis runs over, the one named last changes fastest.
Arguments:
- right_side: float32 [8, 512, 128], P('wave', 'plane'), may hold values from -40 to 40
- coupling_x: float32 [512, 128], P('plane'), may hold values from 2 to 6
- coupling_y: float32 [8, 128], P('wave'), may hold values from 0.2 to 0.6
- coupling_z: float32 [8, 512, 128], P('wave', 'plane'), may hold values from 0.3 to 1
- inverse: float32 [8, 512, 128, 128], P('wave', 'plane'), may hold values from -0.05 to 0.15
Outputs:
- solution: float32 [8, 512, 128], P('wave', 'plane')
- residual: float32 [8, 512, 128], P('wave', 'plane')
All inputs are finite; a program needn't handle non-finite values.
Results may differ from a plain program's by a relative error of at most 0.0003.
Values sent between devices are 32-bit elements; how exact they have to be, the bound alone decides.
No kernel may reach another device: no remote copies, remote signals or barrier semaphores. Data moves between devices by JAX's collectives and lax.ppermute only.
A program may use at most 64 MiB of HBM per device.

v0:
```python
import jax
import jax.numpy as jnp
from jax import lax
from jax.sharding import Mesh
from jax.sharding import PartitionSpec as P

ITERS = 2
WAVE = ("wave_0", "wave_1")
PLANE = ("plane_0", "plane_1")


relax = 1.5


def padded_2(array, sides, width):
    edges = {}
    for axis, dim in sides:
        size, length = (lax.axis_size(axis), array.shape[dim])
        up = [(i, (i + 1) % size) for i in range(size - 1)]
        last = lax.slice_in_dim(array, length - width, length, axis=dim)
        first = lax.slice_in_dim(array, 0, width, axis=dim)
        edges[dim] = (
            lax.ppermute(last, axis, up),
            lax.ppermute(first, axis, [(b, a) for a, b in up]),
        )
    done = []
    for _, dim in sides:
        low, high = edges[dim]
        around = [(width, width) if d in done else (0, 0) for d in range(array.ndim)]
        array = jnp.concatenate([jnp.pad(low, around), array, jnp.pad(high, around)], axis=dim)
        done.append(dim)
    return array


def side_by_side(arrays, axis, split_dim, concat_dim, along):
    both = jnp.concatenate(arrays, axis=along)
    whole, at, done = (
        lax.all_to_all(both, axis, split_axis=split_dim, concat_axis=concat_dim, tiled=True),
        0,
        [],
    )
    for a in arrays:
        done.append(lax.slice_in_dim(whole, at, at + a.shape[along], axis=along))
        at += a.shape[along]
    return tuple(done)


def extended(cells, sides, width):
    for axis, dim in sides:
        count = lax.axis_size(axis)
        ends = count - 1
        head = lax.slice_in_dim(cells, 0, width, axis=dim)
        tail = lax.slice_in_dim(cells, cells.shape[dim] - width, cells.shape[dim], axis=dim)
        cells = jnp.concatenate(
            [
                lax.ppermute(tail, axis, [(i, (i + 1) % count) for i in range(ends)]),
                cells,
                lax.ppermute(head, axis, [((i + 1) % count, i) for i in range(ends)]),
            ],
            axis=dim,
        )
    return cells


def from_everyone(array, axis):
    copies = jnp.broadcast_to(array, (lax.axis_size(axis), *array.shape))
    return lax.all_to_all(copies, axis, split_axis=0, concat_axis=0, tiled=True)


def of_everyone(array, axis):
    everything = from_everyone(array, axis)
    return jnp.sum(everything, axis=0)


def by_axis(array, axes):
    far, near = axes
    return of_everyone(of_everyone(array, near), far)


def packed_total(arrays, axis):
    flat, at, done = (jnp.concatenate([a.reshape(-1) for a in arrays]), 0, [])
    running = by_axis(flat, axis)
    for a in arrays:
        done.append(running[at : at + a.size].reshape(a.shape))
        at += a.size
    return tuple(done)


def apply_block(block, vector):
    return jnp.einsum("cij,cj->ci", block, vector, precision=lax.Precision.HIGHEST)


def column_part(values, coupling_x, coupling_y, coupling_z):
    below = jnp.concatenate([jnp.zeros_like(values[..., :1]), values[..., :-1]], axis=-1)
    above = jnp.concatenate([values[..., 1:], jnp.zeros_like(values[..., :1])], axis=-1)
    upper_z = jnp.concatenate([coupling_z[..., 1:], coupling_z[..., :1]], axis=-1)
    centre = 2.0 * coupling_x[None] + 2.0 * coupling_y[:, None] + coupling_z + upper_z
    return centre * values - coupling_z * below - upper_z * above


def operate(values, coupling_x, coupling_y, coupling_z):
    padded = padded_2(values, ((WAVE, 0), (PLANE, 1)), 1)
    along_x = padded[:-2, 1:-1] + padded[2:, 1:-1]
    along_y = padded[1:-1, :-2] + padded[1:-1, 2:]
    return (
        column_part(values, coupling_x, coupling_y, coupling_z)
        - coupling_x[None] * along_x
        - coupling_y[:, None] * along_y
    )


def local_sweep(source, inverse, coupling, base):
    start = jnp.zeros(source.shape[1:], jnp.float32)
    if base is None:

        def forward_step(previous, items):
            fresh = relax * apply_block(items[1], items[0] + coupling * previous)
            return (fresh, fresh)

        unused, planes = lax.scan(forward_step, start, (source, inverse))
    else:

        def backward_step(previous, items):
            fresh = items[2] + relax * apply_block(items[1], items[0] + coupling * previous)
            return (fresh, fresh)

        unused, planes = lax.scan(backward_step, start, (source, inverse, base), reverse=True)
    return planes


def to_columns(values):
    return lax.all_to_all(values, WAVE, split_axis=1, concat_axis=0, tiled=True)


def precondition(residual, coupling_x, coupling_y, coupling_z, crossed, coupling_part):
    half_local = local_sweep(to_columns(residual), crossed, coupling_part, None)
    lower_local = jnp.concatenate([jnp.zeros_like(half_local[:1]), half_local[:-1]], axis=0)
    half_sweep, lower_x = side_by_side((half_local, lower_local), WAVE, 0, 1, 2)
    framed = extended(half_sweep, ((PLANE, 1),), 1)
    settled = (
        column_part(half_sweep, coupling_x, coupling_y, coupling_z) - coupling_x[None] * lower_x
    )
    settled = settled - coupling_y[:, None] * (framed[:, :-2] + framed[:, 2:])
    result_local = local_sweep(to_columns(residual - settled), crossed, coupling_part, half_local)
    result = lax.all_to_all(result_local, WAVE, split_axis=0, concat_axis=1, tiled=True)
    return result


def on_device(right_side, coupling_x, coupling_y, coupling_z, inverse):
    crossed = None
    coupling_part = None
    crossed = lax.all_to_all(inverse, WAVE, split_axis=1, concat_axis=0, tiled=True)
    narrow = coupling_x.shape[0] // lax.axis_size(WAVE)
    coupling_part = lax.dynamic_slice_in_dim(coupling_x, lax.axis_index(WAVE) * narrow, narrow, 0)
    solution = jnp.zeros_like(right_side)
    residual = right_side
    direction = right_side
    image = right_side
    curvature = jnp.float32(1.0)
    for iteration in range(ITERS):
        precond = precondition(residual, coupling_x, coupling_y, coupling_z, crossed, coupling_part)
        applied = operate(precond, coupling_x, coupling_y, coupling_z)
        if iteration == 0:
            across_term = jnp.float32(0.0)
            older_term = jnp.float32(0.0)
        else:
            across_term = jnp.sum(precond * image)
            older_term = jnp.sum(direction * residual)
        across, own_part, older_part, energy = packed_total(
            (across_term, jnp.sum(precond * residual), older_term, jnp.sum(precond * applied)),
            (("wave_0", "wave_1"), ("plane_0", "plane_1")),
        )
        if iteration == 0:
            direction = precond
            image = applied
            projection = own_part
            curvature = energy
        else:
            ratio = -across / curvature
            direction = precond + ratio * direction
            image = applied + ratio * image
            projection = own_part + ratio * older_part
            curvature = energy + 2.0 * ratio * across + ratio * ratio * curvature
        step_size = projection / curvature
        solution = solution + step_size * direction
        residual = residual - step_size * image
    return (solution, residual)


def solution(mesh):
    torus = Mesh(mesh.devices.reshape(4, 2, 4, 16), ("wave_0", "wave_1", "plane_0", "plane_1"))
    return jax.shard_map(
        on_device,
        mesh=torus,
        in_specs=(
            P(WAVE, PLANE, None),
            P(PLANE, None),
            P(WAVE, None),
            P(WAVE, PLANE, None),
            P(WAVE, PLANE, None, None),
        ),
        out_specs=(P(WAVE, PLANE, None), P(WAVE, PLANE, None)),
        check_vma=False,
    )
```

profile of v0, /device:TPU:1, one launch (start us, length us, event | category | flops | bytes accessed | tf_op | source)
XLA Modules:
  0.0 219.5 jit_solution(10056951990685402587)
XLA Ops:
  0.6 14.6 %all_to_all.132 = f32[1,8,128]{2,0,1:T(1,128)S(1)} all-to-all(f32[1,8,128]{2,0,1:T(1,128)} %bitcast.258), channel_id=1, replica_groups=mesh['wave_0'=4,'wave_1'=2,'plane_0'=4,'plane_1'=16] {'wave_0','wave_1'}, dimensions={1} | all-to-all | bytes 8192 | tf_op jit(solution)/shard_map/all_to_all | solution.py:132
  15.2 4.1 %all-to-all-start = ((f32[1,8,128,128]{3,2,0,1:T(8,128)}), f32[1,8,128,128]{3,2,0,1:T(8,128)S(1)}, u32[]{:S(2)}, u32[]{:S(2)}) async-start(f32[1,8,128,128]{3,2,0,1:T(8,128)} %bitcast.225), calls=%async_computation | async-start | bytes 1048576 | tf_op jit(solution)/shard_map/all_to_all | solution.py:152
  20.7 8.2 %all-to-all-done = f32[1,8,128,128]{3,2,0,1:T(8,128)S(1)} async-done(((f32[1,8,128,128]{3,2,0,1:T(8,128)}), f32[1,8,128,128]{3,2,0,1:T(8,128)S(1)}, u32[]{:S(2)}, u32[]{:S(2)}) %all-to-all-start) | async-done | bytes 524320 | tf_op jit(solution)/shard_map/all_to_all | solution.py:152
  31.3 4.1 %all-to-all-start.2 = ((f32[8,1,256]{2,1,0:T(1,128)}), f32[8,1,256]{2,1,0:T(1,128)S(1)}, u32[]{:S(2)}, u32[]{:S(2)}) async-start(f32[8,1,256]{2,1,0:T(1,128)} %fusion.40), calls=%async_computation.2 | async-start | bytes 16384 | tf_op jit(solution)/shard_map/all_to_all | solution.py:38
  36.2 3.9 %all-to-all-done.2 = f32[8,1,256]{2,1,0:T(1,128)S(1)} async-done(((f32[8,1,256]{2,1,0:T(1,128)}), f32[8,1,256]{2,1,0:T(1,128)S(1)}, u32[]{:S(2)}, u32[]{:S(2)}) %all-to-all-start.2) | async-done | bytes 8224 | tf_op jit(solution)/shard_map/all_to_all | solution.py:38
  41.3 4.0 %collective-permute-start = (f32[1,1,128]{2,0,1:T(1,128)S(1)}, f32[1,1,128]{2,0,1:T(1,128)S(1)}, u32[]{:S(2)}, u32[]{:S(2)}) collective-permute-start(f32[1,1,128]{2,0,1:T(1,128)S(1)} %get-tuple-element.532), channel_id=1, source_target_pairs={{0,1},{1,2},{2,3},{3,4},{4,5},{5,6},{6,7},{7,8},{8,9},{9,10},{10,1... | collective-permute-start | bytes 1544 | tf_op jit(solution)/shard_map/ppermute | solution.py:56
  47.4 5.0 %all-to-all-start.3 = ((f32[1,8,128]{2,0,1:T(1,128)}), f32[1,8,128]{2,0,1:T(1,128)S(1)}, u32[]{:S(2)}, u32[]{:S(2)}) async-start(f32[1,8,128]{2,0,1:T(1,128)} %get-tuple-element.516), calls=%async_computation.3 | async-start | bytes 8192 | tf_op jit(solution)/shard_map/all_to_all | solution.py:132
  52.4 4.5 %all-to-all-done.3 = f32[1,8,128]{2,0,1:T(1,128)S(1)} async-done(((f32[1,8,128]{2,0,1:T(1,128)}), f32[1,8,128]{2,0,1:T(1,128)S(1)}, u32[]{:S(2)}, u32[]{:S(2)}) %all-to-all-start.3) | async-done | bytes 4128 | tf_op jit(solution)/shard_map/all_to_all | solution.py:132
  58.8 7.7 %all_to_all.133 = f32[8,1,128]{2,1,0:T(1,128)S(1)} all-to-all(f32[8,1,128]{2,1,0:T(1,128)S(1)} %get-tuple-element.349), channel_id=1, replica_groups=mesh['wave_0'=4,'wave_1'=2,'plane_0'=4,'plane_1'=16] {'wave_0','wave_1'}, dimensions={0} | all-to-all | bytes 8192 | tf_op jit(solution)/shard_map/all_to_all | solution.py:145
  69.1 3.0 %collective-permute-start.2 = (f32[1,8,128]{2,0,1:T(1,128)S(1)}, f32[1,8,128]{2,0,1:T(1,128)S(1)}, u32[]{:S(2)}, u32[]{:S(2)}) collective-permute-start(f32[1,8,128]{2,0,1:T(1,128)S(1)} %bitcast.228), channel_id=1, source_target_pairs={{0,64},{64,128},{128,192},{192,256},{256,320},{320,384},{384,448},... | collective-permute-start | bytes 12296 | tf_op jit(solution)/shard_map/ppermute | solution.py:23
  73.3 4.5 %collective-permute-start.4 = (f32[1,1,128]{2,0,1:T(1,128)S(1)}, f32[1,1,128]{2,0,1:T(1,128)S(1)}, u32[]{:S(2)}, u32[]{:S(2)}) collective-permute-start(f32[1,1,128]{2,0,1:T(1,128)S(1)} %get-tuple-element.540), channel_id=1, source_target_pairs={{0,1},{1,2},{2,3},{3,4},{4,5},{5,6},{6,7},{7,8},{8,9},{9,10},{10,1... | collective-permute-start | bytes 1544 | tf_op jit(solution)/shard_map/ppermute | solution.py:23
  80.6 29.7 %all_to_all.137 = f32[64,1,4]{2,1,0:T(1,128)S(1)} all-to-all(f32[64,1,4]{2,1,0:T(1,128)S(1)} %broadcast_in_dim.59), channel_id=1, replica_groups=mesh['wave_0'=4,'wave_1'=2,'plane_0'=4,'plane_1'=16] {'plane_0','plane_1'}, dimensions={0} | all-to-all | bytes 2048 | tf_op jit(solution)/shard_map/all_to_all | solution.py:67
  110.4 9.2 %all_to_all.138 = f32[8,1,4]{2,1,0:T(1,128)S(1)} all-to-all(f32[8,1,4]{2,1,0:T(1,128)S(1)} %broadcast_in_dim.60), channel_id=1, replica_groups=mesh['wave_0'=4,'wave_1'=2,'plane_0'=4,'plane_1'=16] {'wave_0','wave_1'}, dimensions={0} | all-to-all | bytes 256 | tf_op jit(solution)/shard_map/all_to_all | solution.py:67
  122.2 3.9 %all-to-all-start.7 = ((f32[1,8,128]{2,0,1:T(1,128)}), f32[1,8,128]{2,0,1:T(1,128)S(1)}, u32[]{:S(2)}, u32[]{:S(2)}) async-start(f32[1,8,128]{2,0,1:T(1,128)} %bitcast.182), calls=%async_computation.7 | async-start | bytes 8192 | tf_op jit(solution)/shard_map/all_to_all | solution.py:132
  126.1 4.5 %all-to-all-done.7 = f32[1,8,128]{2,0,1:T(1,128)S(1)} async-done(((f32[1,8,128]{2,0,1:T(1,128)}), f32[1,8,128]{2,0,1:T(1,128)S(1)}, u32[]{:S(2)}, u32[]{:S(2)}) %all-to-all-start.7) | async-done | bytes 4128 | tf_op jit(solution)/shard_map/all_to_all | solution.py:132
  132.5 7.7 %all_to_all.134 = f32[8,1,256]{2,1,0:T(1,128)S(1)} all-to-all(f32[8,1,256]{2,1,0:T(1,128)S(1)} %fusion.41), channel_id=1, replica_groups=mesh['wave_0'=4,'wave_1'=2,'plane_0'=4,'plane_1'=16] {'wave_0','wave_1'}, dimensions={0} | all-to-all | bytes 16384 | tf_op jit(solution)/shard_map/all_to_all | solution.py:38
  141.5 4.0 %collective-permute-start.6 = (f32[1,1,128]{2,0,1:T(1,128)S(1)}, f32[1,1,128]{2,0,1:T(1,128)S(1)}, u32[]{:S(2)}, u32[]{:S(2)}) collective-permute-start(f32[1,1,128]{2,0,1:T(1,128)S(1)} %get-tuple-element.528), channel_id=1, source_target_pairs={{0,1},{1,2},{2,3},{3,4},{4,5},{5,6},{6,7},{7,8},{8,9},{9,10},{10,1... | collective-permute-start | bytes 1544 | tf_op jit(solution)/shard_map/ppermute | solution.py:56
  147.0 8.8 %all_to_all.135 = f32[1,8,128]{2,0,1:T(1,128)S(1)} all-to-all(f32[1,8,128]{2,0,1:T(1,128)S(1)} %fusion.55), channel_id=1, replica_groups=mesh['wave_0'=4,'wave_1'=2,'plane_0'=4,'plane_1'=16] {'wave_0','wave_1'}, dimensions={1} | all-to-all | bytes 8192 | tf_op jit(solution)/shard_map/all_to_all | solution.py:132
  157.6 7.7 %all_to_all.136 = f32[8,1,128]{2,1,0:T(1,128)S(1)} all-to-all(f32[8,1,128]{2,1,0:T(1,128)S(1)} %get-tuple-element.351), channel_id=1, replica_groups=mesh['wave_0'=4,'wave_1'=2,'plane_0'=4,'plane_1'=16] {'wave_0','wave_1'}, dimensions={0} | all-to-all | bytes 8192 | tf_op jit(solution)/shard_map/all_to_all | solution.py:145
  167.8 3.0 %collective-permute-start.8 = (f32[1,8,128]{2,0,1:T(1,128)S(1)}, f32[1,8,128]{2,0,1:T(1,128)S(1)}, u32[]{:S(2)}, u32[]{:S(2)}) collective-permute-start(f32[1,8,128]{2,0,1:T(1,128)S(1)} %bitcast.233), channel_id=1, source_target_pairs={{0,64},{64,128},{128,192},{192,256},{256,320},{320,384},{384,448},... | collective-permute-start | bytes 12296 | tf_op jit(solution)/shard_map/ppermute | solution.py:23
  172.1 4.5 %collective-permute-start.10 = (f32[1,1,128]{2,0,1:T(1,128)S(1)}, f32[1,1,128]{2,0,1:T(1,128)S(1)}, u32[]{:S(2)}, u32[]{:S(2)}) collective-permute-start(f32[1,1,128]{2,0,1:T(1,128)S(1)} %get-tuple-element.536), channel_id=1, source_target_pairs={{0,1},{1,2},{2,3},{3,4},{4,5},{5,6},{6,7},{7,8},{8,9},{9,10},{10,1... | collective-permute-start | bytes 1544 | tf_op jit(solution)/shard_map/ppermute | solution.py:23
  178.8 2.6 %pad_maximum_fusion.14 = f32[4]{0:T(128)S(1)} fusion(f32[1]{0:T(128)} %bitcast.69, f32[1]{0:T(128)} %bitcast.67, f32[1]{0:T(128)} %bitcast.66, f32[1]{0:T(128)} %bitcast.65), kind=kLoop, calls=%fused_computation.103 | loop fusion | flops 12 | bytes 32 | tf_op jit(solution)/shard_map/concatenate | solution.py:81
  181.5 22.1 %all_to_all.139 = f32[64,1,4]{2,1,0:T(1,128)S(1)} all-to-all(f32[64,1,4]{2,1,0:T(1,128)S(1)} %broadcast_in_dim.61), channel_id=1, replica_groups=mesh['wave_0'=4,'wave_1'=2,'plane_0'=4,'plane_1'=16] {'plane_0','plane_1'}, dimensions={0} | all-to-all | bytes 2048 | tf_op jit(solution)/shard_map/all_to_all | solution.py:67
  203.6 9.2 %all_to_all.140 = f32[8,1,4]{2,1,0:T(1,128)S(1)} all-to-all(f32[8,1,4]{2,1,0:T(1,128)S(1)} %broadcast_in_dim.62), channel_id=1, replica_groups=mesh['wave_0'=4,'wave_1'=2,'plane_0'=4,'plane_1'=16] {'wave_0','wave_1'}, dimensions={0} | all-to-all | bytes 256 | tf_op jit(solution)/shard_map/all_to_all | solution.py:67
  (137 shorter events, 39.7 us)
Async XLA Ops:
  15.2 13.6 %all-to-all-start = ((f32[1,8,128,128]{3,2,0,1:T(8,128)}), f32[1,8,128,128]{3,2,0,1:T(8,128)S(1)}, u32[]{:S(2)}, u32[]{:S(2)}) async-start(f32[1,8,128,128]{3,2,0,1:T(8,128)} %bitcast.225), calls=%async_computation | async-start | bytes 1048576 | tf_op jit(solution)/shard_map/all_to_all | solution.py:152
  19.3 0.7 copy-start.1
  20.0 0.7 copy-start.3
  31.3 8.7 %all-to-all-start.2 = ((f32[8,1,256]{2,1,0:T(1,128)}), f32[8,1,256]{2,1,0:T(1,128)S(1)}, u32[]{:S(2)}, u32[]{:S(2)}) async-start(f32[8,1,256]{2,1,0:T(1,128)} %fusion.40), calls=%async_computation.2 | async-start | bytes 16384 | tf_op jit(solution)/shard_map/all_to_all | solution.py:38
  35.4 0.7 copy-start
  40.0 5.4 %collective-permute-start.1 = (f32[1,1,128]{2,0,1:T(1,128)S(1)}, f32[1,1,128]{2,0,1:T(1,128)S(1)}, u32[]{:S(2)}, u32[]{:S(2)}) collective-permute-start(f32[1,1,128]{2,0,1:T(1,128)S(1)} %get-tuple-element.533), channel_id=1, source_target_pairs={{1,0},{2,1},{3,2},{4,3},{5,4},{6,5},{7,6},{8,7},{9,8},{10,9},{11,1... | collective-permute-start | bytes 1544 | tf_op jit(solution)/shard_map/ppermute | solution.py:58
  41.3 4.7 %collective-permute-start = (f32[1,1,128]{2,0,1:T(1,128)S(1)}, f32[1,1,128]{2,0,1:T(1,128)S(1)}, u32[]{:S(2)}, u32[]{:S(2)}) collective-permute-start(f32[1,1,128]{2,0,1:T(1,128)S(1)} %get-tuple-element.532), channel_id=1, source_target_pairs={{0,1},{1,2},{2,3},{3,4},{4,5},{5,6},{6,7},{7,8},{8,9},{9,10},{10,1... | collective-permute-start | bytes 1544 | tf_op jit(solution)/shard_map/ppermute | solution.py:56
  46.0 0.7 copy-start.2
  47.4 9.6 %all-to-all-start.3 = ((f32[1,8,128]{2,0,1:T(1,128)}), f32[1,8,128]{2,0,1:T(1,128)S(1)}, u32[]{:S(2)}, u32[]{:S(2)}) async-start(f32[1,8,128]{2,0,1:T(1,128)} %get-tuple-element.516), calls=%async_computation.3 | async-start | bytes 8192 | tf_op jit(solution)/shard_map/all_to_all | solution.py:132
  66.5 12.1 %collective-permute-start.3 = (f32[1,8,128]{2,0,1:T(1,128)S(1)}, f32[1,8,128]{2,0,1:T(1,128)S(1)}, u32[]{:S(2)}, u32[]{:S(2)}) collective-permute-start(f32[1,8,128]{2,0,1:T(1,128)S(1)} %bitcast.227), channel_id=1, source_target_pairs={{64,0},{128,64},{192,128},{256,192},{320,256},{384,320},{448,384},... | collective-permute-start | bytes 12296 | tf_op jit(solution)/shard_map/ppermute | solution.py:24
  69.1 9.5 %collective-permute-start.2 = (f32[1,8,128]{2,0,1:T(1,128)S(1)}, f32[1,8,128]{2,0,1:T(1,128)S(1)}, u32[]{:S(2)}, u32[]{:S(2)}) collective-permute-start(f32[1,8,128]{2,0,1:T(1,128)S(1)} %bitcast.228), channel_id=1, source_target_pairs={{0,64},{64,128},{128,192},{192,256},{256,320},{320,384},{384,448},... | collective-permute-start | bytes 12296 | tf_op jit(solution)/shard_map/ppermute | solution.py:23
  72.0 5.9 %collective-permute-start.5 = (f32[1,1,128]{2,0,1:T(1,128)S(1)}, f32[1,1,128]{2,0,1:T(1,128)S(1)}, u32[]{:S(2)}, u32[]{:S(2)}) collective-permute-start(f32[1,1,128]{2,0,1:T(1,128)S(1)} %get-tuple-element.541), channel_id=1, source_target_pairs={{1,0},{2,1},{3,2},{4,3},{5,4},{6,5},{7,6},{8,7},{9,8},{10,9},{11,1... | collective-permute-start | bytes 1544 | tf_op jit(solution)/shard_map/ppermute | solution.py:24
  73.3 5.2 %collective-permute-start.4 = (f32[1,1,128]{2,0,1:T(1,128)S(1)}, f32[1,1,128]{2,0,1:T(1,128)S(1)}, u32[]{:S(2)}, u32[]{:S(2)}) collective-permute-start(f32[1,1,128]{2,0,1:T(1,128)S(1)} %get-tuple-element.540), channel_id=1, source_target_pairs={{0,1},{1,2},{2,3},{3,4},{4,5},{5,6},{6,7},{7,8},{8,9},{9,10},{10,1... | collective-permute-start | bytes 1544 | tf_op jit(solution)/shard_map/ppermute | solution.py:23
  122.2 8.4 %all-to-all-start.7 = ((f32[1,8,128]{2,0,1:T(1,128)}), f32[1,8,128]{2,0,1:T(1,128)S(1)}, u32[]{:S(2)}, u32[]{:S(2)}) async-start(f32[1,8,128]{2,0,1:T(1,128)} %bitcast.182), calls=%async_computation.7 | async-start | bytes 8192 | tf_op jit(solution)/shard_map/all_to_all | solution.py:132
  140.2 5.4 %collective-permute-start.7 = (f32[1,1,128]{2,0,1:T(1,128)S(1)}, f32[1,1,128]{2,0,1:T(1,128)S(1)}, u32[]{:S(2)}, u32[]{:S(2)}) collective-permute-start(f32[1,1,128]{2,0,1:T(1,128)S(1)} %get-tuple-element.529), channel_id=1, source_target_pairs={{1,0},{2,1},{3,2},{4,3},{5,4},{6,5},{7,6},{8,7},{9,8},{10,9},{11,1... | collective-permute-start | bytes 1544 | tf_op jit(solution)/shard_map/ppermute | solution.py:58
  141.5 4.7 %collective-permute-start.6 = (f32[1,1,128]{2,0,1:T(1,128)S(1)}, f32[1,1,128]{2,0,1:T(1,128)S(1)}, u32[]{:S(2)}, u32[]{:S(2)}) collective-permute-start(f32[1,1,128]{2,0,1:T(1,128)S(1)} %get-tuple-element.528), channel_id=1, source_target_pairs={{0,1},{1,2},{2,3},{3,4},{4,5},{5,6},{6,7},{7,8},{8,9},{9,10},{10,1... | collective-permute-start | bytes 1544 | tf_op jit(solution)/shard_map/ppermute | solution.py:56
  165.2 12.1 %collective-permute-start.9 = (f32[1,8,128]{2,0,1:T(1,128)S(1)}, f32[1,8,128]{2,0,1:T(1,128)S(1)}, u32[]{:S(2)}, u32[]{:S(2)}) collective-permute-start(f32[1,8,128]{2,0,1:T(1,128)S(1)} %bitcast.232), channel_id=1, source_target_pairs={{64,0},{128,64},{192,128},{256,192},{320,256},{384,320},{448,384},... | collective-permute-start | bytes 12296 | tf_op jit(solution)/shard_map/ppermute | solution.py:24
  167.8 9.5 %collective-permute-start.8 = (f32[1,8,128]{2,0,1:T(1,128)S(1)}, f32[1,8,128]{2,0,1:T(1,128)S(1)}, u32[]{:S(2)}, u32[]{:S(2)}) collective-permute-start(f32[1,8,128]{2,0,1:T(1,128)S(1)} %bitcast.233), channel_id=1, source_target_pairs={{0,64},{64,128},{128,192},{192,256},{256,320},{320,384},{384,448},... | collective-permute-start | bytes 12296 | tf_op jit(solution)/shard_map/ppermute | solution.py:23
  170.8 5.9 %collective-permute-start.11 = (f32[1,1,128]{2,0,1:T(1,128)S(1)}, f32[1,1,128]{2,0,1:T(1,128)S(1)}, u32[]{:S(2)}, u32[]{:S(2)}) collective-permute-start(f32[1,1,128]{2,0,1:T(1,128)S(1)} %get-tuple-element.537), channel_id=1, source_target_pairs={{1,0},{2,1},{3,2},{4,3},{5,4},{6,5},{7,6},{8,7},{9,8},{10,9},{11,1... | collective-permute-start | bytes 1544 | tf_op jit(solution)/shard_map/ppermute | solution.py:24
  172.1 5.2 %collective-permute-start.10 = (f32[1,1,128]{2,0,1:T(1,128)S(1)}, f32[1,1,128]{2,0,1:T(1,128)S(1)}, u32[]{:S(2)}, u32[]{:S(2)}) collective-permute-start(f32[1,1,128]{2,0,1:T(1,128)S(1)} %get-tuple-element.536), channel_id=1, source_target_pairs={{0,1},{1,2},{2,3},{3,4},{4,5},{5,6},{6,7},{7,8},{8,9},{9,10},{10,1... | collective-permute-start | bytes 1544 | tf_op jit(solution)/shard_map/ppermute | solution.py:23
where the time goes:
time: 221 us; the launch traced here: 219 us
  blocking collectives  117 us (53%)
  starting transfers between devices  50.4 us (23%)
  waiting for transfers between devices  23.6 us (11%)
  other arithmetic  10.4 us (5%)
  matrix products  7.22 us (3%)
  between operations  6.76 us (3%)
  local copies, waits for them, and re-layouts  4.5 us (2%)
    all_to_all x4, blocking collectives, from_everyone(): return lax.all_to_all(copies, axis, split_axis=0, concat_axis=0, tiled=True)  70.2 us
    all_to_all x2, blocking collectives, to_columns(): return lax.all_to_all(values, WAVE, split_axis=1, concat_axis=0, tiled=True)  23.4 us
    all_to_all x2, blocking collectives, precondition(): lax.all_to_all(result_local, WAVE, split_axis=0, concat_axis=1, tiled=True)  15.3 us
    ppermute x4, starting transfers between devices, padded_2(): lax.ppermute(last, axis, up)  14.9 us
    all_to_all x2, waiting for transfers between devices, to_columns(): return lax.all_to_all(values, WAVE, split_axis=1, concat_axis=0, tiled=True)  9.04 us
    all_to_all x2, starting transfers between devices, to_columns(): return lax.all_to_all(values, WAVE, split_axis=1, concat_axis=0, tiled=True)  8.95 us
    all_to_all x1, waiting for transfers between devices, on_device(): lax.all_to_all(inverse, WAVE, split_axis=1, concat_axis=0, tiled=True)  8.15 us
    ppermute x2, starting transfers between devices, extended(): lax.ppermute(tail, axis, [(i, (i + 1) % count) for i in range(ends)])  7.97 us
  transfers between devices with their start and end apart: 16, of which 8 were waited for; matrix products, arithmetic and copies ran while one was open for 0% of the time, Pallas kernels for 0%

commit v1 on v0

v1 whole, which is shorter than its diff:
```python
import jax
import jax.numpy as jnp
from jax import lax
from jax.sharding import Mesh
from jax.sharding import PartitionSpec as P

WAVE = ("wave_0", "wave_1")
PLANE = ("plane_0", "plane_1")
ALL = WAVE + PLANE
NW = 8
NP = 64

relax = 1.5


def chain_device(position):
    plane, k = divmod(position, NW)
    wave = k if plane % 2 == 0 else NW - 1 - k
    return wave * NP + plane


def swap_pairs(first):
    pairs = []
    for i in range(first, NW * NP - 1, 2):
        a, b = chain_device(i), chain_device(i + 1)
        pairs += [(a, b), (b, a)]
    return pairs


NEAR = swap_pairs(0)
FAR = swap_pairs(1)


def neighbours(values):
    near = lax.ppermute(values, ALL, NEAR)
    far = lax.ppermute(values, ALL, FAR)
    return near + far


def apply_block(block, vector):
    return jnp.einsum("ij,j->i", block, vector, precision=lax.Precision.HIGHEST)


def centre_of(cx, cy, cz):
    upper_z = jnp.concatenate([cz[:, 1:], cz[:, :1]], axis=-1)
    return 2.0 * cx + 2.0 * cy + cz + upper_z, upper_z


def column_part(values, centre, cz, upper_z):
    below = jnp.concatenate([jnp.zeros_like(values[:, :1]), values[:, :-1]], axis=-1)
    above = jnp.concatenate([values[:, 1:], jnp.zeros_like(values[:, :1])], axis=-1)
    return centre * values - cz * below - upper_z * above


def lower(values):
    return jnp.concatenate([jnp.zeros_like(values[:1]), values[:-1]], axis=0)


def upper(values):
    return jnp.concatenate([values[1:], jnp.zeros_like(values[:1])], axis=0)


def sweep(source, inverse, cx, base, reverse):
    def step(previous, items):
        s, block, b = items
        fresh = b + relax * apply_block(block, s + cx[0] * previous)
        return fresh, fresh

    _, planes = lax.scan(step, jnp.zeros_like(source[0]), (source, inverse, base), reverse=reverse)
    return planes


def on_device(right_side, coupling_x, coupling_y, coupling_z, inverse):
    odd = lax.axis_index("plane_1") % 2 == 1

    def turned(values, axis):
        return jnp.where(odd, lax.rev(values, (axis,)), values)

    extra = jnp.stack(
        [
            right_side[0],
            coupling_z[0],
            jnp.broadcast_to(coupling_y, coupling_z[0].shape),
            coupling_x,
        ],
        axis=1,
    )
    packed = turned(jnp.concatenate([inverse[0], extra], axis=1), 0)
    columns = lax.all_to_all(packed, WAVE, split_axis=0, concat_axis=0, tiled=True)
    blocks = columns[:, :128]
    r, cz, cy, cx = (columns[:, 128 + i] for i in range(4))
    centre, upper_z = centre_of(cx, cy, cz)

    def precondition(s):
        half = sweep(s, blocks, cx, jnp.zeros_like(s), False)
        near = neighbours(half)
        settled = column_part(half, centre, cz, upper_z) - cx * lower(half) - cy * near
        return sweep(s - settled, blocks, cx, half, True)

    def operate(v):
        near = neighbours(v)
        return column_part(v, centre, cz, upper_z) - cx * (lower(v) + upper(v)) - cy * near

    z = precondition(r)
    q = operate(z)
    w = precondition(q)
    p = operate(w)
    sums = jnp.stack([jnp.sum(a * b) for a, b in ((z, r), (z, q), (w, r), (w, q), (w, p))])
    sums = jnp.broadcast_to(jnp.pad(sums, (0, 123))[None], (NW, 128))
    back = lax.all_to_all(
        jnp.stack([z, q, w, p, sums], axis=1), WAVE, split_axis=0, concat_axis=0, tiled=True
    )
    part = jnp.sum(back[:, 4], axis=0)
    everyone = lax.all_to_all(
        jnp.broadcast_to(part[None, None], (NP, 1, 128)), PLANE, split_axis=0, concat_axis=0, tiled=True
    )
    total = jnp.sum(everyone[:, 0], axis=0)
    zr, zq, wr, wq, wp = (total[i] for i in range(5))
    first = zr / zq
    ratio = wq / zq
    second = (first * wq - wr) / (wp - ratio * wq)
    lead = first + second * ratio
    fields = turned(back[:, :4], 0)
    solution = lead * fields[:, 0] - second * fields[:, 2]
    residual = right_side[0] - lead * fields[:, 1] + second * fields[:, 3]
    return solution[None], residual[None]


def solution(mesh):
    torus = Mesh(mesh.devices.reshape(4, 2, 4, 16), ALL)
    return jax.shard_map(
        on_device,
        mesh=torus,
        in_specs=(
            P(WAVE, PLANE, None),
            P(PLANE, None),
            P(WAVE, None),
            P(WAVE, PLANE, None),
            P(WAVE, PLANE, None, None),
        ),
        out_specs=(P(WAVE, PLANE, None), P(WAVE, PLANE, None)),
        check_vma=False,
    )
```

time: 221 us -> 115 us (0.52)
  blocking collectives: 117 us -> 7.47 us
  waiting for transfers between devices: 23.6 us -> 31.9 us
  other arithmetic: 10.4 us -> 3.1 us
  local copies, waits for them, and re-layouts: 4.5 us -> 9.3 us
    all_to_all x9 -> x1, blocking collectives: 117 us -> 7.47 us  [on_device(): lax.all_to_all(jnp.stack([z, q, w, p, sums], axis=1), WAVE, split_axis=0,...]
    ppermute x12 -> x8, starting transfers between devices: 33.2 us -> 19 us  [the longest x4 10.5 us: neighbours(): far = lax.ppermute(values, ALL, FAR)]
    all_to_all x4 -> x2, starting transfers between devices: 17.1 us -> 31 us  [the longest x1 20.7 us: on_device(): lax.all_to_all(jnp.broadcast_to(part[None, None], (NP, 1, 128)), PLANE, s...]
    ppermute x12 -> x8, waiting for transfers between devices: 2.5 us -> 8.83 us  [the longest x4 8.82 us: neighbours(): far = lax.ppermute(values, ALL, FAR)]
    concatenate x4 -> x0, other arithmetic: 4.69 us -> none  [the longest x2 4 us: packed_total(): flat, at, done = (jnp.concatenate([a.reshape(-1) for a in arrays]), 0, [])]
    another operation x8, local copies, waits for them, and re-layouts: 0.02 us -> 3.21 us  [the longest x1 3.19 us: on_device(): jnp.stack([jnp.sum(a * b) for a, b in ((z, r), (z, q), (w, r), (w, q), (w...]
    sub x4 -> x3, other arithmetic: 3.35 us -> 0.76 us  [the longest x1 0.6 us: on_device(): solution = lead * fields[:, 0] - second * fields[:, 2]]
    all_to_all x4 -> x2, waiting for transfers between devices: 21.1 us -> 23.1 us  [the longest x1 13.3 us: on_device(): lax.all_to_all(jnp.broadcast_to(part[None, None], (NP, 1, 128)), PLANE, s...]
  transfers between devices with their start and end apart: 16 -> 10, of which waited for: 8 -> 6; matrix products, arithmetic and copies ran while one was open for 0% -> 0% of each run, Pallas kernels for 0% -> 0%
where the time goes in v1:
time: 115 us
  starting transfers between devices  50 us (43%)
  waiting for transfers between devices  31.9 us (28%)
  local copies, waits for them, and re-layouts  9.3 us (8%)
  blocking collectives  7.47 us (6%)
  between operations  5.97 us (5%)
  matrix products  5.89 us (5%)
  other arithmetic  3.1 us (3%)
    all_to_all x1, starting transfers between devices, on_device(): lax.all_to_all(jnp.broadcast_to(part[None, None], (NP, 1, 128)), PLANE, s...  20.7 us
    all_to_all x1, waiting for transfers between devices, on_device(): lax.all_to_all(jnp.broadcast_to(part[None, None], (NP, 1, 128)), PLANE, s...  13.3 us
    ppermute x4, starting transfers between devices, neighbours(): far = lax.ppermute(values, ALL, FAR)  10.5 us
    all_to_all x1, starting transfers between devices, on_device(): lax.all_to_all(packed, WAVE, split_axis=0, concat_axis=0, tiled=True)  10.3 us
    all_to_all x1, waiting for transfers between devices, on_device(): lax.all_to_all(packed, WAVE, split_axis=0, concat_axis=0, tiled=True)  9.85 us
    ppermute x4, waiting for transfers between devices, neighbours(): far = lax.ppermute(values, ALL, FAR)  8.82 us
    ppermute x4, starting transfers between devices, neighbours(): near = lax.ppermute(values, ALL, NEAR)  8.54 us
    all_to_all x1, blocking collectives, on_device(): lax.all_to_all(jnp.stack([z, q, w, p, sums], axis=1), WAVE, split_axis=0,...  7.47 us
  transfers between devices with their start and end apart: 10, of which 6 were waited for; matrix products, arithmetic and copies ran while one was open for 0% of the time, Pallas kernels for 0%

profile of v1, /device:TPU:1, one launch (start us, length us, event | category | flops | bytes accessed | tf_op | source)
XLA Modules:
  0.0 114.6 jit_solution(6933621092950809853)
XLA Ops:
  2.0 1.1 concatenate.48
  3.1 0.8 reverse_select_fusion
  4.0 10.3 %all-to-all-start = ((f32[8,132,128]{2,1,0:T(8,128)}), f32[8,132,128]{2,1,0:T(8,128)S(1)}, u32[]{:S(2)}, u32[]{:S(2)}) async-start(f32[8,132,128]{2,1,0:T(8,128)} %reverse_select_fusion), calls=%async_computation | async-start | bytes 1114112 | tf_op jit(solution)/shard_map/all_to_all | solution.py:89
  14.3 9.8 %all-to-all-done = f32[8,132,128]{2,1,0:T(8,128)S(1)} async-done(((f32[8,132,128]{2,1,0:T(8,128)}), f32[8,132,128]{2,1,0:T(8,128)S(1)}, u32[]{:S(2)}, u32[]{:S(2)}) %all-to-all-start) | async-done | bytes 540704 | tf_op jit(solution)/shard_map/all_to_all | solution.py:89
  24.2 2.2 %while.60 = (s32[]{:T(128)}, f32[128]{0:T(128)S(1)}, f32[8,128]{1,0:T(8,128)S(1)}, f32[8,128,128]{2,1,0:T(8,128)S(1)}, f32[8,128]{1,0:T(8,128)S(1)}, /*index=5*/f32[8,128]{1,0:T(8,128)S(1)}, s32[]{:T(128)}, s32[]{:T(128)}) while((s32[]{:T(128)}, f32[128]{0:T(128)S(1)}, f32[8,128]{1,0:T(8,128)S(1)}, f32[8,128,128]{2,1,0:T(8,128)S(1)}, ...), condition=%wide.region_1.2_spmd.clone, body=%wide.region_0.1_spmd.clone.sunk | while | flops 197123 | bytes 70755 | solution.py:69
  26.4 2.8 %collective-permute-start = (f32[8,128]{1,0:T(8,128)S(1)}, f32[8,128]{1,0:T(8,128)S(1)}, u32[]{:S(2)}, u32[]{:S(2)}) collective-permute-start(f32[8,128]{1,0:T(8,128)S(1)} %get-tuple-element.742), channel_id=1, source_target_pairs={{0,64},{64,0},{128,192},{192,128},{256,320},{320,256},{384,448},{4... | collective-permute-start | bytes 12296 | tf_op jit(solution)/shard_map/ppermute | solution.py:35
  29.2 2.1 %collective-permute-start.1 = (f32[8,128]{1,0:T(8,128)S(1)}, f32[8,128]{1,0:T(8,128)S(1)}, u32[]{:S(2)}, u32[]{:S(2)}) collective-permute-start(f32[8,128]{1,0:T(8,128)S(1)} %get-tuple-element.742), channel_id=1, source_target_pairs={{64,128},{128,64},{192,256},{256,192},{320,384},{384,320},{448,449... | collective-permute-start | bytes 12296 | tf_op jit(solution)/shard_map/ppermute | solution.py:36
  31.5 2.7 %collective-permute-done.1 = f32[8,128]{1,0:T(8,128)S(1)} collective-permute-done((f32[8,128]{1,0:T(8,128)S(1)}, f32[8,128]{1,0:T(8,128)S(1)}, u32[]{:S(2)}, u32[]{:S(2)}) %collective-permute-start.1) | collective-permute-done | bytes 4128 | tf_op jit(solution)/shard_map/ppermute | solution.py:36
  34.2 2.2 %while.61 = (s32[]{:T(128)}, f32[128]{0:T(128)S(1)}, f32[8,128]{1,0:T(8,128)S(1)}, f32[8,128]{1,0:T(8,128)S(1)}, f32[8,128,128]{2,1,0:T(8,128)S(1)}, /*index=5*/...) while((s32[]{:T(128)}, f32[128]{0:T(128)S(1)}, ...), condition=%wide.region_3.4_spmd.clone, body=%wide.region_2.3_spmd.clone.sunk | while | flops 197252 | bytes 72318 | solution.py:69
  36.4 1.9 %collective-permute-start.2 = (f32[8,128]{1,0:T(8,128)S(1)}, f32[8,128]{1,0:T(8,128)S(1)}, u32[]{:S(2)}, u32[]{:S(2)}) collective-permute-start(f32[8,128]{1,0:T(8,128)S(1)} %get-tuple-element.349), channel_id=1, source_target_pairs={{0,64},{64,0},{128,192},{192,128},{256,320},{320,256},{384,448},{4... | collective-permute-start | bytes 12296 | tf_op jit(solution)/shard_map/ppermute | solution.py:35
  38.3 2.6 %collective-permute-start.3 = (f32[8,128]{1,0:T(8,128)S(1)}, f32[8,128]{1,0:T(8,128)S(1)}, u32[]{:S(2)}, u32[]{:S(2)}) collective-permute-start(f32[8,128]{1,0:T(8,128)S(1)} %get-tuple-element.349), channel_id=1, source_target_pairs={{64,128},{128,64},{192,256},{256,192},{320,384},{384,320},{448,449... | collective-permute-start | bytes 12296 | tf_op jit(solution)/shard_map/ppermute | solution.py:36
  41.0 2.2 %collective-permute-done.3 = f32[8,128]{1,0:T(8,128)S(1)} collective-permute-done((f32[8,128]{1,0:T(8,128)S(1)}, f32[8,128]{1,0:T(8,128)S(1)}, u32[]{:S(2)}, u32[]{:S(2)}) %collective-permute-start.3) | collective-permute-done | bytes 4128 | tf_op jit(solution)/shard_map/ppermute | solution.py:36
  43.4 2.2 %while.62 = (s32[]{:T(128)}, f32[128]{0:T(128)S(1)}, f32[8,128]{1,0:T(8,128)S(1)}, f32[8,128,128]{2,1,0:T(8,128)S(1)}, f32[8,128]{1,0:T(8,128)S(1)}, /*index=5*/f32[8,128]{1,0:T(8,128)S(1)}, s32[]{:T(128)}, s32[]{:T(128)}) while((s32[]{:T(128)}, f32[128]{0:T(128)S(1)}, f32[8,128]{1,0:T(8,128)S(1)}, f32[8,128,128]{2,1,0:T(8,128)S(1)}, ...), condition=%wide.region_5.6_spmd.clone, body=%wide.region_4.5_spmd.clone.sunk | while | flops 197123 | bytes 70755 | solution.py:69
  45.5 1.9 %collective-permute-start.4 = (f32[8,128]{1,0:T(8,128)S(1)}, f32[8,128]{1,0:T(8,128)S(1)}, u32[]{:S(2)}, u32[]{:S(2)}) collective-permute-start(f32[8,128]{1,0:T(8,128)S(1)} %get-tuple-element.796), channel_id=1, source_target_pairs={{0,64},{64,0},{128,192},{192,128},{256,320},{320,256},{384,448},{4... | collective-permute-start | bytes 12296 | tf_op jit(solution)/shard_map/ppermute | solution.py:35
  47.5 2.7 %collective-permute-start.5 = (f32[8,128]{1,0:T(8,128)S(1)}, f32[8,128]{1,0:T(8,128)S(1)}, u32[]{:S(2)}, u32[]{:S(2)}) collective-permute-start(f32[8,128]{1,0:T(8,128)S(1)} %get-tuple-element.796), channel_id=1, source_target_pairs={{64,128},{128,64},{192,256},{256,192},{320,384},{384,320},{448,449... | collective-permute-start | bytes 12296 | tf_op jit(solution)/shard_map/ppermute | solution.py:36
  50.2 2.1 %collective-permute-done.5 = f32[8,128]{1,0:T(8,128)S(1)} collective-permute-done((f32[8,128]{1,0:T(8,128)S(1)}, f32[8,128]{1,0:T(8,128)S(1)}, u32[]{:S(2)}, u32[]{:S(2)}) %collective-permute-start.5) | collective-permute-done | bytes 4128 | tf_op jit(solution)/shard_map/ppermute | solution.py:36
  52.5 2.2 %while.63 = (s32[]{:T(128)}, f32[128]{0:T(128)S(1)}, f32[8,128]{1,0:T(8,128)S(1)}, f32[8,128]{1,0:T(8,128)S(1)}, f32[8,128,128]{2,1,0:T(8,128)S(1)}, /*index=5*/...) while((s32[]{:T(128)}, f32[128]{0:T(128)S(1)}, ...), condition=%wide.region_7.8_spmd.clone, body=%wide.region_6.7_spmd.clone.sunk | while | flops 197252 | bytes 72318 | solution.py:69
  54.7 1.9 %collective-permute-start.6 = (f32[8,128]{1,0:T(8,128)S(1)}, f32[8,128]{1,0:T(8,128)S(1)}, u32[]{:S(2)}, u32[]{:S(2)}) collective-permute-start(f32[8,128]{1,0:T(8,128)S(1)} %get-tuple-element.351), channel_id=1, source_target_pairs={{0,64},{64,0},{128,192},{192,128},{256,320},{320,256},{384,448},{4... | collective-permute-start | bytes 12296 | tf_op jit(solution)/shard_map/ppermute | solution.py:35
  56.6 3.1 %collective-permute-start.7 = (f32[8,128]{1,0:T(8,128)S(1)}, f32[8,128]{1,0:T(8,128)S(1)}, u32[]{:S(2)}, u32[]{:S(2)}) collective-permute-start(f32[8,128]{1,0:T(8,128)S(1)} %get-tuple-element.351), channel_id=1, source_target_pairs={{64,128},{128,64},{192,256},{256,192},{320,384},{384,320},{448,449... | collective-permute-start | bytes 12296 | tf_op jit(solution)/shard_map/ppermute | solution.py:36
  59.8 1.8 %collective-permute-done.7 = f32[8,128]{1,0:T(8,128)S(1)} collective-permute-done((f32[8,128]{1,0:T(8,128)S(1)}, f32[8,128]{1,0:T(8,128)S(1)}, u32[]{:S(2)}, u32[]{:S(2)}) %collective-permute-start.7) | collective-permute-done | bytes 4128 | tf_op jit(solution)/shard_map/ppermute | solution.py:36
  62.3 3.2 %stack.46 = f32[5]{0:T(128)S(1)} concatenate(f32[1]{0:T(128)} %bitcast.13, f32[1]{0:T(128)} %bitcast.14, f32[1]{0:T(128)} %bitcast.15, f32[1]{0:T(128)} %bitcast.16, f32[1]{0:T(128)} %bitcast.17), dimensions={0} | concatenate | bytes 40 | tf_op jit(solution)/shard_map/stack | solution.py:108
  65.5 7.5 %all_to_all.15 = f32[8,5,128]{2,1,0:T(8,128)S(1)} all-to-all(f32[8,5,128]{2,1,0:T(8,128)S(1)} %copy.31), channel_id=1, replica_groups=mesh['wave_0'=4,'wave_1'=2,'plane_0'=4,'plane_1'=16] {'wave_0','wave_1'}, dimensions={0} | all-to-all | bytes 40960 | tf_op jit(solution)/shard_map/all_to_all | solution.py:110
  73.6 20.7 %all-to-all-start.2 = ((f32[64,1,128]{2,1,0:T(1,128)}), f32[64,1,128]{2,1,0:T(1,128)S(1)}, u32[]{:S(2)}, u32[]{:S(2)}) async-start(f32[64,1,128]{2,1,0:T(1,128)} %broadcast_in_dim.34), calls=%async_computation.2 | async-start | bytes 65536 | tf_op jit(solution)/shard_map/all_to_all | solution.py:114
  94.3 13.3 %all-to-all-done.2 = f32[64,1,128]{2,1,0:T(1,128)S(1)} async-done(((f32[64,1,128]{2,1,0:T(1,128)}), f32[64,1,128]{2,1,0:T(1,128)S(1)}, u32[]{:S(2)}, u32[]{:S(2)}) %all-to-all-start.2) | async-done | bytes 32800 | tf_op jit(solution)/shard_map/all_to_all | solution.py:114
  (146 shorter events, 13.2 us)
Async XLA Ops:
  0.6 0.7 copy-start.3
  1.3 0.7 copy-start.1
  1.3 0.7 copy-start.2
  1.3 0.7 copy-start
  4.0 20.2 %all-to-all-start = ((f32[8,132,128]{2,1,0:T(8,128)}), f32[8,132,128]{2,1,0:T(8,128)S(1)}, u32[]{:S(2)}, u32[]{:S(2)}) async-start(f32[8,132,128]{2,1,0:T(8,128)} %reverse_select_fusion), calls=%async_computation | async-start | bytes 1114112 | tf_op jit(solution)/shard_map/all_to_all | solution.py:89
  26.4 5.0 %collective-permute-start = (f32[8,128]{1,0:T(8,128)S(1)}, f32[8,128]{1,0:T(8,128)S(1)}, u32[]{:S(2)}, u32[]{:S(2)}) collective-permute-start(f32[8,128]{1,0:T(8,128)S(1)} %get-tuple-element.742), channel_id=1, source_target_pairs={{0,64},{64,0},{128,192},{192,128},{256,320},{320,256},{384,448},{4... | collective-permute-start | bytes 12296 | tf_op jit(solution)/shard_map/ppermute | solution.py:35
  29.2 4.9 %collective-permute-start.1 = (f32[8,128]{1,0:T(8,128)S(1)}, f32[8,128]{1,0:T(8,128)S(1)}, u32[]{:S(2)}, u32[]{:S(2)}) collective-permute-start(f32[8,128]{1,0:T(8,128)S(1)} %get-tuple-element.742), channel_id=1, source_target_pairs={{64,128},{128,64},{192,256},{256,192},{320,384},{384,320},{448,449... | collective-permute-start | bytes 12296 | tf_op jit(solution)/shard_map/ppermute | solution.py:36
  36.4 4.6 %collective-permute-start.2 = (f32[8,128]{1,0:T(8,128)S(1)}, f32[8,128]{1,0:T(8,128)S(1)}, u32[]{:S(2)}, u32[]{:S(2)}) collective-permute-start(f32[8,128]{1,0:T(8,128)S(1)} %get-tuple-element.349), channel_id=1, source_target_pairs={{0,64},{64,0},{128,192},{192,128},{256,320},{320,256},{384,448},{4... | collective-permute-start | bytes 12296 | tf_op jit(solution)/shard_map/ppermute | solution.py:35
  38.3 4.9 %collective-permute-start.3 = (f32[8,128]{1,0:T(8,128)S(1)}, f32[8,128]{1,0:T(8,128)S(1)}, u32[]{:S(2)}, u32[]{:S(2)}) collective-permute-start(f32[8,128]{1,0:T(8,128)S(1)} %get-tuple-element.349), channel_id=1, source_target_pairs={{64,128},{128,64},{192,256},{256,192},{320,384},{384,320},{448,449... | collective-permute-start | bytes 12296 | tf_op jit(solution)/shard_map/ppermute | solution.py:36
  45.5 4.7 %collective-permute-start.4 = (f32[8,128]{1,0:T(8,128)S(1)}, f32[8,128]{1,0:T(8,128)S(1)}, u32[]{:S(2)}, u32[]{:S(2)}) collective-permute-start(f32[8,128]{1,0:T(8,128)S(1)} %get-tuple-element.796), channel_id=1, source_target_pairs={{0,64},{64,0},{128,192},{192,128},{256,320},{320,256},{384,448},{4... | collective-permute-start | bytes 12296 | tf_op jit(solution)/shard_map/ppermute | solution.py:35
  47.5 4.9 %collective-permute-start.5 = (f32[8,128]{1,0:T(8,128)S(1)}, f32[8,128]{1,0:T(8,128)S(1)}, u32[]{:S(2)}, u32[]{:S(2)}) collective-permute-start(f32[8,128]{1,0:T(8,128)S(1)} %get-tuple-element.796), channel_id=1, source_target_pairs={{64,128},{128,64},{192,256},{256,192},{320,384},{384,320},{448,449... | collective-permute-start | bytes 12296 | tf_op jit(solution)/shard_map/ppermute | solution.py:36
  54.7 5.1 %collective-permute-start.6 = (f32[8,128]{1,0:T(8,128)S(1)}, f32[8,128]{1,0:T(8,128)S(1)}, u32[]{:S(2)}, u32[]{:S(2)}) collective-permute-start(f32[8,128]{1,0:T(8,128)S(1)} %get-tuple-element.351), channel_id=1, source_target_pairs={{0,64},{64,0},{128,192},{192,128},{256,320},{320,256},{384,448},{4... | collective-permute-start | bytes 12296 | tf_op jit(solution)/shard_map/ppermute | solution.py:35
  56.6 4.9 %collective-permute-start.7 = (f32[8,128]{1,0:T(8,128)S(1)}, f32[8,128]{1,0:T(8,128)S(1)}, u32[]{:S(2)}, u32[]{:S(2)}) collective-permute-start(f32[8,128]{1,0:T(8,128)S(1)} %get-tuple-element.351), channel_id=1, source_target_pairs={{64,128},{128,64},{192,256},{256,192},{320,384},{384,320},{448,449... | collective-permute-start | bytes 12296 | tf_op jit(solution)/shard_map/ppermute | solution.py:36
  73.6 34.0 %all-to-all-start.2 = ((f32[64,1,128]{2,1,0:T(1,128)}), f32[64,1,128]{2,1,0:T(1,128)S(1)}, u32[]{:S(2)}, u32[]{:S(2)}) async-start(f32[64,1,128]{2,1,0:T(1,128)} %broadcast_in_dim.34), calls=%async_computation.2 | async-start | bytes 65536 | tf_op jit(solution)/shard_map/all_to_all | solution.py:114

commit v2 on v1

--- a/solution.py
+++ b/solution.py
@@ -32,9 +32,9 @@
 
 
 def neighbours(values):
+    far = lax.ppermute(values, ALL, FAR)
     near = lax.ppermute(values, ALL, NEAR)
-    far = lax.ppermute(values, ALL, FAR)
-    return near + far
+    return far + near
 
 
 def apply_block(block, vector):

time: 115 us -> 108 us (0.939)
  waiting for transfers between devices: 31.9 us -> 27.3 us
  starting transfers between devices: 50 us -> 46.4 us
    ppermute x4, waiting for transfers between devices: 8.82 us -> 0.63 us  [neighbours(): far = lax.ppermute(values, ALL, FAR)]
    ppermute x4, waiting for transfers between devices: 0.01 us -> 3.52 us  [neighbours(): near = lax.ppermute(values, ALL, NEAR)]
    all_to_all x1, starting transfers between devices: 20.7 us -> 17.3 us  [on_device(): lax.all_to_all(jnp.broadcast_to(part[None, None], (NP, 1, 128)), PLANE, s...]
  transfers between devices with their start and end apart: 10 -> 10, of which waited for: 6 -> 8; matrix products, arithmetic and copies ran while one was open for 0% -> 0% of each run, Pallas kernels for 0% -> 0%
where the time goes in v2:
time: 108 us; the launch traced here: 107 us
  starting transfers between devices  46.4 us (43%)
  waiting for transfers between devices  27.3 us (25%)
  local copies, waits for them, and re-layouts  9.3 us (9%)
  blocking collectives  8.02 us (7%)
  between operations  5.96 us (6%)
  matrix products  5.89 us (5%)
  other arithmetic  3.1 us (3%)
    all_to_all x1, starting transfers between devices, on_device(): lax.all_to_all(jnp.broadcast_to(part[None, None], (NP, 1, 128)), PLANE, s...  17.3 us
    all_to_all x1, waiting for transfers between devices, on_device(): lax.all_to_all(jnp.broadcast_to(part[None, None], (NP, 1, 128)), PLANE, s...  13.3 us
    ppermute x4, starting transfers between devices, neighbours(): far = lax.ppermute(values, ALL, FAR)  11.1 us
    all_to_all x1, starting transfers between devices, on_device(): lax.all_to_all(packed, WAVE, split_axis=0, concat_axis=0, tiled=True)  10.3 us
    all_to_all x1, waiting for transfers between devices, on_device(): lax.all_to_all(packed, WAVE, split_axis=0, concat_axis=0, tiled=True)  9.85 us
    all_to_all x1, blocking collectives, on_device(): lax.all_to_all(jnp.stack([z, q, w, p, sums], axis=1), WAVE, split_axis=0,...  8.02 us
    ppermute x4, starting transfers between devices, neighbours(): near = lax.ppermute(values, ALL, NEAR)  7.68 us
    dot_general x32, matrix products, apply_block(): return jnp.einsum('ij,j->i', block, vector, precision=lax.Precision.HIGHEST)  5.89 us
  transfers between devices with their start and end apart: 10, of which 8 were waited for; matrix products, arithmetic and copies ran while one was open for 0% of the time, Pallas kernels for 0%

profile of v2, /device:TPU:1, one launch (start us, length us, event | category | flops | bytes accessed | tf_op | source)
XLA Modules:
  0.0 106.9 jit_solution(7046473541420996628)
XLA Ops:
  2.0 1.1 %concatenate.48 = f32[8,132,128]{2,1,0:T(8,128)S(1)} concatenate(f32[8,128,128]{2,1,0:T(8,128)} %bitcast.203, f32[8,1,128]{2,1,0:T(1,128)S(1)} %bitcast.218, f32[8,1,128]{2,1,0:T(1,128)S(1)} %bitcast.228, f32[8,1,128]{2,1,0:T(1,128)S(1)} %stack_broadcast_in_dim.4, f32[8,1,128]{2,1,0:T(1,128)S(1)} %bitcast.229), dimensions={1} | concatenate | bytes 1081344 | tf_op jit(solution)/shard_map/concatenate | solution.py:88
  3.1 0.8 reverse_select_fusion
  4.0 10.3 %all-to-all-start = ((f32[8,132,128]{2,1,0:T(8,128)}), f32[8,132,128]{2,1,0:T(8,128)S(1)}, u32[]{:S(2)}, u32[]{:S(2)}) async-start(f32[8,132,128]{2,1,0:T(8,128)} %reverse_select_fusion), calls=%async_computation | async-start | bytes 1114112 | tf_op jit(solution)/shard_map/all_to_all | solution.py:89
  14.3 9.8 %all-to-all-done = f32[8,132,128]{2,1,0:T(8,128)S(1)} async-done(((f32[8,132,128]{2,1,0:T(8,128)}), f32[8,132,128]{2,1,0:T(8,128)S(1)}, u32[]{:S(2)}, u32[]{:S(2)}) %all-to-all-start) | async-done | bytes 540704 | tf_op jit(solution)/shard_map/all_to_all | solution.py:89
  24.2 2.2 %while.60 = (s32[]{:T(128)}, f32[128]{0:T(128)S(1)}, f32[8,128]{1,0:T(8,128)S(1)}, f32[8,128,128]{2,1,0:T(8,128)S(1)}, f32[8,128]{1,0:T(8,128)S(1)}, /*index=5*/f32[8,128]{1,0:T(8,128)S(1)}, s32[]{:T(128)}, s32[]{:T(128)}) while((s32[]{:T(128)}, f32[128]{0:T(128)S(1)}, f32[8,128]{1,0:T(8,128)S(1)}, f32[8,128,128]{2,1,0:T(8,128)S(1)}, ...), condition=%wide.region_1.2_spmd.clone, body=%wide.region_0.1_spmd.clone.sunk | while | flops 197123 | bytes 70755 | solution.py:69
  26.4 3.0 %collective-permute-start = (f32[8,128]{1,0:T(8,128)S(1)}, f32[8,128]{1,0:T(8,128)S(1)}, u32[]{:S(2)}, u32[]{:S(2)}) collective-permute-start(f32[8,128]{1,0:T(8,128)S(1)} %get-tuple-element.742), channel_id=1, source_target_pairs={{64,128},{128,64},{192,256},{256,192},{320,384},{384,320},{448,449... | collective-permute-start | bytes 12296 | tf_op jit(solution)/shard_map/ppermute | solution.py:35
  29.4 1.9 %collective-permute-start.1 = (f32[8,128]{1,0:T(8,128)S(1)}, f32[8,128]{1,0:T(8,128)S(1)}, u32[]{:S(2)}, u32[]{:S(2)}) collective-permute-start(f32[8,128]{1,0:T(8,128)S(1)} %get-tuple-element.742), channel_id=1, source_target_pairs={{0,64},{64,0},{128,192},{192,128},{256,320},{320,256},{384,448},{4... | collective-permute-start | bytes 12296 | tf_op jit(solution)/shard_map/ppermute | solution.py:36
  31.5 1.0 collective-permute-done.1
  32.5 2.2 %while.61 = (s32[]{:T(128)}, f32[128]{0:T(128)S(1)}, f32[8,128]{1,0:T(8,128)S(1)}, f32[8,128]{1,0:T(8,128)S(1)}, f32[8,128,128]{2,1,0:T(8,128)S(1)}, /*index=5*/...) while((s32[]{:T(128)}, f32[128]{0:T(128)S(1)}, ...), condition=%wide.region_3.4_spmd.clone, body=%wide.region_2.3_spmd.clone.sunk | while | flops 197252 | bytes 72318 | solution.py:69
  34.7 2.6 %collective-permute-start.2 = (f32[8,128]{1,0:T(8,128)S(1)}, f32[8,128]{1,0:T(8,128)S(1)}, u32[]{:S(2)}, u32[]{:S(2)}) collective-permute-start(f32[8,128]{1,0:T(8,128)S(1)} %get-tuple-element.349), channel_id=1, source_target_pairs={{64,128},{128,64},{192,256},{256,192},{320,384},{384,320},{448,449... | collective-permute-start | bytes 12296 | tf_op jit(solution)/shard_map/ppermute | solution.py:35
  37.3 1.9 %collective-permute-start.3 = (f32[8,128]{1,0:T(8,128)S(1)}, f32[8,128]{1,0:T(8,128)S(1)}, u32[]{:S(2)}, u32[]{:S(2)}) collective-permute-start(f32[8,128]{1,0:T(8,128)S(1)} %get-tuple-element.349), channel_id=1, source_target_pairs={{0,64},{64,0},{128,192},{192,128},{256,320},{320,256},{384,448},{4... | collective-permute-start | bytes 12296 | tf_op jit(solution)/shard_map/ppermute | solution.py:36
  39.7 0.7 collective-permute-done.3
  40.5 2.2 %while.62 = (s32[]{:T(128)}, f32[128]{0:T(128)S(1)}, f32[8,128]{1,0:T(8,128)S(1)}, f32[8,128,128]{2,1,0:T(8,128)S(1)}, f32[8,128]{1,0:T(8,128)S(1)}, /*index=5*/f32[8,128]{1,0:T(8,128)S(1)}, s32[]{:T(128)}, s32[]{:T(128)}) while((s32[]{:T(128)}, f32[128]{0:T(128)S(1)}, f32[8,128]{1,0:T(8,128)S(1)}, f32[8,128,128]{2,1,0:T(8,128)S(1)}, ...), condition=%wide.region_5.6_spmd.clone, body=%wide.region_4.5_spmd.clone.sunk | while | flops 197123 | bytes 70755 | solution.py:69
  42.7 3.0 %collective-permute-start.4 = (f32[8,128]{1,0:T(8,128)S(1)}, f32[8,128]{1,0:T(8,128)S(1)}, u32[]{:S(2)}, u32[]{:S(2)}) collective-permute-start(f32[8,128]{1,0:T(8,128)S(1)} %get-tuple-element.796), channel_id=1, source_target_pairs={{64,128},{128,64},{192,256},{256,192},{320,384},{384,320},{448,449... | collective-permute-start | bytes 12296 | tf_op jit(solution)/shard_map/ppermute | solution.py:35
  45.6 1.9 %collective-permute-start.5 = (f32[8,128]{1,0:T(8,128)S(1)}, f32[8,128]{1,0:T(8,128)S(1)}, u32[]{:S(2)}, u32[]{:S(2)}) collective-permute-start(f32[8,128]{1,0:T(8,128)S(1)} %get-tuple-element.796), channel_id=1, source_target_pairs={{0,64},{64,0},{128,192},{192,128},{256,320},{320,256},{384,448},{4... | collective-permute-start | bytes 12296 | tf_op jit(solution)/shard_map/ppermute | solution.py:36
  47.6 1.1 collective-permute-done.5
  48.8 2.2 %while.63 = (s32[]{:T(128)}, f32[128]{0:T(128)S(1)}, f32[8,128]{1,0:T(8,128)S(1)}, f32[8,128]{1,0:T(8,128)S(1)}, f32[8,128,128]{2,1,0:T(8,128)S(1)}, /*index=5*/...) while((s32[]{:T(128)}, f32[128]{0:T(128)S(1)}, ...), condition=%wide.region_7.8_spmd.clone, body=%wide.region_6.7_spmd.clone.sunk | while | flops 197252 | bytes 72318 | solution.py:69
  51.0 2.6 %collective-permute-start.6 = (f32[8,128]{1,0:T(8,128)S(1)}, f32[8,128]{1,0:T(8,128)S(1)}, u32[]{:S(2)}, u32[]{:S(2)}) collective-permute-start(f32[8,128]{1,0:T(8,128)S(1)} %get-tuple-element.351), channel_id=1, source_target_pairs={{64,128},{128,64},{192,256},{256,192},{320,384},{384,320},{448,449... | collective-permute-start | bytes 12296 | tf_op jit(solution)/shard_map/ppermute | solution.py:35
  53.6 1.9 %collective-permute-start.7 = (f32[8,128]{1,0:T(8,128)S(1)}, f32[8,128]{1,0:T(8,128)S(1)}, u32[]{:S(2)}, u32[]{:S(2)}) collective-permute-start(f32[8,128]{1,0:T(8,128)S(1)} %get-tuple-element.351), channel_id=1, source_target_pairs={{0,64},{64,0},{128,192},{192,128},{256,320},{320,256},{384,448},{4... | collective-permute-start | bytes 12296 | tf_op jit(solution)/shard_map/ppermute | solution.py:36
  56.6 0.7 multiply_reduce_fusion
  57.4 3.2 %stack.46 = f32[5]{0:T(128)S(1)} concatenate(f32[1]{0:T(128)} %bitcast.13, f32[1]{0:T(128)} %bitcast.14, f32[1]{0:T(128)} %bitcast.15, f32[1]{0:T(128)} %bitcast.16, f32[1]{0:T(128)} %bitcast.17), dimensions={0} | concatenate | bytes 40 | tf_op jit(solution)/shard_map/stack | solution.py:108
  60.6 8.0 %all_to_all.15 = f32[8,5,128]{2,1,0:T(8,128)S(1)} all-to-all(f32[8,5,128]{2,1,0:T(8,128)S(1)} %copy.31), channel_id=1, replica_groups=mesh['wave_0'=4,'wave_1'=2,'plane_0'=4,'plane_1'=16] {'wave_0','wave_1'}, dimensions={0} | all-to-all | bytes 40960 | tf_op jit(solution)/shard_map/all_to_all | solution.py:110
  69.3 17.3 %all-to-all-start.2 = ((f32[64,1,128]{2,1,0:T(1,128)}), f32[64,1,128]{2,1,0:T(1,128)S(1)}, u32[]{:S(2)}, u32[]{:S(2)}) async-start(f32[64,1,128]{2,1,0:T(1,128)} %broadcast_in_dim.34), calls=%async_computation.2 | async-start | bytes 65536 | tf_op jit(solution)/shard_map/all_to_all | solution.py:114
  86.6 13.3 %all-to-all-done.2 = f32[64,1,128]{2,1,0:T(1,128)S(1)} async-done(((f32[64,1,128]{2,1,0:T(1,128)}), f32[64,1,128]{2,1,0:T(1,128)S(1)}, u32[]{:S(2)}, u32[]{:S(2)}) %all-to-all-start.2) | async-done | bytes 32800 | tf_op jit(solution)/shard_map/all_to_all | solution.py:114
  (146 shorter events, 13.8 us)
Async XLA Ops:
  0.6 0.7 copy-start.3
  1.3 0.7 copy-start.1
  1.3 0.7 copy-start.2
  1.3 0.7 copy-start
  4.0 20.2 %all-to-all-start = ((f32[8,132,128]{2,1,0:T(8,128)}), f32[8,132,128]{2,1,0:T(8,128)S(1)}, u32[]{:S(2)}, u32[]{:S(2)}) async-start(f32[8,132,128]{2,1,0:T(8,128)} %reverse_select_fusion), calls=%async_computation | async-start | bytes 1114112 | tf_op jit(solution)/shard_map/all_to_all | solution.py:89
  26.4 5.0 %collective-permute-start = (f32[8,128]{1,0:T(8,128)S(1)}, f32[8,128]{1,0:T(8,128)S(1)}, u32[]{:S(2)}, u32[]{:S(2)}) collective-permute-start(f32[8,128]{1,0:T(8,128)S(1)} %get-tuple-element.742), channel_id=1, source_target_pairs={{64,128},{128,64},{192,256},{256,192},{320,384},{384,320},{448,449... | collective-permute-start | bytes 12296 | tf_op jit(solution)/shard_map/ppermute | solution.py:35
  29.4 3.1 %collective-permute-start.1 = (f32[8,128]{1,0:T(8,128)S(1)}, f32[8,128]{1,0:T(8,128)S(1)}, u32[]{:S(2)}, u32[]{:S(2)}) collective-permute-start(f32[8,128]{1,0:T(8,128)S(1)} %get-tuple-element.742), channel_id=1, source_target_pairs={{0,64},{64,0},{128,192},{192,128},{256,320},{320,256},{384,448},{4... | collective-permute-start | bytes 12296 | tf_op jit(solution)/shard_map/ppermute | solution.py:36
  34.7 4.9 %collective-permute-start.2 = (f32[8,128]{1,0:T(8,128)S(1)}, f32[8,128]{1,0:T(8,128)S(1)}, u32[]{:S(2)}, u32[]{:S(2)}) collective-permute-start(f32[8,128]{1,0:T(8,128)S(1)} %get-tuple-element.349), channel_id=1, source_target_pairs={{64,128},{128,64},{192,256},{256,192},{320,384},{384,320},{448,449... | collective-permute-start | bytes 12296 | tf_op jit(solution)/shard_map/ppermute | solution.py:35
  37.3 3.1 %collective-permute-start.3 = (f32[8,128]{1,0:T(8,128)S(1)}, f32[8,128]{1,0:T(8,128)S(1)}, u32[]{:S(2)}, u32[]{:S(2)}) collective-permute-start(f32[8,128]{1,0:T(8,128)S(1)} %get-tuple-element.349), channel_id=1, source_target_pairs={{0,64},{64,0},{128,192},{192,128},{256,320},{320,256},{384,448},{4... | collective-permute-start | bytes 12296 | tf_op jit(solution)/shard_map/ppermute | solution.py:36
  42.7 5.0 %collective-permute-start.4 = (f32[8,128]{1,0:T(8,128)S(1)}, f32[8,128]{1,0:T(8,128)S(1)}, u32[]{:S(2)}, u32[]{:S(2)}) collective-permute-start(f32[8,128]{1,0:T(8,128)S(1)} %get-tuple-element.796), channel_id=1, source_target_pairs={{64,128},{128,64},{192,256},{256,192},{320,384},{384,320},{448,449... | collective-permute-start | bytes 12296 | tf_op jit(solution)/shard_map/ppermute | solution.py:35
  45.6 3.1 %collective-permute-start.5 = (f32[8,128]{1,0:T(8,128)S(1)}, f32[8,128]{1,0:T(8,128)S(1)}, u32[]{:S(2)}, u32[]{:S(2)}) collective-permute-start(f32[8,128]{1,0:T(8,128)S(1)} %get-tuple-element.796), channel_id=1, source_target_pairs={{0,64},{64,0},{128,192},{192,128},{256,320},{320,256},{384,448},{4... | collective-permute-start | bytes 12296 | tf_op jit(solution)/shard_map/ppermute | solution.py:36
  51.0 4.9 %collective-permute-start.6 = (f32[8,128]{1,0:T(8,128)S(1)}, f32[8,128]{1,0:T(8,128)S(1)}, u32[]{:S(2)}, u32[]{:S(2)}) collective-permute-start(f32[8,128]{1,0:T(8,128)S(1)} %get-tuple-element.351), channel_id=1, source_target_pairs={{64,128},{128,64},{192,256},{256,192},{320,384},{384,320},{448,449... | collective-permute-start | bytes 12296 | tf_op jit(solution)/shard_map/ppermute | solution.py:35
  53.6 3.1 %collective-permute-start.7 = (f32[8,128]{1,0:T(8,128)S(1)}, f32[8,128]{1,0:T(8,128)S(1)}, u32[]{:S(2)}, u32[]{:S(2)}) collective-permute-start(f32[8,128]{1,0:T(8,128)S(1)} %get-tuple-element.351), channel_id=1, source_target_pairs={{0,64},{64,0},{128,192},{192,128},{256,320},{320,256},{384,448},{4... | collective-permute-start | bytes 12296 | tf_op jit(solution)/shard_map/ppermute | solution.py:36
  69.3 30.6 %all-to-all-start.2 = ((f32[64,1,128]{2,1,0:T(1,128)}), f32[64,1,128]{2,1,0:T(1,128)S(1)}, u32[]{:S(2)}, u32[]{:S(2)}) async-start(f32[64,1,128]{2,1,0:T(1,128)} %broadcast_in_dim.34), calls=%async_computation.2 | async-start | bytes 65536 | tf_op jit(solution)/shard_map/all_to_all | solution.py:114

commit v3 on v2

v3 whole, which is shorter than its diff:
```python
import jax
import jax.numpy as jnp
from jax import lax
from jax.experimental import pallas as pl
from jax.experimental.pallas import tpu as pltpu
from jax.sharding import Mesh
from jax.sharding import PartitionSpec as P

WAVE = ("wave_0", "wave_1")
PLANE = ("plane_0", "plane_1")
ALL = WAVE + PLANE
NW = 8
NP = 64
B = 128
R, CZ, CX, CY = B, B + 1, B + 2, B + 3
ROWS = B + 8

relax = 1.5

VMEM = pl.BlockSpec(memory_space=pltpu.VMEM)
HBM = pl.BlockSpec(memory_space=pl.ANY)


def chain_device(position):
    plane, k = divmod(position, NW)
    wave = k if plane % 2 == 0 else NW - 1 - k
    return wave * NP + plane


def swap_pairs(first):
    pairs = []
    for i in range(first, NW * NP - 1, 2):
        a, b = chain_device(i), chain_device(i + 1)
        pairs += [(a, b), (b, a)]
    return pairs


NEAR = swap_pairs(0)
FAR = swap_pairs(1)


def neighbours(values):
    far = lax.ppermute(values, ALL, FAR)
    near = lax.ppermute(values, ALL, NEAR)
    return far, near


def f32(*shape):
    return jax.ShapeDtypeStruct(shape, jnp.float32)


def on_chip(*shape):
    return pltpu.VMEM(shape, jnp.float32)


def turned(j):
    parity = lax.axis_index("plane_1") % 2
    return j + parity * (NW - 1 - 2 * j)


def pack_kernel(inverse, right, cz, cx, cy, packed, r_out, cz_v, cx_v, cy_v, sems, small):
    copies = [
        pltpu.make_async_copy(right.at[0], r_out, small.at[0]),
        pltpu.make_async_copy(cz.at[0], cz_v, small.at[1]),
        pltpu.make_async_copy(cx, cx_v, small.at[2]),
        pltpu.make_async_copy(cy, cy_v, small.at[3]),
    ]
    for copy in copies:
        copy.start()
    blocks = [
        pltpu.make_async_copy(inverse.at[0, j], packed.at[turned(j), 0:B, :], sems.at[j])
        for j in range(NW)
    ]
    for copy in blocks:
        copy.start()
    for copy in copies:
        copy.wait()
    r_v, cz_a, cx_a, cy_a = r_out[...], cz_v[...], cx_v[...], cy_v[...]
    for j in range(NW):
        rows = [r_v[j : j + 1], cz_a[j : j + 1], cx_a[j : j + 1], cy_a]
        rows.append(jnp.zeros((ROWS - B - 4, B), jnp.float32))
        packed[turned(j), B:ROWS, :] = jnp.concatenate(rows, axis=0)
    for copy in blocks:
        copy.wait()


def pack(inverse, right_side, coupling_z, coupling_x, coupling_y):
    return pl.pallas_call(
        pack_kernel,
        out_shape=(on_chip(NW, ROWS, B), on_chip(NW, B)),
        in_specs=[HBM] * 5,
        out_specs=(VMEM, VMEM),
        scratch_shapes=[
            pltpu.VMEM((NW, B), jnp.float32),
            pltpu.VMEM((NW, B), jnp.float32),
            pltpu.VMEM((1, B), jnp.float32),
            pltpu.SemaphoreType.DMA((NW,)),
            pltpu.SemaphoreType.DMA((4,)),
        ],
        name="pack",
    )(inverse, right_side, coupling_z, coupling_x, coupling_y)


def times_block(columns, x, vector):
    return jnp.sum(columns[x, 0:B, :] * vector, axis=1).reshape(1, B)


def forward(columns, source, out):
    cx = columns[0, CX : CX + 1, :]
    previous = None
    for x in range(NW):
        s = source(x)
        if previous is not None:
            s = s + cx * previous
        previous = relax * times_block(columns, x, s)
        out[x : x + 1, :] = previous


def first_kernel(columns, half):
    forward(columns, lambda x: columns[x, R : R + 1, :], half)


def image_kernel(columns, local, far, near, cy, image, half):
    image[...] = local[...] - cy[...] * (far[...] + near[...])
    value = image[...]
    forward(columns, lambda x: value[x : x + 1], half)


def backward_kernel(columns, base, near, far, cy, half, out):
    source = base[...] + cy[...] * (far[...] + near[...])
    cx = columns[0, CX : CX + 1, :]
    previous = None
    for x in reversed(range(NW)):
        s = source[x : x + 1]
        if previous is not None:
            s = s + cx * previous
        previous = half[x : x + 1, :] + relax * times_block(columns, x, s)
        out[x : x + 1, :] = previous


def sums_kernel(r, z, q, w, local, far, near, cy, back):
    z_a, q_a, w_a = z[...], q[...], w[...]
    p_a = local[...] - cy[...] * (far[...] + near[...])
    lane = lax.broadcasted_iota(jnp.int32, (1, B), 1)
    row = jnp.zeros((1, B), jnp.float32)
    for k, product in enumerate((z_a * r[...], z_a * q_a, w_a * r[...], w_a * q_a, w_a * p_a)):
        total = jnp.sum(jnp.sum(product, axis=0, keepdims=True), axis=1, keepdims=True)
        row = jnp.where(lane == k, total, row)
    rest = jnp.zeros((3, B), jnp.float32)
    for x in range(NW):
        at = slice(x, x + 1)
        back[x] = jnp.concatenate([z_a[at], q_a[at], w_a[at], p_a[at], row, rest], axis=0)


def share_kernel(back, out):
    part = back[0, 4:5, :]
    for x in range(1, NW):
        part = part + back[x, 4:5, :]
    out[...] = jnp.broadcast_to(part[None], (NP, 1, B))


def final_kernel(everyone, back, r, solution_out, residual_out):
    total = jnp.sum(everyone[...], axis=0)
    zr, zq, wr, wq, wp = (total[:, k : k + 1] for k in range(5))
    first = zr / zq
    ratio = wq / zq
    second = (first * wq - wr) / (wp - ratio * wq)
    lead = first + second * ratio
    for j in range(NW):
        field = back[turned(j)]
        solution_out[0, j : j + 1, :] = lead * field[0:1] - second * field[2:3]
        residual_out[0, j : j + 1, :] = r[j : j + 1] - lead * field[1:2] + second * field[3:4]


def local(kernel, out, name):
    def call(*args):
        specs = tuple(VMEM for _ in out) if isinstance(out, tuple) else VMEM
        args = [pltpu.with_memory_space_constraint(a, pltpu.VMEM) for a in args]
        return pl.pallas_call(
            kernel, out_shape=out, in_specs=[VMEM] * len(args), out_specs=specs, name=name
        )(*args)

    return call


def column_part(values, centre, cz, upper_z):
    below = jnp.concatenate([jnp.zeros_like(values[:, :1]), values[:, :-1]], axis=-1)
    above = jnp.concatenate([values[:, 1:], jnp.zeros_like(values[:, :1])], axis=-1)
    return centre * values - cz * below - upper_z * above


def lower(values):
    return jnp.concatenate([jnp.zeros_like(values[:1]), values[:-1]], axis=0)


def upper(values):
    return jnp.concatenate([values[1:], jnp.zeros_like(values[:1])], axis=0)


def on_device(right_side, coupling_x, coupling_y, coupling_z, inverse):
    packed, own = pack(inverse, right_side, coupling_z, coupling_x, coupling_y)
    columns = lax.all_to_all(packed, WAVE, split_axis=0, concat_axis=0, tiled=True)
    r, cz, cx, cy = (columns[:, i] for i in (R, CZ, CX, CY))
    upper_z = jnp.concatenate([cz[:, 1:], cz[:, :1]], axis=-1)
    centre = 2.0 * cx + 2.0 * cy + cz + upper_z

    def before(source, half):
        return source - column_part(half, centre, cz, upper_z) + cx * lower(half)

    def image_part(values):
        return column_part(values, centre, cz, upper_z) - cx * (lower(values) + upper(values))

    field = on_chip(NW, B)
    half = local(first_kernel, field, "first")(columns)
    far, near = neighbours(half)
    z = local(backward_kernel, field, "backward")(columns, before(r, half), near, far, cy, half)
    far, near = neighbours(z)
    q, half = local(image_kernel, (field, field), "image")(columns, image_part(z), far, near, cy)
    far, near = neighbours(half)
    w = local(backward_kernel, field, "backward")(columns, before(q, half), near, far, cy, half)
    far, near = neighbours(w)
    back = local(sums_kernel, on_chip(NW, 8, B), "sums")(r, z, q, w, image_part(w), far, near, cy)
    back = lax.all_to_all(back, WAVE, split_axis=0, concat_axis=0, tiled=True)
    share = local(share_kernel, on_chip(NP, 1, B), "share")(back)
    everyone = lax.all_to_all(share, PLANE, split_axis=0, concat_axis=0, tiled=True)
    out = f32(1, NW, B)
    return local(final_kernel, (out, out), "final")(everyone, back, own)


def solution(mesh):
    torus = Mesh(mesh.devices.reshape(4, 2, 4, 16), ALL)
    return jax.shard_map(
        on_device,
        mesh=torus,
        in_specs=(
            P(WAVE, PLANE, None),
            P(PLANE, None),
            P(WAVE, None),
            P(WAVE, PLANE, None),
            P(WAVE, PLANE, None, None),
        ),
        out_specs=(P(WAVE, PLANE, None), P(WAVE, PLANE, None)),
        check_vma=False,
    )
```

time: 108 us -> 88.8 us (0.82)
  blocking collectives: 8.02 us -> 58.4 us
  starting transfers between devices: 46.4 us -> 18.8 us
  waiting for transfers between devices: 27.3 us -> 4.1 us
  local copies, waits for them, and re-layouts: 9.3 us -> 0.39 us
  matrix products: 5.89 us -> 0 us
  Pallas kernels: 0 us -> 5.44 us
  between operations: 5.96 us -> 0.77 us
  other arithmetic: 3.1 us -> 0.33 us
    all_to_all x1 -> x3, blocking collectives: 8.02 us -> 58.4 us  [the longest x1 31 us: on_device(): lax.all_to_all(share, PLANE, split_axis=0, concat_axis=0, tiled=True)]
    all_to_all x2 -> x0, starting transfers between devices: 27.6 us -> none  [the longest x1 17.3 us: on_device(): lax.all_to_all(jnp.broadcast_to(part[None, None], (NP, 1, 128)), PLANE, s...]
    all_to_all x2 -> x0, waiting for transfers between devices: 23.1 us -> none  [the longest x1 13.3 us: on_device(): lax.all_to_all(jnp.broadcast_to(part[None, None], (NP, 1, 128)), PLANE, s...]
    dot_general x32 -> x0, matrix products: 5.89 us -> none  [apply_block(): return jnp.einsum('ij,j->i', block, vector, precision=lax.Precision.HIGHEST)]
    pallas_call x0 -> x8, Pallas kernels: none -> 5.44 us  [the longest x7 4.21 us: call(): pl.pallas_call(kernel, out_shape=out, in_specs=[VMEM] * len(args), out_sp...]
    another operation x8 -> x0, local copies, waits for them, and re-layouts: 3.21 us -> none  [the longest x1 3.19 us: on_device(): jnp.stack([jnp.sum(a * b) for a, b in ((z, r), (z, q), (w, r), (w, q), (w...]
    dynamic_update_slice x32 -> x0, local copies, waits for them, and re-layouts: 1.84 us -> none  [sweep(): lax.scan(step, jnp.zeros_like(source[0]), (source, inverse, base), revers...]
    unnamed x11 -> x0, local copies, waits for them, and re-layouts: 1.36 us -> none
  transfers between devices with their start and end apart: 10 -> 8, of which waited for: 8 -> 6; matrix products, arithmetic and copies ran while one was open for 0% -> 0% of each run, Pallas kernels for 0% -> 0%
where the time goes in v3:
time: 88.8 us; the launch traced here: 88.2 us
  blocking collectives  58.4 us (66%)
  starting transfers between devices  18.8 us (21%)
  Pallas kernels  5.44 us (6%)
  waiting for transfers between devices  4.1 us (5%)
    all_to_all x1, blocking collectives, on_device(): lax.all_to_all(share, PLANE, split_axis=0, concat_axis=0, tiled=True)  31 us
    all_to_all x1, blocking collectives, on_device(): lax.all_to_all(packed, WAVE, split_axis=0, concat_axis=0, tiled=True)  19.4 us
    ppermute x4, starting transfers between devices, neighbours(): far = lax.ppermute(values, ALL, FAR)  11.1 us
    all_to_all x1, blocking collectives, on_device(): back = lax.all_to_all(back, WAVE, split_axis=0, concat_axis=0, tiled=True)  8.01 us
    ppermute x4, starting transfers between devices, neighbours(): near = lax.ppermute(values, ALL, NEAR)  7.68 us
    pallas_call x7, Pallas kernels, call(): pl.pallas_call(kernel, out_shape=out, in_specs=[VMEM] * len(args), out_sp...  4.21 us
    ppermute x4, waiting for transfers between devices, neighbours(): near = lax.ppermute(values, ALL, NEAR)  3.68 us
  transfers between devices with their start and end apart: 8, of which 6 were waited for; matrix products, arithmetic and copies ran while one was open for 0% of the time, Pallas kernels for 0%

profile of v3, /device:TPU:1, one launch (start us, length us, event | category | flops | bytes accessed | tf_op | source)
XLA Modules:
  0.0 88.2 jit_solution(9927785839814002029)
XLA Ops:
  0.6 1.2 %pack.1 = (f32[8,136,128]{2,1,0:T(8,128)S(1)}, f32[8,128]{1,0:T(8,128)S(1)}) custom-call(f32[1,8,128,128]{3,2,1,0:T(8,128)} %inverse.1, f32[1,8,128]{2,1,0:T(8,128)} %right.1, f32[1,8,128]{2,1,0:T(8,128)} %cz.1, f32[8,128]{1,0:T(8,128)} %cx.1, f32[1,128]{1,0:T(1,128)} %cy.1), custom_call_target="tpu_custom_call" | custom-call | tf_op jit(solution)/shard_map/pack/pallas_call | solution.py:88
  1.9 19.4 %all_to_all.15.columns = f32[8,136,128]{2,1,0:T(8,128)S(1)} all-to-all(f32[8,136,128]{2,1,0:T(8,128)S(1)} %get-tuple-element.6), channel_id=1, replica_groups=mesh['wave_0'=4,'wave_1'=2,'plane_0'=4,'plane_1'=16] {'wave_0','wave_1'}, dimensions={0} | all-to-all | bytes 1114112 | tf_op jit(solution)/shard_map/all_to_all | solution.py:202
  21.3 0.8 first.1.half
  22.1 2.6 %collective-permute-start.1 = (f32[8,128]{1,0:T(8,128)S(1)}, f32[8,128]{1,0:T(8,128)S(1)}, u32[]{:S(2)}, u32[]{:S(2)}) collective-permute-start(f32[8,128]{1,0:T(8,128)S(1)} %first.1.half), channel_id=1, source_target_pairs={{64,128},{128,64},{192,256},{256,192},{320,384},{384,320},{448,449... | collective-permute-start | bytes 12296 | tf_op jit(solution)/shard_map/ppermute | solution.py:43
  24.8 1.9 %collective-permute-start = (f32[8,128]{1,0:T(8,128)S(1)}, f32[8,128]{1,0:T(8,128)S(1)}, u32[]{:S(2)}, u32[]{:S(2)}) collective-permute-start(f32[8,128]{1,0:T(8,128)S(1)} %first.1.half), channel_id=1, source_target_pairs={{0,64},{64,0},{128,192},{192,128},{256,320},{320,256},{384,448},{4... | collective-permute-start | bytes 12296 | tf_op jit(solution)/shard_map/ppermute | solution.py:44
  26.9 0.2 collective-permute-done.1.far
  27.1 0.8 collective-permute-done.near
  27.9 0.8 backward.2.z
  28.7 2.9 %collective-permute-start.2 = (f32[8,128]{1,0:T(8,128)S(1)}, f32[8,128]{1,0:T(8,128)S(1)}, u32[]{:S(2)}, u32[]{:S(2)}) collective-permute-start(f32[8,128]{1,0:T(8,128)S(1)} %backward.2.z), channel_id=1, source_target_pairs={{64,128},{128,64},{192,256},{256,192},{320,384},{384,320},{448,449... | collective-permute-start | bytes 12296 | tf_op jit(solution)/shard_map/ppermute | solution.py:43
  31.6 1.9 %collective-permute-start.3 = (f32[8,128]{1,0:T(8,128)S(1)}, f32[8,128]{1,0:T(8,128)S(1)}, u32[]{:S(2)}, u32[]{:S(2)}) collective-permute-start(f32[8,128]{1,0:T(8,128)S(1)} %backward.2.z), channel_id=1, source_target_pairs={{0,64},{64,0},{128,192},{192,128},{256,320},{320,256},{384,448},{4... | collective-permute-start | bytes 12296 | tf_op jit(solution)/shard_map/ppermute | solution.py:44
  33.7 1.0 %collective-permute-done.3.near = f32[8,128]{1,0:T(8,128)S(1)} collective-permute-done((f32[8,128]{1,0:T(8,128)S(1)}, f32[8,128]{1,0:T(8,128)S(1)}, u32[]{:S(2)}, u32[]{:S(2)}) %collective-permute-start.3) | collective-permute-done | bytes 4128 | tf_op jit(solution)/shard_map/ppermute | solution.py:44
  34.7 0.8 image.1
  35.6 2.6 %collective-permute-start.5 = (f32[8,128]{1,0:T(8,128)S(1)}, f32[8,128]{1,0:T(8,128)S(1)}, u32[]{:S(2)}, u32[]{:S(2)}) collective-permute-start(f32[8,128]{1,0:T(8,128)S(1)} %get-tuple-element.8.half), channel_id=1, source_target_pairs={{64,128},{128,64},{192,256},{256,192},{320,384},{384,320},{448,449... | collective-permute-start | bytes 12296 | tf_op jit(solution)/shard_map/ppermute | solution.py:43
  38.2 1.9 %collective-permute-start.4 = (f32[8,128]{1,0:T(8,128)S(1)}, f32[8,128]{1,0:T(8,128)S(1)}, u32[]{:S(2)}, u32[]{:S(2)}) collective-permute-start(f32[8,128]{1,0:T(8,128)S(1)} %get-tuple-element.8.half), channel_id=1, source_target_pairs={{0,64},{64,0},{128,192},{192,128},{256,320},{320,256},{384,448},{4... | collective-permute-start | bytes 12296 | tf_op jit(solution)/shard_map/ppermute | solution.py:44
  40.2 0.3 collective-permute-done.5.far
  40.5 0.8 collective-permute-done.4.near
  41.3 0.8 backward.3.w
  42.2 2.9 %collective-permute-start.6 = (f32[8,128]{1,0:T(8,128)S(1)}, f32[8,128]{1,0:T(8,128)S(1)}, u32[]{:S(2)}, u32[]{:S(2)}) collective-permute-start(f32[8,128]{1,0:T(8,128)S(1)} %backward.3.w), channel_id=1, source_target_pairs={{64,128},{128,64},{192,256},{256,192},{320,384},{384,320},{448,449... | collective-permute-start | bytes 12296 | tf_op jit(solution)/shard_map/ppermute | solution.py:43
  45.1 1.9 %collective-permute-start.7 = (f32[8,128]{1,0:T(8,128)S(1)}, f32[8,128]{1,0:T(8,128)S(1)}, u32[]{:S(2)}, u32[]{:S(2)}) collective-permute-start(f32[8,128]{1,0:T(8,128)S(1)} %backward.3.w), channel_id=1, source_target_pairs={{0,64},{64,0},{128,192},{192,128},{256,320},{320,256},{384,448},{4... | collective-permute-start | bytes 12296 | tf_op jit(solution)/shard_map/ppermute | solution.py:44
  47.1 1.0 %collective-permute-done.7.near = f32[8,128]{1,0:T(8,128)S(1)} collective-permute-done((f32[8,128]{1,0:T(8,128)S(1)}, f32[8,128]{1,0:T(8,128)S(1)}, u32[]{:S(2)}, u32[]{:S(2)}) %collective-permute-start.7) | collective-permute-done | bytes 4128 | tf_op jit(solution)/shard_map/ppermute | solution.py:44
  48.1 0.1 sums.1
  48.2 8.0 %all_to_all.16.back = f32[8,8,128]{2,1,0:T(8,128)S(1)} all-to-all(f32[8,8,128]{2,1,0:T(8,128)S(1)} %sums.1), channel_id=1, replica_groups=mesh['wave_0'=4,'wave_1'=2,'plane_0'=4,'plane_1'=16] {'wave_0','wave_1'}, dimensions={0} | all-to-all | bytes 65536 | tf_op jit(solution)/shard_map/all_to_all | solution.py:223
  56.3 31.0 %all_to_all.17.everyone = f32[64,1,128]{2,1,0:T(1,128)S(1)} all-to-all(f32[64,1,128]{2,1,0:T(1,128)S(1)} %share.1), channel_id=1, replica_groups=mesh['wave_0'=4,'wave_1'=2,'plane_0'=4,'plane_1'=16] {'plane_0','plane_1'}, dimensions={0} | all-to-all | bytes 65536 | tf_op jit(solution)/shard_map/all_to_all | solution.py:225
  87.3 1.0 %final.1 = (f32[1,8,128]{2,1,0:T(8,128)}, f32[1,8,128]{2,1,0:T(8,128)}) custom-call(f32[64,1,128]{2,1,0:T(1,128)S(1)} %all_to_all.17.everyone, f32[8,8,128]{2,1,0:T(8,128)S(1)} %all_to_all.16.back, f32[8,128]{1,0:T(8,128)S(1)} %get-tuple-element.9.r), custom_call_target="tpu_custom_call" | custom-call | tf_op jit(solution)/shard_map/final/pallas_call | solution.py:179
  (15 shorter events, 0.7 us)
Async XLA Ops:
  22.1 4.9 %collective-permute-start.1 = (f32[8,128]{1,0:T(8,128)S(1)}, f32[8,128]{1,0:T(8,128)S(1)}, u32[]{:S(2)}, u32[]{:S(2)}) collective-permute-start(f32[8,128]{1,0:T(8,128)S(1)} %first.1.half), channel_id=1, source_target_pairs={{64,128},{128,64},{192,256},{256,192},{320,384},{384,320},{448,449... | collective-permute-start | bytes 12296 | tf_op jit(solution)/shard_map/ppermute | solution.py:43
  24.8 3.1 %collective-permute-start = (f32[8,128]{1,0:T(8,128)S(1)}, f32[8,128]{1,0:T(8,128)S(1)}, u32[]{:S(2)}, u32[]{:S(2)}) collective-permute-start(f32[8,128]{1,0:T(8,128)S(1)} %first.1.half), channel_id=1, source_target_pairs={{0,64},{64,0},{128,192},{192,128},{256,320},{320,256},{384,448},{4... | collective-permute-start | bytes 12296 | tf_op jit(solution)/shard_map/ppermute | solution.py:44
  28.7 4.9 %collective-permute-start.2 = (f32[8,128]{1,0:T(8,128)S(1)}, f32[8,128]{1,0:T(8,128)S(1)}, u32[]{:S(2)}, u32[]{:S(2)}) collective-permute-start(f32[8,128]{1,0:T(8,128)S(1)} %backward.2.z), channel_id=1, source_target_pairs={{64,128},{128,64},{192,256},{256,192},{320,384},{384,320},{448,449... | collective-permute-start | bytes 12296 | tf_op jit(solution)/shard_map/ppermute | solution.py:43
  31.6 3.1 %collective-permute-start.3 = (f32[8,128]{1,0:T(8,128)S(1)}, f32[8,128]{1,0:T(8,128)S(1)}, u32[]{:S(2)}, u32[]{:S(2)}) collective-permute-start(f32[8,128]{1,0:T(8,128)S(1)} %backward.2.z), channel_id=1, source_target_pairs={{0,64},{64,0},{128,192},{192,128},{256,320},{320,256},{384,448},{4... | collective-permute-start | bytes 12296 | tf_op jit(solution)/shard_map/ppermute | solution.py:44
  35.6 4.9 %collective-permute-start.5 = (f32[8,128]{1,0:T(8,128)S(1)}, f32[8,128]{1,0:T(8,128)S(1)}, u32[]{:S(2)}, u32[]{:S(2)}) collective-permute-start(f32[8,128]{1,0:T(8,128)S(1)} %get-tuple-element.8.half), channel_id=1, source_target_pairs={{64,128},{128,64},{192,256},{256,192},{320,384},{384,320},{448,449... | collective-permute-start | bytes 12296 | tf_op jit(solution)/shard_map/ppermute | solution.py:43
  38.2 3.1 %collective-permute-start.4 = (f32[8,128]{1,0:T(8,128)S(1)}, f32[8,128]{1,0:T(8,128)S(1)}, u32[]{:S(2)}, u32[]{:S(2)}) collective-permute-start(f32[8,128]{1,0:T(8,128)S(1)} %get-tuple-element.8.half), channel_id=1, source_target_pairs={{0,64},{64,0},{128,192},{192,128},{256,320},{320,256},{384,448},{4... | collective-permute-start | bytes 12296 | tf_op jit(solution)/shard_map/ppermute | solution.py:44
  42.2 4.9 %collective-permute-start.6 = (f32[8,128]{1,0:T(8,128)S(1)}, f32[8,128]{1,0:T(8,128)S(1)}, u32[]{:S(2)}, u32[]{:S(2)}) collective-permute-start(f32[8,128]{1,0:T(8,128)S(1)} %backward.3.w), channel_id=1, source_target_pairs={{64,128},{128,64},{192,256},{256,192},{320,384},{384,320},{448,449... | collective-permute-start | bytes 12296 | tf_op jit(solution)/shard_map/ppermute | solution.py:43
  45.1 3.1 %collective-permute-start.7 = (f32[8,128]{1,0:T(8,128)S(1)}, f32[8,128]{1,0:T(8,128)S(1)}, u32[]{:S(2)}, u32[]{:S(2)}) collective-permute-start(f32[8,128]{1,0:T(8,128)S(1)} %backward.3.w), channel_id=1, source_target_pairs={{0,64},{64,0},{128,192},{192,128},{256,320},{320,256},{384,448},{4... | collective-permute-start | bytes 12296 | tf_op jit(solution)/shard_map/ppermute | solution.py:44

commit v4 on v3

--- a/solution.py
+++ b/solution.py
@@ -21,10 +21,13 @@
 HBM = pl.BlockSpec(memory_space=pl.ANY)
 
 
+EVEN = (7, 6, 5, 4, 3, 2, 0, 1)
+ODD = EVEN[::-1]
+
+
 def chain_device(position):
     plane, k = divmod(position, NW)
-    wave = k if plane % 2 == 0 else NW - 1 - k
-    return wave * NP + plane
+    return (ODD if plane % 2 else EVEN)[k] * NP + plane
 
 
 def swap_pairs(first):
@@ -55,7 +58,7 @@
 
 def turned(j):
     parity = lax.axis_index("plane_1") % 2
-    return j + parity * (NW - 1 - 2 * j)
+    return EVEN[j] + parity * (ODD[j] - EVEN[j])
 
 
 def pack_kernel(inverse, right, cz, cx, cy, packed, r_out, cz_v, cx_v, cy_v, sems, small):

time: 88.8 us -> 86.6 us (0.975)
  blocking collectives: 58.4 us -> 55.5 us
  starting transfers between devices: 18.8 us -> 20.9 us
  waiting for transfers between devices: 4.1 us -> 2.78 us
    ppermute x4, starting transfers between devices: 7.68 us -> 11.7 us  [neighbours(): near = lax.ppermute(values, ALL, NEAR)]
    all_to_all x1, blocking collectives: 31 us -> 28.1 us  [on_device(): lax.all_to_all(share, PLANE, split_axis=0, concat_axis=0, tiled=True)]
    ppermute x4, starting transfers between devices: 11.1 us -> 9.18 us  [neighbours(): far = lax.ppermute(values, ALL, FAR)]
    ppermute x4, waiting for transfers between devices: 3.68 us -> 2.77 us  [neighbours(): near = lax.ppermute(values, ALL, NEAR)]
  transfers between devices with their start and end apart: 8 -> 8, of which waited for: 6 -> 4; matrix products, arithmetic and copies ran while one was open for 0% -> 0% of each run, Pallas kernels for 0% -> 0%
where the time goes in v4:
time: 86.6 us; the launch traced here: 86.1 us
  blocking collectives  55.5 us (64%)
  starting transfers between devices  20.9 us (24%)
  Pallas kernels  5.44 us (6%)
  waiting for transfers between devices  2.78 us (3%)
    all_to_all x1, blocking collectives, on_device(): lax.all_to_all(share, PLANE, split_axis=0, concat_axis=0, tiled=True)  28.1 us
    all_to_all x1, blocking collectives, on_device(): lax.all_to_all(packed, WAVE, split_axis=0, concat_axis=0, tiled=True)  19.4 us
    ppermute x4, starting transfers between devices, neighbours(): near = lax.ppermute(values, ALL, NEAR)  11.7 us
    ppermute x4, starting transfers between devices, neighbours(): far = lax.ppermute(values, ALL, FAR)  9.18 us
    all_to_all x1, blocking collectives, on_device(): back = lax.all_to_all(back, WAVE, split_axis=0, concat_axis=0, tiled=True)  7.96 us
    pallas_call x7, Pallas kernels, call(): pl.pallas_call(kernel, out_shape=out, in_specs=[VMEM] * len(args), out_sp...  4.21 us
    ppermute x4, waiting for transfers between devices, neighbours(): near = lax.ppermute(values, ALL, NEAR)  2.77 us
  transfers between devices with their start and end apart: 8, of which 4 were waited for; matrix products, arithmetic and copies ran while one was open for 0% of the time, Pallas kernels for 0%

profile of v4, /device:TPU:1, one launch (start us, length us, event | category | flops | bytes accessed | tf_op | source)
XLA Modules:
  0.0 86.1 jit_solution(4018168124126707215)
XLA Ops:
  0.6 1.2 %pack.1 = (f32[8,136,128]{2,1,0:T(8,128)S(1)}, f32[8,128]{1,0:T(8,128)S(1)}) custom-call(f32[1,8,128,128]{3,2,1,0:T(8,128)} %inverse.1, f32[1,8,128]{2,1,0:T(8,128)} %right.1, f32[1,8,128]{2,1,0:T(8,128)} %cz.1, f32[8,128]{1,0:T(8,128)} %cx.1, f32[1,128]{1,0:T(1,128)} %cy.1), custom_call_target="tpu_custom_call" | custom-call | tf_op jit(solution)/shard_map/pack/pallas_call | solution.py:91
  1.9 19.4 %all_to_all.15.columns = f32[8,136,128]{2,1,0:T(8,128)S(1)} all-to-all(f32[8,136,128]{2,1,0:T(8,128)S(1)} %get-tuple-element.6), channel_id=1, replica_groups=mesh['wave_0'=4,'wave_1'=2,'plane_0'=4,'plane_1'=16] {'wave_0','wave_1'}, dimensions={0} | all-to-all | bytes 1114112 | tf_op jit(solution)/shard_map/all_to_all | solution.py:205
  21.3 0.8 first.1.half
  22.1 1.9 %collective-permute-start.1 = (f32[8,128]{1,0:T(8,128)S(1)}, f32[8,128]{1,0:T(8,128)S(1)}, u32[]{:S(2)}, u32[]{:S(2)}) collective-permute-start(f32[8,128]{1,0:T(8,128)S(1)} %first.1.half), channel_id=1, source_target_pairs={{384,320},{320,384},{256,192},{192,256},{128,0},{0,128},{64,65},{6... | collective-permute-start | bytes 12296 | tf_op jit(solution)/shard_map/ppermute | solution.py:46
  24.1 3.0 %collective-permute-start = (f32[8,128]{1,0:T(8,128)S(1)}, f32[8,128]{1,0:T(8,128)S(1)}, u32[]{:S(2)}, u32[]{:S(2)}) collective-permute-start(f32[8,128]{1,0:T(8,128)S(1)} %first.1.half), channel_id=1, source_target_pairs={{448,384},{384,448},{320,256},{256,320},{192,128},{128,192},{0,64}... | collective-permute-start | bytes 12296 | tf_op jit(solution)/shard_map/ppermute | solution.py:47
  27.2 0.1 multiply_add_fusion.1
  27.3 0.6 collective-permute-done.near
  27.9 0.8 backward.2.z
  28.8 2.6 %collective-permute-start.2 = (f32[8,128]{1,0:T(8,128)S(1)}, f32[8,128]{1,0:T(8,128)S(1)}, u32[]{:S(2)}, u32[]{:S(2)}) collective-permute-start(f32[8,128]{1,0:T(8,128)S(1)} %backward.2.z), channel_id=1, source_target_pairs={{384,320},{320,384},{256,192},{192,256},{128,0},{0,128},{64,65},{6... | collective-permute-start | bytes 12296 | tf_op jit(solution)/shard_map/ppermute | solution.py:46
  31.4 3.0 %collective-permute-start.3 = (f32[8,128]{1,0:T(8,128)S(1)}, f32[8,128]{1,0:T(8,128)S(1)}, u32[]{:S(2)}, u32[]{:S(2)}) collective-permute-start(f32[8,128]{1,0:T(8,128)S(1)} %backward.2.z), channel_id=1, source_target_pairs={{448,384},{384,448},{320,256},{256,320},{192,128},{128,192},{0,64}... | collective-permute-start | bytes 12296 | tf_op jit(solution)/shard_map/ppermute | solution.py:47
  34.5 0.7 collective-permute-done.3.near
  35.2 0.8 image.1
  36.1 1.9 %collective-permute-start.5 = (f32[8,128]{1,0:T(8,128)S(1)}, f32[8,128]{1,0:T(8,128)S(1)}, u32[]{:S(2)}, u32[]{:S(2)}) collective-permute-start(f32[8,128]{1,0:T(8,128)S(1)} %get-tuple-element.8.half), channel_id=1, source_target_pairs={{384,320},{320,384},{256,192},{192,256},{128,0},{0,128},{64,65},{6... | collective-permute-start | bytes 12296 | tf_op jit(solution)/shard_map/ppermute | solution.py:46
  38.0 2.8 %collective-permute-start.4 = (f32[8,128]{1,0:T(8,128)S(1)}, f32[8,128]{1,0:T(8,128)S(1)}, u32[]{:S(2)}, u32[]{:S(2)}) collective-permute-start(f32[8,128]{1,0:T(8,128)S(1)} %get-tuple-element.8.half), channel_id=1, source_target_pairs={{448,384},{384,448},{320,256},{256,320},{192,128},{128,192},{0,64}... | collective-permute-start | bytes 12296 | tf_op jit(solution)/shard_map/ppermute | solution.py:47
  40.8 0.1 multiply_add_fusion.base
  40.9 0.7 collective-permute-done.4.near
  41.6 0.8 backward.3.w
  42.5 2.8 %collective-permute-start.6 = (f32[8,128]{1,0:T(8,128)S(1)}, f32[8,128]{1,0:T(8,128)S(1)}, u32[]{:S(2)}, u32[]{:S(2)}) collective-permute-start(f32[8,128]{1,0:T(8,128)S(1)} %backward.3.w), channel_id=1, source_target_pairs={{384,320},{320,384},{256,192},{192,256},{128,0},{0,128},{64,65},{6... | collective-permute-start | bytes 12296 | tf_op jit(solution)/shard_map/ppermute | solution.py:46
  45.3 2.8 %collective-permute-start.7 = (f32[8,128]{1,0:T(8,128)S(1)}, f32[8,128]{1,0:T(8,128)S(1)}, u32[]{:S(2)}, u32[]{:S(2)}) collective-permute-start(f32[8,128]{1,0:T(8,128)S(1)} %backward.3.w), channel_id=1, source_target_pairs={{448,384},{384,448},{320,256},{256,320},{192,128},{128,192},{0,64}... | collective-permute-start | bytes 12296 | tf_op jit(solution)/shard_map/ppermute | solution.py:47
  48.2 0.7 collective-permute-done.7.near
  48.9 0.1 sums.1
  49.0 8.0 %all_to_all.16.back = f32[8,8,128]{2,1,0:T(8,128)S(1)} all-to-all(f32[8,8,128]{2,1,0:T(8,128)S(1)} %sums.1), channel_id=1, replica_groups=mesh['wave_0'=4,'wave_1'=2,'plane_0'=4,'plane_1'=16] {'wave_0','wave_1'}, dimensions={0} | all-to-all | bytes 65536 | tf_op jit(solution)/shard_map/all_to_all | solution.py:226
  57.0 28.1 %all_to_all.17.everyone = f32[64,1,128]{2,1,0:T(1,128)S(1)} all-to-all(f32[64,1,128]{2,1,0:T(1,128)S(1)} %share.1), channel_id=1, replica_groups=mesh['wave_0'=4,'wave_1'=2,'plane_0'=4,'plane_1'=16] {'plane_0','plane_1'}, dimensions={0} | all-to-all | bytes 65536 | tf_op jit(solution)/shard_map/all_to_all | solution.py:228
  85.1 1.0 %final.1 = (f32[1,8,128]{2,1,0:T(8,128)}, f32[1,8,128]{2,1,0:T(8,128)}) custom-call(f32[64,1,128]{2,1,0:T(1,128)S(1)} %all_to_all.17.everyone, f32[8,8,128]{2,1,0:T(8,128)S(1)} %all_to_all.16.back, f32[8,128]{1,0:T(8,128)S(1)} %get-tuple-element.9.r), custom_call_target="tpu_custom_call" | custom-call | tf_op jit(solution)/shard_map/final/pallas_call | solution.py:182
  (15 shorter events, 0.6 us)
Async XLA Ops:
  22.1 5.1 %collective-permute-start.1 = (f32[8,128]{1,0:T(8,128)S(1)}, f32[8,128]{1,0:T(8,128)S(1)}, u32[]{:S(2)}, u32[]{:S(2)}) collective-permute-start(f32[8,128]{1,0:T(8,128)S(1)} %first.1.half), channel_id=1, source_target_pairs={{384,320},{320,384},{256,192},{192,256},{128,0},{0,128},{64,65},{6... | collective-permute-start | bytes 12296 | tf_op jit(solution)/shard_map/ppermute | solution.py:46
  24.1 3.8 %collective-permute-start = (f32[8,128]{1,0:T(8,128)S(1)}, f32[8,128]{1,0:T(8,128)S(1)}, u32[]{:S(2)}, u32[]{:S(2)}) collective-permute-start(f32[8,128]{1,0:T(8,128)S(1)} %first.1.half), channel_id=1, source_target_pairs={{448,384},{384,448},{320,256},{256,320},{192,128},{128,192},{0,64}... | collective-permute-start | bytes 12296 | tf_op jit(solution)/shard_map/ppermute | solution.py:47
  28.8 5.7 %collective-permute-start.2 = (f32[8,128]{1,0:T(8,128)S(1)}, f32[8,128]{1,0:T(8,128)S(1)}, u32[]{:S(2)}, u32[]{:S(2)}) collective-permute-start(f32[8,128]{1,0:T(8,128)S(1)} %backward.2.z), channel_id=1, source_target_pairs={{384,320},{320,384},{256,192},{192,256},{128,0},{0,128},{64,65},{6... | collective-permute-start | bytes 12296 | tf_op jit(solution)/shard_map/ppermute | solution.py:46
  31.4 3.8 %collective-permute-start.3 = (f32[8,128]{1,0:T(8,128)S(1)}, f32[8,128]{1,0:T(8,128)S(1)}, u32[]{:S(2)}, u32[]{:S(2)}) collective-permute-start(f32[8,128]{1,0:T(8,128)S(1)} %backward.2.z), channel_id=1, source_target_pairs={{448,384},{384,448},{320,256},{256,320},{192,128},{128,192},{0,64}... | collective-permute-start | bytes 12296 | tf_op jit(solution)/shard_map/ppermute | solution.py:47
  36.1 4.8 %collective-permute-start.5 = (f32[8,128]{1,0:T(8,128)S(1)}, f32[8,128]{1,0:T(8,128)S(1)}, u32[]{:S(2)}, u32[]{:S(2)}) collective-permute-start(f32[8,128]{1,0:T(8,128)S(1)} %get-tuple-element.8.half), channel_id=1, source_target_pairs={{384,320},{320,384},{256,192},{192,256},{128,0},{0,128},{64,65},{6... | collective-permute-start | bytes 12296 | tf_op jit(solution)/shard_map/ppermute | solution.py:46
  38.0 3.6 %collective-permute-start.4 = (f32[8,128]{1,0:T(8,128)S(1)}, f32[8,128]{1,0:T(8,128)S(1)}, u32[]{:S(2)}, u32[]{:S(2)}) collective-permute-start(f32[8,128]{1,0:T(8,128)S(1)} %get-tuple-element.8.half), channel_id=1, source_target_pairs={{448,384},{384,448},{320,256},{256,320},{192,128},{128,192},{0,64}... | collective-permute-start | bytes 12296 | tf_op jit(solution)/shard_map/ppermute | solution.py:47
  42.5 5.7 %collective-permute-start.6 = (f32[8,128]{1,0:T(8,128)S(1)}, f32[8,128]{1,0:T(8,128)S(1)}, u32[]{:S(2)}, u32[]{:S(2)}) collective-permute-start(f32[8,128]{1,0:T(8,128)S(1)} %backward.3.w), channel_id=1, source_target_pairs={{384,320},{320,384},{256,192},{192,256},{128,0},{0,128},{64,65},{6... | collective-permute-start | bytes 12296 | tf_op jit(solution)/shard_map/ppermute | solution.py:46
  45.3 3.6 %collective-permute-start.7 = (f32[8,128]{1,0:T(8,128)S(1)}, f32[8,128]{1,0:T(8,128)S(1)}, u32[]{:S(2)}, u32[]{:S(2)}) collective-permute-start(f32[8,128]{1,0:T(8,128)S(1)} %backward.3.w), channel_id=1, source_target_pairs={{448,384},{384,448},{320,256},{256,320},{192,128},{128,192},{0,64}... | collective-permute-start | bytes 12296 | tf_op jit(solution)/shard_map/ppermute | solution.py:47

commit v5 on v4

--- a/solution.py
+++ b/solution.py
@@ -141,29 +141,30 @@
         out[x : x + 1, :] = previous
 
 
-def sums_kernel(r, z, q, w, local, far, near, cy, back):
+def sums_kernel(r, z, q, w, local, far, near, cy, p, share):
     z_a, q_a, w_a = z[...], q[...], w[...]
     p_a = local[...] - cy[...] * (far[...] + near[...])
+    p[...] = p_a
     lane = lax.broadcasted_iota(jnp.int32, (1, B), 1)
     row = jnp.zeros((1, B), jnp.float32)
     for k, product in enumerate((z_a * r[...], z_a * q_a, w_a * r[...], w_a * q_a, w_a * p_a)):
         total = jnp.sum(jnp.sum(product, axis=0, keepdims=True), axis=1, keepdims=True)
         row = jnp.where(lane == k, total, row)
+    share[...] = jnp.broadcast_to(row[None], (NP, 1, B))
+
+
+def carry_kernel(everyone, z, q, w, p, back):
+    row = jnp.sum(everyone[...], axis=0)
     rest = jnp.zeros((3, B), jnp.float32)
     for x in range(NW):
         at = slice(x, x + 1)
-        back[x] = jnp.concatenate([z_a[at], q_a[at], w_a[at], p_a[at], row, rest], axis=0)
-
-
-def share_kernel(back, out):
-    part = back[0, 4:5, :]
+        back[x] = jnp.concatenate([z[at], q[at], w[at], p[at], row, rest], axis=0)
+
+
+def final_kernel(back, r, solution_out, residual_out):
+    total = back[0, 4:5, :]
     for x in range(1, NW):
-        part = part + back[x, 4:5, :]
-    out[...] = jnp.broadcast_to(part[None], (NP, 1, B))
-
-
-def final_kernel(everyone, back, r, solution_out, residual_out):
-    total = jnp.sum(everyone[...], axis=0)
+        total = total + back[x, 4:5, :]
     zr, zq, wr, wq, wp = (total[:, k : k + 1] for k in range(5))
     first = zr / zq
     ratio = wq / zq
@@ -222,12 +223,13 @@
     far, near = neighbours(half)
     w = local(backward_kernel, field, "backward")(columns, before(q, half), near, far, cy, half)
     far, near = neighbours(w)
-    back = local(sums_kernel, on_chip(NW, 8, B), "sums")(r, z, q, w, image_part(w), far, near, cy)
+    sums = (field, on_chip(NP, 1, B))
+    p, share = local(sums_kernel, sums, "sums")(r, z, q, w, image_part(w), far, near, cy)
+    everyone = lax.all_to_all(share, PLANE, split_axis=0, concat_axis=0, tiled=True)
+    back = local(carry_kernel, on_chip(NW, 8, B), "carry")(everyone, z, q, w, p)
     back = lax.all_to_all(back, WAVE, split_axis=0, concat_axis=0, tiled=True)
-    share = local(share_kernel, on_chip(NP, 1, B), "share")(back)
-    everyone = lax.all_to_all(share, PLANE, split_axis=0, concat_axis=0, tiled=True)
     out = f32(1, NW, B)
-    return local(final_kernel, (out, out), "final")(everyone, back, own)
+    return local(final_kernel, (out, out), "final")(back, own)
 
 
 def solution(mesh):

time: 86.6 us -> 90.4 us (1.044)
  waiting for transfers between devices: 2.78 us -> 5.54 us
  blocking collectives: 55.5 us -> 57.2 us
    ppermute x4, waiting for transfers between devices: 0.01 us -> 4.2 us  [neighbours(): far = lax.ppermute(values, ALL, FAR)]
    all_to_all x1, blocking collectives: 7.96 us -> 9.83 us  [on_device(): back = lax.all_to_all(back, WAVE, split_axis=0, concat_axis=0, tiled=True)]
    ppermute x4, waiting for transfers between devices: 2.77 us -> 1.34 us  [neighbours(): near = lax.ppermute(values, ALL, NEAR)]
where the time goes in v5:
time: 90.4 us; the launch traced here: 89.9 us
  blocking collectives  57.2 us (63%)
  starting transfers between devices  20.3 us (22%)
  waiting for transfers between devices  5.54 us (6%)
  Pallas kernels  5.44 us (6%)
    all_to_all x1, blocking collectives, on_device(): lax.all_to_all(share, PLANE, split_axis=0, concat_axis=0, tiled=True)  27.9 us
    all_to_all x1, blocking collectives, on_device(): lax.all_to_all(packed, WAVE, split_axis=0, concat_axis=0, tiled=True)  19.4 us
    ppermute x4, starting transfers between devices, neighbours(): near = lax.ppermute(values, ALL, NEAR)  11.7 us
    all_to_all x1, blocking collectives, on_device(): back = lax.all_to_all(back, WAVE, split_axis=0, concat_axis=0, tiled=True)  9.83 us
    ppermute x4, starting transfers between devices, neighbours(): far = lax.ppermute(values, ALL, FAR)  8.62 us
    pallas_call x7, Pallas kernels, call(): pl.pallas_call(kernel, out_shape=out, in_specs=[VMEM] * len(args), out_sp...  4.21 us
    ppermute x4, waiting for transfers between devices, neighbours(): far = lax.ppermute(values, ALL, FAR)  4.2 us
  transfers between devices with their start and end apart: 8, of which 4 were waited for; matrix products, arithmetic and copies ran while one was open for 0% of the time, Pallas kernels for 0%

profile of v5, /device:TPU:1, one launch (start us, length us, event | category | flops | bytes accessed | tf_op | source)
XLA Modules:
  0.0 89.9 jit_solution(15542707804062598962)
XLA Ops:
  0.6 1.2 %pack.1 = (f32[8,136,128]{2,1,0:T(8,128)S(1)}, f32[8,128]{1,0:T(8,128)S(1)}) custom-call(f32[1,8,128,128]{3,2,1,0:T(8,128)} %inverse.1, f32[1,8,128]{2,1,0:T(8,128)} %right.1, f32[1,8,128]{2,1,0:T(8,128)} %cz.1, f32[8,128]{1,0:T(8,128)} %cx.1, f32[1,128]{1,0:T(1,128)} %cy.1), custom_call_target="tpu_custom_call" | custom-call | tf_op jit(solution)/shard_map/pack/pallas_call | solution.py:91
  1.9 19.4 %all_to_all.15.columns = f32[8,136,128]{2,1,0:T(8,128)S(1)} all-to-all(f32[8,136,128]{2,1,0:T(8,128)S(1)} %get-tuple-element.8), channel_id=1, replica_groups=mesh['wave_0'=4,'wave_1'=2,'plane_0'=4,'plane_1'=16] {'wave_0','wave_1'}, dimensions={0} | all-to-all | bytes 1114112 | tf_op jit(solution)/shard_map/all_to_all | solution.py:206
  21.3 0.8 first.1.half
  22.1 1.9 %collective-permute-start.1 = (f32[8,128]{1,0:T(8,128)S(1)}, f32[8,128]{1,0:T(8,128)S(1)}, u32[]{:S(2)}, u32[]{:S(2)}) collective-permute-start(f32[8,128]{1,0:T(8,128)S(1)} %first.1.half), channel_id=1, source_target_pairs={{384,320},{320,384},{256,192},{192,256},{128,0},{0,128},{64,65},{6... | collective-permute-start | bytes 12296 | tf_op jit(solution)/shard_map/ppermute | solution.py:46
  24.1 3.0 %collective-permute-start = (f32[8,128]{1,0:T(8,128)S(1)}, f32[8,128]{1,0:T(8,128)S(1)}, u32[]{:S(2)}, u32[]{:S(2)}) collective-permute-start(f32[8,128]{1,0:T(8,128)S(1)} %first.1.half), channel_id=1, source_target_pairs={{448,384},{384,448},{320,256},{256,320},{192,128},{128,192},{0,64}... | collective-permute-start | bytes 12296 | tf_op jit(solution)/shard_map/ppermute | solution.py:47
  27.2 0.1 multiply_add_fusion.1
  27.3 0.6 collective-permute-done.near
  27.9 0.8 backward.2.z
  28.8 2.2 %collective-permute-start.3 = (f32[8,128]{1,0:T(8,128)S(1)}, f32[8,128]{1,0:T(8,128)S(1)}, u32[]{:S(2)}, u32[]{:S(2)}) collective-permute-start(f32[8,128]{1,0:T(8,128)S(1)} %backward.2.z), channel_id=1, source_target_pairs={{448,384},{384,448},{320,256},{256,320},{192,128},{128,192},{0,64}... | collective-permute-start | bytes 12296 | tf_op jit(solution)/shard_map/ppermute | solution.py:47
  31.0 2.4 %collective-permute-start.2 = (f32[8,128]{1,0:T(8,128)S(1)}, f32[8,128]{1,0:T(8,128)S(1)}, u32[]{:S(2)}, u32[]{:S(2)}) collective-permute-start(f32[8,128]{1,0:T(8,128)S(1)} %backward.2.z), channel_id=1, source_target_pairs={{384,320},{320,384},{256,192},{192,256},{128,0},{0,128},{64,65},{6... | collective-permute-start | bytes 12296 | tf_op jit(solution)/shard_map/ppermute | solution.py:46
  33.5 1.9 %collective-permute-done.2.far = f32[8,128]{1,0:T(8,128)S(1)} collective-permute-done((f32[8,128]{1,0:T(8,128)S(1)}, f32[8,128]{1,0:T(8,128)S(1)}, u32[]{:S(2)}, u32[]{:S(2)}) %collective-permute-start.2) | collective-permute-done | bytes 4128 | tf_op jit(solution)/shard_map/ppermute | solution.py:46
  35.4 0.8 image.1
  36.3 2.4 %collective-permute-start.5 = (f32[8,128]{1,0:T(8,128)S(1)}, f32[8,128]{1,0:T(8,128)S(1)}, u32[]{:S(2)}, u32[]{:S(2)}) collective-permute-start(f32[8,128]{1,0:T(8,128)S(1)} %get-tuple-element.10.half), channel_id=1, source_target_pairs={{384,320},{320,384},{256,192},{192,256},{128,0},{0,128},{64,65},{6... | collective-permute-start | bytes 12296 | tf_op jit(solution)/shard_map/ppermute | solution.py:46
  38.7 4.2 %collective-permute-start.4 = (f32[8,128]{1,0:T(8,128)S(1)}, f32[8,128]{1,0:T(8,128)S(1)}, u32[]{:S(2)}, u32[]{:S(2)}) collective-permute-start(f32[8,128]{1,0:T(8,128)S(1)} %get-tuple-element.10.half), channel_id=1, source_target_pairs={{448,384},{384,448},{320,256},{256,320},{192,128},{128,192},{0,64}... | collective-permute-start | bytes 12296 | tf_op jit(solution)/shard_map/ppermute | solution.py:47
  42.9 0.1 multiply_add_fusion.base
  42.9 0.7 collective-permute-done.4.near
  43.7 0.8 backward.3.w
  44.5 2.2 %collective-permute-start.7 = (f32[8,128]{1,0:T(8,128)S(1)}, f32[8,128]{1,0:T(8,128)S(1)}, u32[]{:S(2)}, u32[]{:S(2)}) collective-permute-start(f32[8,128]{1,0:T(8,128)S(1)} %backward.3.w), channel_id=1, source_target_pairs={{448,384},{384,448},{320,256},{256,320},{192,128},{128,192},{0,64}... | collective-permute-start | bytes 12296 | tf_op jit(solution)/shard_map/ppermute | solution.py:47
  46.8 1.9 %collective-permute-start.6 = (f32[8,128]{1,0:T(8,128)S(1)}, f32[8,128]{1,0:T(8,128)S(1)}, u32[]{:S(2)}, u32[]{:S(2)}) collective-permute-start(f32[8,128]{1,0:T(8,128)S(1)} %backward.3.w), channel_id=1, source_target_pairs={{384,320},{320,384},{256,192},{192,256},{128,0},{0,128},{64,65},{6... | collective-permute-start | bytes 12296 | tf_op jit(solution)/shard_map/ppermute | solution.py:46
  48.8 2.3 %collective-permute-done.6.far = f32[8,128]{1,0:T(8,128)S(1)} collective-permute-done((f32[8,128]{1,0:T(8,128)S(1)}, f32[8,128]{1,0:T(8,128)S(1)}, u32[]{:S(2)}, u32[]{:S(2)}) %collective-permute-start.6) | collective-permute-done | bytes 4128 | tf_op jit(solution)/shard_map/ppermute | solution.py:46
  51.1 0.1 sums.1
  51.2 27.9 %all_to_all.16.everyone = f32[64,1,128]{2,1,0:T(1,128)S(1)} all-to-all(f32[64,1,128]{2,1,0:T(1,128)S(1)} %get-tuple-element.11), channel_id=1, replica_groups=mesh['wave_0'=4,'wave_1'=2,'plane_0'=4,'plane_1'=16] {'plane_0','plane_1'}, dimensions={0} | all-to-all | bytes 65536 | tf_op jit(solution)/shard_map/all_to_all | solution.py:228
  79.2 9.8 %all_to_all.17.back = f32[8,8,128]{2,1,0:T(8,128)S(1)} all-to-all(f32[8,8,128]{2,1,0:T(8,128)S(1)} %carry.1), channel_id=1, replica_groups=mesh['wave_0'=4,'wave_1'=2,'plane_0'=4,'plane_1'=16] {'wave_0','wave_1'}, dimensions={0} | all-to-all | bytes 65536 | tf_op jit(solution)/shard_map/all_to_all | solution.py:230
  89.0 0.9 final.1
  (15 shorter events, 0.6 us)
Async XLA Ops:
  22.1 5.1 %collective-permute-start.1 = (f32[8,128]{1,0:T(8,128)S(1)}, f32[8,128]{1,0:T(8,128)S(1)}, u32[]{:S(2)}, u32[]{:S(2)}) collective-permute-start(f32[8,128]{1,0:T(8,128)S(1)} %first.1.half), channel_id=1, source_target_pairs={{384,320},{320,384},{256,192},{192,256},{128,0},{0,128},{64,65},{6... | collective-permute-start | bytes 12296 | tf_op jit(solution)/shard_map/ppermute | solution.py:46
  24.1 3.8 %collective-permute-start = (f32[8,128]{1,0:T(8,128)S(1)}, f32[8,128]{1,0:T(8,128)S(1)}, u32[]{:S(2)}, u32[]{:S(2)}) collective-permute-start(f32[8,128]{1,0:T(8,128)S(1)} %first.1.half), channel_id=1, source_target_pairs={{448,384},{384,448},{320,256},{256,320},{192,128},{128,192},{0,64}... | collective-permute-start | bytes 12296 | tf_op jit(solution)/shard_map/ppermute | solution.py:47
  28.8 4.7 %collective-permute-start.3 = (f32[8,128]{1,0:T(8,128)S(1)}, f32[8,128]{1,0:T(8,128)S(1)}, u32[]{:S(2)}, u32[]{:S(2)}) collective-permute-start(f32[8,128]{1,0:T(8,128)S(1)} %backward.2.z), channel_id=1, source_target_pairs={{448,384},{384,448},{320,256},{256,320},{192,128},{128,192},{0,64}... | collective-permute-start | bytes 12296 | tf_op jit(solution)/shard_map/ppermute | solution.py:47
  31.0 4.4 %collective-permute-start.2 = (f32[8,128]{1,0:T(8,128)S(1)}, f32[8,128]{1,0:T(8,128)S(1)}, u32[]{:S(2)}, u32[]{:S(2)}) collective-permute-start(f32[8,128]{1,0:T(8,128)S(1)} %backward.2.z), channel_id=1, source_target_pairs={{384,320},{320,384},{256,192},{192,256},{128,0},{0,128},{64,65},{6... | collective-permute-start | bytes 12296 | tf_op jit(solution)/shard_map/ppermute | solution.py:46
  36.3 6.7 %collective-permute-start.5 = (f32[8,128]{1,0:T(8,128)S(1)}, f32[8,128]{1,0:T(8,128)S(1)}, u32[]{:S(2)}, u32[]{:S(2)}) collective-permute-start(f32[8,128]{1,0:T(8,128)S(1)} %get-tuple-element.10.half), channel_id=1, source_target_pairs={{384,320},{320,384},{256,192},{192,256},{128,0},{0,128},{64,65},{6... | collective-permute-start | bytes 12296 | tf_op jit(solution)/shard_map/ppermute | solution.py:46
  38.7 5.0 %collective-permute-start.4 = (f32[8,128]{1,0:T(8,128)S(1)}, f32[8,128]{1,0:T(8,128)S(1)}, u32[]{:S(2)}, u32[]{:S(2)}) collective-permute-start(f32[8,128]{1,0:T(8,128)S(1)} %get-tuple-element.10.half), channel_id=1, source_target_pairs={{448,384},{384,448},{320,256},{256,320},{192,128},{128,192},{0,64}... | collective-permute-start | bytes 12296 | tf_op jit(solution)/shard_map/ppermute | solution.py:47
  44.5 4.3 %collective-permute-start.7 = (f32[8,128]{1,0:T(8,128)S(1)}, f32[8,128]{1,0:T(8,128)S(1)}, u32[]{:S(2)}, u32[]{:S(2)}) collective-permute-start(f32[8,128]{1,0:T(8,128)S(1)} %backward.3.w), channel_id=1, source_target_pairs={{448,384},{384,448},{320,256},{256,320},{192,128},{128,192},{0,64}... | collective-permute-start | bytes 12296 | tf_op jit(solution)/shard_map/ppermute | solution.py:47
  46.8 4.4 %collective-permute-start.6 = (f32[8,128]{1,0:T(8,128)S(1)}, f32[8,128]{1,0:T(8,128)S(1)}, u32[]{:S(2)}, u32[]{:S(2)}) collective-permute-start(f32[8,128]{1,0:T(8,128)S(1)} %backward.3.w), channel_id=1, source_target_pairs={{384,320},{320,384},{256,192},{192,256},{128,0},{0,128},{64,65},{6... | collective-permute-start | bytes 12296 | tf_op jit(solution)/shard_map/ppermute | solution.py:46

commit v6 on v5

--- a/solution.py
+++ b/solution.py
@@ -123,7 +123,7 @@
     forward(columns, lambda x: columns[x, R : R + 1, :], half)
 
 
-def image_kernel(columns, local, far, near, cy, image, half):
+def image_kernel(columns, local, near, far, cy, image, half):
     image[...] = local[...] - cy[...] * (far[...] + near[...])
     value = image[...]
     forward(columns, lambda x: value[x : x + 1], half)
@@ -141,7 +141,7 @@
         out[x : x + 1, :] = previous
 
 
-def sums_kernel(r, z, q, w, local, far, near, cy, p, share):
+def sums_kernel(r, z, q, w, local, near, far, cy, p, share):
     z_a, q_a, w_a = z[...], q[...], w[...]
     p_a = local[...] - cy[...] * (far[...] + near[...])
     p[...] = p_a
@@ -219,12 +219,12 @@
     far, near = neighbours(half)
     z = local(backward_kernel, field, "backward")(columns, before(r, half), near, far, cy, half)
     far, near = neighbours(z)
-    q, half = local(image_kernel, (field, field), "image")(columns, image_part(z), far, near, cy)
+    q, half = local(image_kernel, (field, field), "image")(columns, image_part(z), near, far, cy)
     far, near = neighbours(half)
     w = local(backward_kernel, field, "backward")(columns, before(q, half), near, far, cy, half)
     far, near = neighbours(w)
     sums = (field, on_chip(NP, 1, B))
-    p, share = local(sums_kernel, sums, "sums")(r, z, q, w, image_part(w), far, near, cy)
+    p, share = local(sums_kernel, sums, "sums")(r, z, q, w, image_part(w), near, far, cy)
     everyone = lax.all_to_all(share, PLANE, split_axis=0, concat_axis=0, tiled=True)
     back = local(carry_kernel, on_chip(NW, 8, B), "carry")(everyone, z, q, w, p)
     back = lax.all_to_all(back, WAVE, split_axis=0, concat_axis=0, tiled=True)

time: 90.4 us -> 88 us (0.973)
  waiting for transfers between devices: 5.54 us -> 2.78 us
    ppermute x4, waiting for transfers between devices: 4.2 us -> 0.01 us  [neighbours(): far = lax.ppermute(values, ALL, FAR)]
    ppermute x4, waiting for transfers between devices: 1.34 us -> 2.77 us  [neighbours(): near = lax.ppermute(values, ALL, NEAR)]
where the time goes in v6:
time: 88 us; the launch traced here: 87.5 us
  blocking collectives  56.9 us (65%)
  starting transfers between devices  20.9 us (24%)
  Pallas kernels  5.44 us (6%)
  waiting for transfers between devices  2.78 us (3%)
    all_to_all x1, blocking collectives, on_device(): lax.all_to_all(share, PLANE, split_axis=0, concat_axis=0, tiled=True)  27.9 us
    all_to_all x1, blocking collectives, on_device(): lax.all_to_all(packed, WAVE, split_axis=0, concat_axis=0, tiled=True)  19.4 us
    ppermute x4, starting transfers between devices, neighbours(): near = lax.ppermute(values, ALL, NEAR)  11.7 us
    all_to_all x1, blocking collectives, on_device(): back = lax.all_to_all(back, WAVE, split_axis=0, concat_axis=0, tiled=True)  9.57 us
    ppermute x4, starting transfers between devices, neighbours(): far = lax.ppermute(values, ALL, FAR)  9.18 us
    pallas_call x7, Pallas kernels, call(): pl.pallas_call(kernel, out_shape=out, in_specs=[VMEM] * len(args), out_sp...  4.21 us
    ppermute x4, waiting for transfers between devices, neighbours(): near = lax.ppermute(values, ALL, NEAR)  2.77 us
  transfers between devices with their start and end apart: 8, of which 4 were waited for; matrix products, arithmetic and copies ran while one was open for 0% of the time, Pallas kernels for 0%

profile of v6, /device:TPU:1, one launch (start us, length us, event | category | flops | bytes accessed | tf_op | source)
XLA Modules:
  0.0 87.5 jit_solution(2112433000870731109)
XLA Ops:
  0.6 1.2 %pack.1 = (f32[8,136,128]{2,1,0:T(8,128)S(1)}, f32[8,128]{1,0:T(8,128)S(1)}) custom-call(f32[1,8,128,128]{3,2,1,0:T(8,128)} %inverse.1, f32[1,8,128]{2,1,0:T(8,128)} %right.1, f32[1,8,128]{2,1,0:T(8,128)} %cz.1, f32[8,128]{1,0:T(8,128)} %cx.1, f32[1,128]{1,0:T(1,128)} %cy.1), custom_call_target="tpu_custom_call" | custom-call | tf_op jit(solution)/shard_map/pack/pallas_call | solution.py:91
  1.9 19.4 %all_to_all.15.columns = f32[8,136,128]{2,1,0:T(8,128)S(1)} all-to-all(f32[8,136,128]{2,1,0:T(8,128)S(1)} %get-tuple-element.8), channel_id=1, replica_groups=mesh['wave_0'=4,'wave_1'=2,'plane_0'=4,'plane_1'=16] {'wave_0','wave_1'}, dimensions={0} | all-to-all | bytes 1114112 | tf_op jit(solution)/shard_map/all_to_all | solution.py:206
  21.3 0.8 first.1.half
  22.1 1.9 %collective-permute-start.1 = (f32[8,128]{1,0:T(8,128)S(1)}, f32[8,128]{1,0:T(8,128)S(1)}, u32[]{:S(2)}, u32[]{:S(2)}) collective-permute-start(f32[8,128]{1,0:T(8,128)S(1)} %first.1.half), channel_id=1, source_target_pairs={{384,320},{320,384},{256,192},{192,256},{128,0},{0,128},{64,65},{6... | collective-permute-start | bytes 12296 | tf_op jit(solution)/shard_map/ppermute | solution.py:46
  24.1 3.0 %collective-permute-start = (f32[8,128]{1,0:T(8,128)S(1)}, f32[8,128]{1,0:T(8,128)S(1)}, u32[]{:S(2)}, u32[]{:S(2)}) collective-permute-start(f32[8,128]{1,0:T(8,128)S(1)} %first.1.half), channel_id=1, source_target_pairs={{448,384},{384,448},{320,256},{256,320},{192,128},{128,192},{0,64}... | collective-permute-start | bytes 12296 | tf_op jit(solution)/shard_map/ppermute | solution.py:47
  27.2 0.1 multiply_add_fusion.1
  27.3 0.6 collective-permute-done.near
  27.9 0.8 backward.2.z
  28.8 2.6 %collective-permute-start.3 = (f32[8,128]{1,0:T(8,128)S(1)}, f32[8,128]{1,0:T(8,128)S(1)}, u32[]{:S(2)}, u32[]{:S(2)}) collective-permute-start(f32[8,128]{1,0:T(8,128)S(1)} %backward.2.z), channel_id=1, source_target_pairs={{384,320},{320,384},{256,192},{192,256},{128,0},{0,128},{64,65},{6... | collective-permute-start | bytes 12296 | tf_op jit(solution)/shard_map/ppermute | solution.py:46
  31.4 3.0 %collective-permute-start.2 = (f32[8,128]{1,0:T(8,128)S(1)}, f32[8,128]{1,0:T(8,128)S(1)}, u32[]{:S(2)}, u32[]{:S(2)}) collective-permute-start(f32[8,128]{1,0:T(8,128)S(1)} %backward.2.z), channel_id=1, source_target_pairs={{448,384},{384,448},{320,256},{256,320},{192,128},{128,192},{0,64}... | collective-permute-start | bytes 12296 | tf_op jit(solution)/shard_map/ppermute | solution.py:47
  34.5 0.7 collective-permute-done.2.near
  35.2 0.8 image.1
  36.1 1.9 %collective-permute-start.5 = (f32[8,128]{1,0:T(8,128)S(1)}, f32[8,128]{1,0:T(8,128)S(1)}, u32[]{:S(2)}, u32[]{:S(2)}) collective-permute-start(f32[8,128]{1,0:T(8,128)S(1)} %get-tuple-element.10.half), channel_id=1, source_target_pairs={{384,320},{320,384},{256,192},{192,256},{128,0},{0,128},{64,65},{6... | collective-permute-start | bytes 12296 | tf_op jit(solution)/shard_map/ppermute | solution.py:46
  38.0 2.8 %collective-permute-start.4 = (f32[8,128]{1,0:T(8,128)S(1)}, f32[8,128]{1,0:T(8,128)S(1)}, u32[]{:S(2)}, u32[]{:S(2)}) collective-permute-start(f32[8,128]{1,0:T(8,128)S(1)} %get-tuple-element.10.half), channel_id=1, source_target_pairs={{448,384},{384,448},{320,256},{256,320},{192,128},{128,192},{0,64}... | collective-permute-start | bytes 12296 | tf_op jit(solution)/shard_map/ppermute | solution.py:47
  40.8 0.1 multiply_add_fusion.base
  40.9 0.7 collective-permute-done.4.near
  41.6 0.8 backward.3.w
  42.5 2.8 %collective-permute-start.7 = (f32[8,128]{1,0:T(8,128)S(1)}, f32[8,128]{1,0:T(8,128)S(1)}, u32[]{:S(2)}, u32[]{:S(2)}) collective-permute-start(f32[8,128]{1,0:T(8,128)S(1)} %backward.3.w), channel_id=1, source_target_pairs={{384,320},{320,384},{256,192},{192,256},{128,0},{0,128},{64,65},{6... | collective-permute-start | bytes 12296 | tf_op jit(solution)/shard_map/ppermute | solution.py:46
  45.3 2.8 %collective-permute-start.6 = (f32[8,128]{1,0:T(8,128)S(1)}, f32[8,128]{1,0:T(8,128)S(1)}, u32[]{:S(2)}, u32[]{:S(2)}) collective-permute-start(f32[8,128]{1,0:T(8,128)S(1)} %backward.3.w), channel_id=1, source_target_pairs={{448,384},{384,448},{320,256},{256,320},{192,128},{128,192},{0,64}... | collective-permute-start | bytes 12296 | tf_op jit(solution)/shard_map/ppermute | solution.py:47
  48.2 0.7 collective-permute-done.6.near
  48.9 0.1 sums.1
  49.0 27.9 %all_to_all.16.everyone = f32[64,1,128]{2,1,0:T(1,128)S(1)} all-to-all(f32[64,1,128]{2,1,0:T(1,128)S(1)} %get-tuple-element.11), channel_id=1, replica_groups=mesh['wave_0'=4,'wave_1'=2,'plane_0'=4,'plane_1'=16] {'plane_0','plane_1'}, dimensions={0} | all-to-all | bytes 65536 | tf_op jit(solution)/shard_map/all_to_all | solution.py:228
  77.0 9.6 %all_to_all.17.back = f32[8,8,128]{2,1,0:T(8,128)S(1)} all-to-all(f32[8,8,128]{2,1,0:T(8,128)S(1)} %carry.1), channel_id=1, replica_groups=mesh['wave_0'=4,'wave_1'=2,'plane_0'=4,'plane_1'=16] {'wave_0','wave_1'}, dimensions={0} | all-to-all | bytes 65536 | tf_op jit(solution)/shard_map/all_to_all | solution.py:230
  86.6 0.9 %final.1 = (f32[1,8,128]{2,1,0:T(8,128)}, f32[1,8,128]{2,1,0:T(8,128)}) custom-call(f32[8,8,128]{2,1,0:T(8,128)S(1)} %all_to_all.17.back, f32[8,128]{1,0:T(8,128)S(1)} %get-tuple-element.13.r), custom_call_target="tpu_custom_call" | custom-call | tf_op jit(solution)/shard_map/final/pallas_call | solution.py:183
  (15 shorter events, 0.6 us)
Async XLA Ops:
  22.1 5.1 %collective-permute-start.1 = (f32[8,128]{1,0:T(8,128)S(1)}, f32[8,128]{1,0:T(8,128)S(1)}, u32[]{:S(2)}, u32[]{:S(2)}) collective-permute-start(f32[8,128]{1,0:T(8,128)S(1)} %first.1.half), channel_id=1, source_target_pairs={{384,320},{320,384},{256,192},{192,256},{128,0},{0,128},{64,65},{6... | collective-permute-start | bytes 12296 | tf_op jit(solution)/shard_map/ppermute | solution.py:46
  24.1 3.8 %collective-permute-start = (f32[8,128]{1,0:T(8,128)S(1)}, f32[8,128]{1,0:T(8,128)S(1)}, u32[]{:S(2)}, u32[]{:S(2)}) collective-permute-start(f32[8,128]{1,0:T(8,128)S(1)} %first.1.half), channel_id=1, source_target_pairs={{448,384},{384,448},{320,256},{256,320},{192,128},{128,192},{0,64}... | collective-permute-start | bytes 12296 | tf_op jit(solution)/shard_map/ppermute | solution.py:47
  28.8 5.7 %collective-permute-start.3 = (f32[8,128]{1,0:T(8,128)S(1)}, f32[8,128]{1,0:T(8,128)S(1)}, u32[]{:S(2)}, u32[]{:S(2)}) collective-permute-start(f32[8,128]{1,0:T(8,128)S(1)} %backward.2.z), channel_id=1, source_target_pairs={{384,320},{320,384},{256,192},{192,256},{128,0},{0,128},{64,65},{6... | collective-permute-start | bytes 12296 | tf_op jit(solution)/shard_map/ppermute | solution.py:46
  31.4 3.8 %collective-permute-start.2 = (f32[8,128]{1,0:T(8,128)S(1)}, f32[8,128]{1,0:T(8,128)S(1)}, u32[]{:S(2)}, u32[]{:S(2)}) collective-permute-start(f32[8,128]{1,0:T(8,128)S(1)} %backward.2.z), channel_id=1, source_target_pairs={{448,384},{384,448},{320,256},{256,320},{192,128},{128,192},{0,64}... | collective-permute-start | bytes 12296 | tf_op jit(solution)/shard_map/ppermute | solution.py:47
  36.1 4.8 %collective-permute-start.5 = (f32[8,128]{1,0:T(8,128)S(1)}, f32[8,128]{1,0:T(8,128)S(1)}, u32[]{:S(2)}, u32[]{:S(2)}) collective-permute-start(f32[8,128]{1,0:T(8,128)S(1)} %get-tuple-element.10.half), channel_id=1, source_target_pairs={{384,320},{320,384},{256,192},{192,256},{128,0},{0,128},{64,65},{6... | collective-permute-start | bytes 12296 | tf_op jit(solution)/shard_map/ppermute | solution.py:46
  38.0 3.6 %collective-permute-start.4 = (f32[8,128]{1,0:T(8,128)S(1)}, f32[8,128]{1,0:T(8,128)S(1)}, u32[]{:S(2)}, u32[]{:S(2)}) collective-permute-start(f32[8,128]{1,0:T(8,128)S(1)} %get-tuple-element.10.half), channel_id=1, source_target_pairs={{448,384},{384,448},{320,256},{256,320},{192,128},{128,192},{0,64}... | collective-permute-start | bytes 12296 | tf_op jit(solution)/shard_map/ppermute | solution.py:47
  42.5 5.7 %collective-permute-start.7 = (f32[8,128]{1,0:T(8,128)S(1)}, f32[8,128]{1,0:T(8,128)S(1)}, u32[]{:S(2)}, u32[]{:S(2)}) collective-permute-start(f32[8,128]{1,0:T(8,128)S(1)} %backward.3.w), channel_id=1, source_target_pairs={{384,320},{320,384},{256,192},{192,256},{128,0},{0,128},{64,65},{6... | collective-permute-start | bytes 12296 | tf_op jit(solution)/shard_map/ppermute | solution.py:46
  45.3 3.6 %collective-permute-start.6 = (f32[8,128]{1,0:T(8,128)S(1)}, f32[8,128]{1,0:T(8,128)S(1)}, u32[]{:S(2)}, u32[]{:S(2)}) collective-permute-start(f32[8,128]{1,0:T(8,128)S(1)} %backward.3.w), channel_id=1, source_target_pairs={{448,384},{384,448},{320,256},{256,320},{192,128},{128,192},{0,64}... | collective-permute-start | bytes 12296 | tf_op jit(solution)/shard_map/ppermute | solution.py:47

commit v7 on v4

--- a/solution.py
+++ b/solution.py
@@ -39,6 +39,7 @@
 
 
 NEAR = swap_pairs(0)
+GROUPS = [[w * NP + (p + 40) % NP for p in range(NP)] for w in range(NW)]
 FAR = swap_pairs(1)
 
 
@@ -225,7 +226,9 @@
     back = local(sums_kernel, on_chip(NW, 8, B), "sums")(r, z, q, w, image_part(w), far, near, cy)
     back = lax.all_to_all(back, WAVE, split_axis=0, concat_axis=0, tiled=True)
     share = local(share_kernel, on_chip(NP, 1, B), "share")(back)
-    everyone = lax.all_to_all(share, PLANE, split_axis=0, concat_axis=0, tiled=True)
+    everyone = lax.all_to_all(
+        share, ALL, split_axis=0, concat_axis=0, tiled=True, axis_index_groups=GROUPS
+    )
     out = f32(1, NW, B)
     return local(final_kernel, (out, out), "final")(everyone, back, own)
 

time: 86.6 us -> 81.6 us (0.942)
  blocking collectives: 55.5 us -> 50.2 us
    all_to_all x1, blocking collectives: 28.1 us -> 22.8 us  [on_device(): lax.all_to_all(share, ALL, split_axis=0, concat_axis=0, tiled=True, axis_...]
  transfers between devices with their start and end apart: 8 -> 8, of which waited for: 4 -> 4; matrix products, arithmetic and copies ran while one was open for 0% -> 1% of each run, Pallas kernels for 0% -> 0%
where the time goes in v7:
time: 81.6 us; the launch traced here: 80.8 us
  blocking collectives  50.2 us (62%)
  starting transfers between devices  20.9 us (26%)
  Pallas kernels  5.44 us (7%)
  waiting for transfers between devices  2.78 us (3%)
    all_to_all x1, blocking collectives, on_device(): lax.all_to_all(share, ALL, split_axis=0, concat_axis=0, tiled=True, axis_...  22.8 us
    all_to_all x1, blocking collectives, on_device(): lax.all_to_all(packed, WAVE, split_axis=0, concat_axis=0, tiled=True)  19.4 us
    ppermute x4, starting transfers between devices, neighbours(): near = lax.ppermute(values, ALL, NEAR)  11.7 us
    ppermute x4, starting transfers between devices, neighbours(): far = lax.ppermute(values, ALL, FAR)  9.18 us
    all_to_all x1, blocking collectives, on_device(): back = lax.all_to_all(back, WAVE, split_axis=0, concat_axis=0, tiled=True)  7.96 us
    pallas_call x7, Pallas kernels, call(): pl.pallas_call(kernel, out_shape=out, in_specs=[VMEM] * len(args), out_sp...  4.21 us
    ppermute x4, waiting for transfers between devices, neighbours(): near = lax.ppermute(values, ALL, NEAR)  2.77 us
  transfers between devices with their start and end apart: 8, of which 4 were waited for; matrix products, arithmetic and copies ran while one was open for 1% of the time, Pallas kernels for 0%

profile of v7, /device:TPU:1, one launch (start us, length us, event | category | flops | bytes accessed | tf_op | source)
XLA Modules:
  0.0 80.8 jit_solution(3786333267143274589)
XLA Ops:
  0.6 1.2 %pack.1 = (f32[8,136,128]{2,1,0:T(8,128)S(1)}, f32[8,128]{1,0:T(8,128)S(1)}) custom-call(f32[1,8,128,128]{3,2,1,0:T(8,128)} %inverse.1, f32[1,8,128]{2,1,0:T(8,128)} %right.1, f32[1,8,128]{2,1,0:T(8,128)} %cz.1, f32[8,128]{1,0:T(8,128)} %cx.1, f32[1,128]{1,0:T(1,128)} %cy.1), custom_call_target="tpu_custom_call" | custom-call | tf_op jit(solution)/shard_map/pack/pallas_call | solution.py:92
  1.9 19.4 %all_to_all.15.columns = f32[8,136,128]{2,1,0:T(8,128)S(1)} all-to-all(f32[8,136,128]{2,1,0:T(8,128)S(1)} %get-tuple-element.6), channel_id=1, replica_groups=mesh['wave_0'=4,'wave_1'=2,'plane_0'=4,'plane_1'=16] {'wave_0','wave_1'}, dimensions={0} | all-to-all | bytes 1114112 | tf_op jit(solution)/shard_map/all_to_all | solution.py:206
  21.3 0.8 first.1.half
  22.1 1.9 %collective-permute-start.1 = (f32[8,128]{1,0:T(8,128)S(1)}, f32[8,128]{1,0:T(8,128)S(1)}, u32[]{:S(2)}, u32[]{:S(2)}) collective-permute-start(f32[8,128]{1,0:T(8,128)S(1)} %first.1.half), channel_id=1, source_target_pairs={{384,320},{320,384},{256,192},{192,256},{128,0},{0,128},{64,65},{6... | collective-permute-start | bytes 12296 | tf_op jit(solution)/shard_map/ppermute | solution.py:47
  24.1 3.0 %collective-permute-start = (f32[8,128]{1,0:T(8,128)S(1)}, f32[8,128]{1,0:T(8,128)S(1)}, u32[]{:S(2)}, u32[]{:S(2)}) collective-permute-start(f32[8,128]{1,0:T(8,128)S(1)} %first.1.half), channel_id=1, source_target_pairs={{448,384},{384,448},{320,256},{256,320},{192,128},{128,192},{0,64}... | collective-permute-start | bytes 12296 | tf_op jit(solution)/shard_map/ppermute | solution.py:48
  27.2 0.1 multiply_add_fusion.1
  27.3 0.6 collective-permute-done.near
  27.9 0.8 backward.2.z
  28.8 2.6 %collective-permute-start.2 = (f32[8,128]{1,0:T(8,128)S(1)}, f32[8,128]{1,0:T(8,128)S(1)}, u32[]{:S(2)}, u32[]{:S(2)}) collective-permute-start(f32[8,128]{1,0:T(8,128)S(1)} %backward.2.z), channel_id=1, source_target_pairs={{384,320},{320,384},{256,192},{192,256},{128,0},{0,128},{64,65},{6... | collective-permute-start | bytes 12296 | tf_op jit(solution)/shard_map/ppermute | solution.py:47
  31.4 3.0 %collective-permute-start.3 = (f32[8,128]{1,0:T(8,128)S(1)}, f32[8,128]{1,0:T(8,128)S(1)}, u32[]{:S(2)}, u32[]{:S(2)}) collective-permute-start(f32[8,128]{1,0:T(8,128)S(1)} %backward.2.z), channel_id=1, source_target_pairs={{448,384},{384,448},{320,256},{256,320},{192,128},{128,192},{0,64}... | collective-permute-start | bytes 12296 | tf_op jit(solution)/shard_map/ppermute | solution.py:48
  34.5 0.7 collective-permute-done.3.near
  35.2 0.8 image.1
  36.1 1.9 %collective-permute-start.5 = (f32[8,128]{1,0:T(8,128)S(1)}, f32[8,128]{1,0:T(8,128)S(1)}, u32[]{:S(2)}, u32[]{:S(2)}) collective-permute-start(f32[8,128]{1,0:T(8,128)S(1)} %get-tuple-element.8.half), channel_id=1, source_target_pairs={{384,320},{320,384},{256,192},{192,256},{128,0},{0,128},{64,65},{6... | collective-permute-start | bytes 12296 | tf_op jit(solution)/shard_map/ppermute | solution.py:47
  38.0 2.8 %collective-permute-start.4 = (f32[8,128]{1,0:T(8,128)S(1)}, f32[8,128]{1,0:T(8,128)S(1)}, u32[]{:S(2)}, u32[]{:S(2)}) collective-permute-start(f32[8,128]{1,0:T(8,128)S(1)} %get-tuple-element.8.half), channel_id=1, source_target_pairs={{448,384},{384,448},{320,256},{256,320},{192,128},{128,192},{0,64}... | collective-permute-start | bytes 12296 | tf_op jit(solution)/shard_map/ppermute | solution.py:48
  40.8 0.1 multiply_add_fusion.base
  40.9 0.7 collective-permute-done.4.near
  41.6 0.8 backward.3.w
  42.5 2.8 %collective-permute-start.6 = (f32[8,128]{1,0:T(8,128)S(1)}, f32[8,128]{1,0:T(8,128)S(1)}, u32[]{:S(2)}, u32[]{:S(2)}) collective-permute-start(f32[8,128]{1,0:T(8,128)S(1)} %backward.3.w), channel_id=1, source_target_pairs={{384,320},{320,384},{256,192},{192,256},{128,0},{0,128},{64,65},{6... | collective-permute-start | bytes 12296 | tf_op jit(solution)/shard_map/ppermute | solution.py:47
  45.3 2.8 %collective-permute-start.7 = (f32[8,128]{1,0:T(8,128)S(1)}, f32[8,128]{1,0:T(8,128)S(1)}, u32[]{:S(2)}, u32[]{:S(2)}) collective-permute-start(f32[8,128]{1,0:T(8,128)S(1)} %backward.3.w), channel_id=1, source_target_pairs={{448,384},{384,448},{320,256},{256,320},{192,128},{128,192},{0,64}... | collective-permute-start | bytes 12296 | tf_op jit(solution)/shard_map/ppermute | solution.py:48
  48.2 0.7 collective-permute-done.7.near
  48.9 0.1 sums.1
  49.0 8.0 %all_to_all.16.back = f32[8,8,128]{2,1,0:T(8,128)S(1)} all-to-all(f32[8,8,128]{2,1,0:T(8,128)S(1)} %sums.1), channel_id=1, replica_groups=mesh['wave_0'=4,'wave_1'=2,'plane_0'=4,'plane_1'=16] {'wave_0','wave_1'}, dimensions={0} | all-to-all | bytes 65536 | tf_op jit(solution)/shard_map/all_to_all | solution.py:227
  57.0 22.8 %all_to_all.17.everyone = f32[64,1,128]{2,1,0:T(1,128)S(1)} all-to-all(f32[64,1,128]{2,1,0:T(1,128)S(1)} %share.1), channel_id=1, replica_groups={{40,41,42,43,44,45,46,47,48,49,50,51,52,53,54,55,56,57,58,59,60,61,62,6..., dimensions={0} | all-to-all | bytes 65536 | tf_op jit(solution)/shard_map/all_to_all | solution.py:229
  79.8 1.0 %final.1 = (f32[1,8,128]{2,1,0:T(8,128)}, f32[1,8,128]{2,1,0:T(8,128)}) custom-call(f32[64,1,128]{2,1,0:T(1,128)S(1)} %all_to_all.17.everyone, f32[8,8,128]{2,1,0:T(8,128)S(1)} %all_to_all.16.back, f32[8,128]{1,0:T(8,128)S(1)} %get-tuple-element.9.r), custom_call_target="tpu_custom_call" | custom-call | tf_op jit(solution)/shard_map/final/pallas_call | solution.py:183
  (15 shorter events, 0.6 us)
Async XLA Ops:
  22.1 5.1 %collective-permute-start.1 = (f32[8,128]{1,0:T(8,128)S(1)}, f32[8,128]{1,0:T(8,128)S(1)}, u32[]{:S(2)}, u32[]{:S(2)}) collective-permute-start(f32[8,128]{1,0:T(8,128)S(1)} %first.1.half), channel_id=1, source_target_pairs={{384,320},{320,384},{256,192},{192,256},{128,0},{0,128},{64,65},{6... | collective-permute-start | bytes 12296 | tf_op jit(solution)/shard_map/ppermute | solution.py:47
  24.1 3.8 %collective-permute-start = (f32[8,128]{1,0:T(8,128)S(1)}, f32[8,128]{1,0:T(8,128)S(1)}, u32[]{:S(2)}, u32[]{:S(2)}) collective-permute-start(f32[8,128]{1,0:T(8,128)S(1)} %first.1.half), channel_id=1, source_target_pairs={{448,384},{384,448},{320,256},{256,320},{192,128},{128,192},{0,64}... | collective-permute-start | bytes 12296 | tf_op jit(solution)/shard_map/ppermute | solution.py:48
  28.8 5.7 %collective-permute-start.2 = (f32[8,128]{1,0:T(8,128)S(1)}, f32[8,128]{1,0:T(8,128)S(1)}, u32[]{:S(2)}, u32[]{:S(2)}) collective-permute-start(f32[8,128]{1,0:T(8,128)S(1)} %backward.2.z), channel_id=1, source_target_pairs={{384,320},{320,384},{256,192},{192,256},{128,0},{0,128},{64,65},{6... | collective-permute-start | bytes 12296 | tf_op jit(solution)/shard_map/ppermute | solution.py:47
  31.4 3.8 %collective-permute-start.3 = (f32[8,128]{1,0:T(8,128)S(1)}, f32[8,128]{1,0:T(8,128)S(1)}, u32[]{:S(2)}, u32[]{:S(2)}) collective-permute-start(f32[8,128]{1,0:T(8,128)S(1)} %backward.2.z), channel_id=1, source_target_pairs={{448,384},{384,448},{320,256},{256,320},{192,128},{128,192},{0,64}... | collective-permute-start | bytes 12296 | tf_op jit(solution)/shard_map/ppermute | solution.py:48
  36.1 4.8 %collective-permute-start.5 = (f32[8,128]{1,0:T(8,128)S(1)}, f32[8,128]{1,0:T(8,128)S(1)}, u32[]{:S(2)}, u32[]{:S(2)}) collective-permute-start(f32[8,128]{1,0:T(8,128)S(1)} %get-tuple-element.8.half), channel_id=1, source_target_pairs={{384,320},{320,384},{256,192},{192,256},{128,0},{0,128},{64,65},{6... | collective-permute-start | bytes 12296 | tf_op jit(solution)/shard_map/ppermute | solution.py:47
  38.0 3.6 %collective-permute-start.4 = (f32[8,128]{1,0:T(8,128)S(1)}, f32[8,128]{1,0:T(8,128)S(1)}, u32[]{:S(2)}, u32[]{:S(2)}) collective-permute-start(f32[8,128]{1,0:T(8,128)S(1)} %get-tuple-element.8.half), channel_id=1, source_target_pairs={{448,384},{384,448},{320,256},{256,320},{192,128},{128,192},{0,64}... | collective-permute-start | bytes 12296 | tf_op jit(solution)/shard_map/ppermute | solution.py:48
  42.5 5.7 %collective-permute-start.6 = (f32[8,128]{1,0:T(8,128)S(1)}, f32[8,128]{1,0:T(8,128)S(1)}, u32[]{:S(2)}, u32[]{:S(2)}) collective-permute-start(f32[8,128]{1,0:T(8,128)S(1)} %backward.3.w), channel_id=1, source_target_pairs={{384,320},{320,384},{256,192},{192,256},{128,0},{0,128},{64,65},{6... | collective-permute-start | bytes 12296 | tf_op jit(solution)/shard_map/ppermute | solution.py:47
  45.3 3.6 %collective-permute-start.7 = (f32[8,128]{1,0:T(8,128)S(1)}, f32[8,128]{1,0:T(8,128)S(1)}, u32[]{:S(2)}, u32[]{:S(2)}) collective-permute-start(f32[8,128]{1,0:T(8,128)S(1)} %backward.3.w), channel_id=1, source_target_pairs={{448,384},{384,448},{320,256},{256,320},{192,128},{128,192},{0,64}... | collective-permute-start | bytes 12296 | tf_op jit(solution)/shard_map/ppermute | solution.py:48

commit v8 on v4

--- a/solution.py
+++ b/solution.py
@@ -39,6 +39,17 @@
 
 
 NEAR = swap_pairs(0)
+PLANE_GROUPS = [[w * NP + (p + 40) % NP for p in range(NP)] for w in range(NW)]
+LEAD_IN = 5
+LEAD_OUT = 5
+
+
+def wave_groups(lead):
+    return [[(w + lead) % NW * NP + p for w in range(NW)] for p in range(NP)]
+
+
+def place(wave, lead):
+    return (wave - lead) % NW
 FAR = swap_pairs(1)
 
 
@@ -48,6 +59,12 @@
     return far, near
 
 
+def exchanged(values, groups):
+    return lax.all_to_all(
+        values, ALL, split_axis=0, concat_axis=0, tiled=True, axis_index_groups=groups
+    )
+
+
 def f32(*shape):
     return jax.ShapeDtypeStruct(shape, jnp.float32)
 
@@ -56,9 +73,10 @@
     return pltpu.VMEM(shape, jnp.float32)
 
 
-def turned(j):
+def turned(j, lead):
     parity = lax.axis_index("plane_1") % 2
-    return EVEN[j] + parity * (ODD[j] - EVEN[j])
+    even, odd = place(EVEN[j], lead), place(ODD[j], lead)
+    return even + parity * (odd - even)
 
 
 def pack_kernel(inverse, right, cz, cx, cy, packed, r_out, cz_v, cx_v, cy_v, sems, small):
@@ -71,7 +89,7 @@
     for copy in copies:
         copy.start()
     blocks = [
-        pltpu.make_async_copy(inverse.at[0, j], packed.at[turned(j), 0:B, :], sems.at[j])
+        pltpu.make_async_copy(inverse.at[0, j], packed.at[turned(j, LEAD_IN), 0:B, :], sems.at[j])
         for j in range(NW)
     ]
     for copy in blocks:
@@ -82,7 +100,7 @@
     for j in range(NW):
         rows = [r_v[j : j + 1], cz_a[j : j + 1], cx_a[j : j + 1], cy_a]
         rows.append(jnp.zeros((ROWS - B - 4, B), jnp.float32))
-        packed[turned(j), B:ROWS, :] = jnp.concatenate(rows, axis=0)
+        packed[turned(j, LEAD_IN), B:ROWS, :] = jnp.concatenate(rows, axis=0)
     for copy in blocks:
         copy.wait()
 
@@ -105,7 +123,8 @@
 
 
 def times_block(columns, x, vector):
-    return jnp.sum(columns[x, 0:B, :] * vector, axis=1).reshape(1, B)
+    block = columns[place(x, LEAD_IN), 0:B, :]
+    return jnp.sum(block * vector, axis=1).reshape(1, B)
 
 
 def forward(columns, source, out):
@@ -120,7 +139,7 @@
 
 
 def first_kernel(columns, half):
-    forward(columns, lambda x: columns[x, R : R + 1, :], half)
+    forward(columns, lambda x: columns[place(x, LEAD_IN), R : R + 1, :], half)
 
 
 def image_kernel(columns, local, far, near, cy, image, half):
@@ -152,7 +171,7 @@
     rest = jnp.zeros((3, B), jnp.float32)
     for x in range(NW):
         at = slice(x, x + 1)
-        back[x] = jnp.concatenate([z_a[at], q_a[at], w_a[at], p_a[at], row, rest], axis=0)
+        back[place(x, LEAD_OUT)] = jnp.concatenate([z_a[at], q_a[at], w_a[at], p_a[at], row, rest], axis=0)
 
 
 def share_kernel(back, out):
@@ -170,7 +189,7 @@
     second = (first * wq - wr) / (wp - ratio * wq)
     lead = first + second * ratio
     for j in range(NW):
-        field = back[turned(j)]
+        field = back[turned(j, LEAD_OUT)]
         solution_out[0, j : j + 1, :] = lead * field[0:1] - second * field[2:3]
         residual_out[0, j : j + 1, :] = r[j : j + 1] - lead * field[1:2] + second * field[3:4]
 
@@ -202,8 +221,8 @@
 
 def on_device(right_side, coupling_x, coupling_y, coupling_z, inverse):
     packed, own = pack(inverse, right_side, coupling_z, coupling_x, coupling_y)
-    columns = lax.all_to_all(packed, WAVE, split_axis=0, concat_axis=0, tiled=True)
-    r, cz, cx, cy = (columns[:, i] for i in (R, CZ, CX, CY))
+    columns = exchanged(packed, wave_groups(LEAD_IN))
+    r, cz, cx, cy = (jnp.roll(columns[:, i], LEAD_IN, axis=0) for i in (R, CZ, CX, CY))
     upper_z = jnp.concatenate([cz[:, 1:], cz[:, :1]], axis=-1)
     centre = 2.0 * cx + 2.0 * cy + cz + upper_z
 
@@ -223,9 +242,9 @@
     w = local(backward_kernel, field, "backward")(columns, before(q, half), near, far, cy, half)
     far, near = neighbours(w)
     back = local(sums_kernel, on_chip(NW, 8, B), "sums")(r, z, q, w, image_part(w), far, near, cy)
-    back = lax.all_to_all(back, WAVE, split_axis=0, concat_axis=0, tiled=True)
+    back = exchanged(back, wave_groups(LEAD_OUT))
     share = local(share_kernel, on_chip(NP, 1, B), "share")(back)
-    everyone = lax.all_to_all(share, PLANE, split_axis=0, concat_axis=0, tiled=True)
+    everyone = exchanged(share, PLANE_GROUPS)
     out = f32(1, NW, B)
     return local(final_kernel, (out, out), "final")(everyone, back, own)
 

time: 86.6 us -> 79.3 us (0.916)
  blocking collectives: 55.5 us -> 46.8 us
  starting transfers between devices: 20.9 us -> 21.9 us
    all_to_all x3, blocking collectives: 55.5 us -> 46.8 us  [exchanged(): lax.all_to_all(values, ALL, split_axis=0, concat_axis=0, tiled=True, axis...]
    ppermute x4, starting transfers between devices: 11.7 us -> 13.4 us  [neighbours(): near = lax.ppermute(values, ALL, NEAR)]
  transfers between devices with their start and end apart: 8 -> 8, of which waited for: 4 -> 4; matrix products, arithmetic and copies ran while one was open for 0% -> 1% of each run, Pallas kernels for 0% -> 0%
where the time goes in v8:
time: 79.3 us; the launch traced here: 78.3 us
  blocking collectives  46.8 us (59%)
  starting transfers between devices  21.9 us (28%)
  Pallas kernels  5.44 us (7%)
  waiting for transfers between devices  2.73 us (3%)
  between operations  0.8 us (1%)
    all_to_all x3, blocking collectives, exchanged(): lax.all_to_all(values, ALL, split_axis=0, concat_axis=0, tiled=True, axis...  46.8 us
    ppermute x4, starting transfers between devices, neighbours(): near = lax.ppermute(values, ALL, NEAR)  13.4 us
    ppermute x4, starting transfers between devices, neighbours(): far = lax.ppermute(values, ALL, FAR)  8.52 us
    pallas_call x7, Pallas kernels, call(): pl.pallas_call(kernel, out_shape=out, in_specs=[VMEM] * len(args), out_sp...  4.21 us
    ppermute x4, waiting for transfers between devices, neighbours(): near = lax.ppermute(values, ALL, NEAR)  2.72 us
  transfers between devices with their start and end apart: 8, of which 4 were waited for; matrix products, arithmetic and copies ran while one was open for 1% of the time, Pallas kernels for 0%

profile of v8, /device:TPU:1, one launch (start us, length us, event | category | flops | bytes accessed | tf_op | source)
XLA Modules:
  0.0 78.3 jit_solution(9665487492071589673)
XLA Ops:
  0.6 1.2 %pack.1 = (f32[8,136,128]{2,1,0:T(8,128)S(1)}, f32[8,128]{1,0:T(8,128)S(1)}) custom-call(f32[1,8,128,128]{3,2,1,0:T(8,128)} %inverse.1, f32[1,8,128]{2,1,0:T(8,128)} %right.1, f32[1,8,128]{2,1,0:T(8,128)} %cz.1, f32[8,128]{1,0:T(8,128)} %cx.1, f32[1,128]{1,0:T(1,128)} %cy.1), custom_call_target="tpu_custom_call" | custom-call | tf_op jit(solution)/shard_map/pack/pallas_call | solution.py:109
  1.9 18.1 %all_to_all.15.columns = f32[8,136,128]{2,1,0:T(8,128)S(1)} all-to-all(f32[8,136,128]{2,1,0:T(8,128)S(1)} %get-tuple-element.6), channel_id=1, replica_groups={{320,384,448,0,64,128,192,256},{321,385,449,1,65,129,193,257},{322,386,..., dimensions={0} | all-to-all | bytes 1114112 | tf_op jit(solution)/shard_map/all_to_all | solution.py:63
  19.9 0.8 first.1.half
  20.8 1.9 %collective-permute-start.1 = (f32[8,128]{1,0:T(8,128)S(1)}, f32[8,128]{1,0:T(8,128)S(1)}, u32[]{:S(2)}, u32[]{:S(2)}) collective-permute-start(f32[8,128]{1,0:T(8,128)S(1)} %first.1.half), channel_id=1, source_target_pairs={{384,320},{320,384},{256,192},{192,256},{128,0},{0,128},{64,65},{6... | collective-permute-start | bytes 12296 | tf_op jit(solution)/shard_map/ppermute | solution.py:57
  22.7 4.2 %collective-permute-start = (f32[8,128]{1,0:T(8,128)S(1)}, f32[8,128]{1,0:T(8,128)S(1)}, u32[]{:S(2)}, u32[]{:S(2)}) collective-permute-start(f32[8,128]{1,0:T(8,128)S(1)} %first.1.half), channel_id=1, source_target_pairs={{448,384},{384,448},{320,256},{256,320},{192,128},{128,192},{0,64}... | collective-permute-start | bytes 12296 | tf_op jit(solution)/shard_map/ppermute | solution.py:58
  27.1 0.6 collective-permute-done.near
  27.7 0.8 %backward.2.z = f32[8,128]{1,0:T(8,128)S(1)} custom-call(f32[8,136,128]{2,1,0:T(8,128)S(1)} %all_to_all.15.columns, f32[8,128]{1,0:T(8,128)S(1)} %get-tuple-element.10.base, f32[8,128]{1,0:T(8,128)S(1)} %collective-permute-done.near, f32[8,128]{1,0:T(8,128)S(1)} %collective-permute-done.1.far, f32[8,128]{1,0:T(8,128)S(1)} %get-tuple-element.11.cy, ...), custom_call_target="tpu_custom_call" | custom-call | tf_op jit(solution)/shard_map/backward/pallas_call | solution.py:201
  28.6 1.9 %collective-permute-start.2 = (f32[8,128]{1,0:T(8,128)S(1)}, f32[8,128]{1,0:T(8,128)S(1)}, u32[]{:S(2)}, u32[]{:S(2)}) collective-permute-start(f32[8,128]{1,0:T(8,128)S(1)} %backward.2.z), channel_id=1, source_target_pairs={{384,320},{320,384},{256,192},{192,256},{128,0},{0,128},{64,65},{6... | collective-permute-start | bytes 12296 | tf_op jit(solution)/shard_map/ppermute | solution.py:57
  30.5 3.6 %collective-permute-start.3 = (f32[8,128]{1,0:T(8,128)S(1)}, f32[8,128]{1,0:T(8,128)S(1)}, u32[]{:S(2)}, u32[]{:S(2)}) collective-permute-start(f32[8,128]{1,0:T(8,128)S(1)} %backward.2.z), channel_id=1, source_target_pairs={{448,384},{384,448},{320,256},{256,320},{192,128},{128,192},{0,64}... | collective-permute-start | bytes 12296 | tf_op jit(solution)/shard_map/ppermute | solution.py:58
  34.0 0.1 multiply_subtract_fusion.1.local
  34.1 0.7 collective-permute-done.3.near
  34.8 0.8 image.1
  35.7 2.0 %collective-permute-start.5 = (f32[8,128]{1,0:T(8,128)S(1)}, f32[8,128]{1,0:T(8,128)S(1)}, u32[]{:S(2)}, u32[]{:S(2)}) collective-permute-start(f32[8,128]{1,0:T(8,128)S(1)} %get-tuple-element.8.half), channel_id=1, source_target_pairs={{384,320},{320,384},{256,192},{192,256},{128,0},{0,128},{64,65},{6... | collective-permute-start | bytes 12296 | tf_op jit(solution)/shard_map/ppermute | solution.py:57
  37.8 2.8 %collective-permute-start.4 = (f32[8,128]{1,0:T(8,128)S(1)}, f32[8,128]{1,0:T(8,128)S(1)}, u32[]{:S(2)}, u32[]{:S(2)}) collective-permute-start(f32[8,128]{1,0:T(8,128)S(1)} %get-tuple-element.8.half), channel_id=1, source_target_pairs={{448,384},{384,448},{320,256},{256,320},{192,128},{128,192},{0,64}... | collective-permute-start | bytes 12296 | tf_op jit(solution)/shard_map/ppermute | solution.py:58
  40.6 0.1 multiply_add_fusion.base
  40.7 0.7 collective-permute-done.4.near
  41.4 0.8 %backward.3.w = f32[8,128]{1,0:T(8,128)S(1)} custom-call(f32[8,136,128]{2,1,0:T(8,128)S(1)} %all_to_all.15.columns, f32[8,128]{1,0:T(8,128)S(1)} %multiply_add_fusion.base, f32[8,128]{1,0:T(8,128)S(1)} %collective-permute-done.4.near, f32[8,128]{1,0:T(8,128)S(1)} %collective-permute-done.5.far, f32[8,128]{1,0:T(8,128)S(1)} %get-tuple-element.11.cy, ...), custom_call_target="tpu_custom_call" | custom-call | tf_op jit(solution)/shard_map/backward/pallas_call | solution.py:201
  42.3 2.7 %collective-permute-start.6 = (f32[8,128]{1,0:T(8,128)S(1)}, f32[8,128]{1,0:T(8,128)S(1)}, u32[]{:S(2)}, u32[]{:S(2)}) collective-permute-start(f32[8,128]{1,0:T(8,128)S(1)} %backward.3.w), channel_id=1, source_target_pairs={{384,320},{320,384},{256,192},{192,256},{128,0},{0,128},{64,65},{6... | collective-permute-start | bytes 12296 | tf_op jit(solution)/shard_map/ppermute | solution.py:57
  44.9 2.8 %collective-permute-start.7 = (f32[8,128]{1,0:T(8,128)S(1)}, f32[8,128]{1,0:T(8,128)S(1)}, u32[]{:S(2)}, u32[]{:S(2)}) collective-permute-start(f32[8,128]{1,0:T(8,128)S(1)} %backward.3.w), channel_id=1, source_target_pairs={{448,384},{384,448},{320,256},{256,320},{192,128},{128,192},{0,64}... | collective-permute-start | bytes 12296 | tf_op jit(solution)/shard_map/ppermute | solution.py:58
  47.8 0.7 collective-permute-done.7.near
  48.5 0.1 sums.1
  48.6 6.6 %all_to_all.16.back = f32[8,8,128]{2,1,0:T(8,128)S(1)} all-to-all(f32[8,8,128]{2,1,0:T(8,128)S(1)} %sums.1), channel_id=1, replica_groups={{320,384,448,0,64,128,192,256},{321,385,449,1,65,129,193,257},{322,386,..., dimensions={0} | all-to-all | bytes 65536 | tf_op jit(solution)/shard_map/all_to_all | solution.py:63
  55.2 22.1 %all_to_all.17.everyone = f32[64,1,128]{2,1,0:T(1,128)S(1)} all-to-all(f32[64,1,128]{2,1,0:T(1,128)S(1)} %share.1), channel_id=1, replica_groups={{40,41,42,43,44,45,46,47,48,49,50,51,52,53,54,55,56,57,58,59,60,61,62,6..., dimensions={0} | all-to-all | bytes 65536 | tf_op jit(solution)/shard_map/all_to_all | solution.py:63
  77.4 1.0 %final.1 = (f32[1,8,128]{2,1,0:T(8,128)}, f32[1,8,128]{2,1,0:T(8,128)}) custom-call(f32[64,1,128]{2,1,0:T(1,128)S(1)} %all_to_all.17.everyone, f32[8,8,128]{2,1,0:T(8,128)S(1)} %all_to_all.16.back, f32[8,128]{1,0:T(8,128)S(1)} %get-tuple-element.9.r), custom_call_target="tpu_custom_call" | custom-call | tf_op jit(solution)/shard_map/final/pallas_call | solution.py:201
  (21 shorter events, 0.6 us)
Async XLA Ops:
  20.8 6.3 %collective-permute-start.1 = (f32[8,128]{1,0:T(8,128)S(1)}, f32[8,128]{1,0:T(8,128)S(1)}, u32[]{:S(2)}, u32[]{:S(2)}) collective-permute-start(f32[8,128]{1,0:T(8,128)S(1)} %first.1.half), channel_id=1, source_target_pairs={{384,320},{320,384},{256,192},{192,256},{128,0},{0,128},{64,65},{6... | collective-permute-start | bytes 12296 | tf_op jit(solution)/shard_map/ppermute | solution.py:57
  22.7 5.0 %collective-permute-start = (f32[8,128]{1,0:T(8,128)S(1)}, f32[8,128]{1,0:T(8,128)S(1)}, u32[]{:S(2)}, u32[]{:S(2)}) collective-permute-start(f32[8,128]{1,0:T(8,128)S(1)} %first.1.half), channel_id=1, source_target_pairs={{448,384},{384,448},{320,256},{256,320},{192,128},{128,192},{0,64}... | collective-permute-start | bytes 12296 | tf_op jit(solution)/shard_map/ppermute | solution.py:58
  28.6 5.6 %collective-permute-start.2 = (f32[8,128]{1,0:T(8,128)S(1)}, f32[8,128]{1,0:T(8,128)S(1)}, u32[]{:S(2)}, u32[]{:S(2)}) collective-permute-start(f32[8,128]{1,0:T(8,128)S(1)} %backward.2.z), channel_id=1, source_target_pairs={{384,320},{320,384},{256,192},{192,256},{128,0},{0,128},{64,65},{6... | collective-permute-start | bytes 12296 | tf_op jit(solution)/shard_map/ppermute | solution.py:57
  30.5 4.4 %collective-permute-start.3 = (f32[8,128]{1,0:T(8,128)S(1)}, f32[8,128]{1,0:T(8,128)S(1)}, u32[]{:S(2)}, u32[]{:S(2)}) collective-permute-start(f32[8,128]{1,0:T(8,128)S(1)} %backward.2.z), channel_id=1, source_target_pairs={{448,384},{384,448},{320,256},{256,320},{192,128},{128,192},{0,64}... | collective-permute-start | bytes 12296 | tf_op jit(solution)/shard_map/ppermute | solution.py:58
  35.7 5.0 %collective-permute-start.5 = (f32[8,128]{1,0:T(8,128)S(1)}, f32[8,128]{1,0:T(8,128)S(1)}, u32[]{:S(2)}, u32[]{:S(2)}) collective-permute-start(f32[8,128]{1,0:T(8,128)S(1)} %get-tuple-element.8.half), channel_id=1, source_target_pairs={{384,320},{320,384},{256,192},{192,256},{128,0},{0,128},{64,65},{6... | collective-permute-start | bytes 12296 | tf_op jit(solution)/shard_map/ppermute | solution.py:57
  37.8 3.6 %collective-permute-start.4 = (f32[8,128]{1,0:T(8,128)S(1)}, f32[8,128]{1,0:T(8,128)S(1)}, u32[]{:S(2)}, u32[]{:S(2)}) collective-permute-start(f32[8,128]{1,0:T(8,128)S(1)} %get-tuple-element.8.half), channel_id=1, source_target_pairs={{448,384},{384,448},{320,256},{256,320},{192,128},{128,192},{0,64}... | collective-permute-start | bytes 12296 | tf_op jit(solution)/shard_map/ppermute | solution.py:58
  42.3 5.6 %collective-permute-start.6 = (f32[8,128]{1,0:T(8,128)S(1)}, f32[8,128]{1,0:T(8,128)S(1)}, u32[]{:S(2)}, u32[]{:S(2)}) collective-permute-start(f32[8,128]{1,0:T(8,128)S(1)} %backward.3.w), channel_id=1, source_target_pairs={{384,320},{320,384},{256,192},{192,256},{128,0},{0,128},{64,65},{6... | collective-permute-start | bytes 12296 | tf_op jit(solution)/shard_map/ppermute | solution.py:57
  44.9 3.6 %collective-permute-start.7 = (f32[8,128]{1,0:T(8,128)S(1)}, f32[8,128]{1,0:T(8,128)S(1)}, u32[]{:S(2)}, u32[]{:S(2)}) collective-permute-start(f32[8,128]{1,0:T(8,128)S(1)} %backward.3.w), channel_id=1, source_target_pairs={{448,384},{384,448},{320,256},{256,320},{192,128},{128,192},{0,64}... | collective-permute-start | bytes 12296 | tf_op jit(solution)/shard_map/ppermute | solution.py:58

commit v9 on v4

--- a/solution.py
+++ b/solution.py
@@ -39,6 +39,10 @@
 
 
 NEAR = swap_pairs(0)
+PLANE_GROUPS = [[w * NP + (p + 40) % NP for p in range(NP)] for w in range(NW)]
+ORDER = (5, 6, 7, 0, 1, 2, 3, 4)
+WAVE_GROUPS = [[w * NP + p for w in ORDER] for p in range(NP)]
+PLACE = tuple(ORDER.index(w) for w in range(NW))
 FAR = swap_pairs(1)
 
 
@@ -48,6 +52,12 @@
     return far, near
 
 
+def exchanged(values, groups):
+    return lax.all_to_all(
+        values, ALL, split_axis=0, concat_axis=0, tiled=True, axis_index_groups=groups
+    )
+
+
 def f32(*shape):
     return jax.ShapeDtypeStruct(shape, jnp.float32)
 
@@ -58,7 +68,8 @@
 
 def turned(j):
     parity = lax.axis_index("plane_1") % 2
-    return EVEN[j] + parity * (ODD[j] - EVEN[j])
+    even, odd = PLACE[EVEN[j]], PLACE[ODD[j]]
+    return even + parity * (odd - even)
 
 
 def pack_kernel(inverse, right, cz, cx, cy, packed, r_out, cz_v, cx_v, cy_v, sems, small):
@@ -105,7 +116,8 @@
 
 
 def times_block(columns, x, vector):
-    return jnp.sum(columns[x, 0:B, :] * vector, axis=1).reshape(1, B)
+    block = columns[PLACE[x], 0:B, :]
+    return jnp.sum(block * vector, axis=1).reshape(1, B)
 
 
 def forward(columns, source, out):
@@ -120,13 +132,55 @@
 
 
 def first_kernel(columns, half):
-    forward(columns, lambda x: columns[x, R : R + 1, :], half)
-
-
-def image_kernel(columns, local, far, near, cy, image, half):
+    forward(columns, lambda x: columns[PLACE[x], R : R + 1, :], half)
+
+
+def image_kernel(columns, local, near, far, cy, image, half):
     image[...] = local[...] - cy[...] * (far[...] + near[...])
     value = image[...]
     forward(columns, lambda x: value[x : x + 1], half)
+
+
+def column_part(values, centre, cz, upper_z):
+    lane = lax.broadcasted_iota(jnp.int32, values.shape, 1)
+    below = jnp.where(lane == 0, 0.0, pltpu.roll(values, 1, 1))
+    above = jnp.where(lane == B - 1, 0.0, pltpu.roll(values, B - 1, 1))
+    return centre * values - cz * below - upper_z * above
+
+
+def lower(values):
+    return jnp.concatenate([jnp.zeros((1, B), jnp.float32), values[:-1]], axis=0)
+
+
+def upper(values):
+    return jnp.concatenate([values[1:], jnp.zeros((1, B), jnp.float32)], axis=0)
+
+
+def source_part(source, half, cx, cz, upper_z, centre):
+    return source - column_part(half, centre, cz, upper_z) + cx * lower(half)
+
+
+def settle_first_kernel(columns, half, base, r, faces, cy):
+    rows = [
+        jnp.concatenate([columns[PLACE[x], i : i + 1, :] for x in range(NW)], axis=0)
+        for i in (R, CX, CZ, CY)
+    ]
+    upper_z = pltpu.roll(rows[2], B - 1, 1)
+    centre = 2.0 * rows[1] + 2.0 * rows[3] + rows[2] + upper_z
+    r[...] = rows[0]
+    cy[...] = rows[3]
+    for k, face in enumerate((rows[1], rows[2], upper_z, centre)):
+        faces[k] = face
+    base[...] = source_part(rows[0], half[...], rows[1], rows[2], upper_z, centre)
+
+
+def settle_kernel(source, half, faces, base):
+    base[...] = source_part(source[...], half[...], *(faces[k] for k in range(4)))
+
+
+def image_part_kernel(values, faces, out):
+    v = values[...]
+    out[...] = column_part(v, faces[3], faces[1], faces[2]) - faces[0] * (lower(v) + upper(v))
 
 
 def backward_kernel(columns, base, near, far, cy, half, out):
@@ -141,7 +195,7 @@
         out[x : x + 1, :] = previous
 
 
-def sums_kernel(r, z, q, w, local, far, near, cy, back):
+def sums_kernel(r, z, q, w, local, near, far, cy, back):
     z_a, q_a, w_a = z[...], q[...], w[...]
     p_a = local[...] - cy[...] * (far[...] + near[...])
     lane = lax.broadcasted_iota(jnp.int32, (1, B), 1)
@@ -152,7 +206,7 @@
     rest = jnp.zeros((3, B), jnp.float32)
     for x in range(NW):
         at = slice(x, x + 1)
-        back[x] = jnp.concatenate([z_a[at], q_a[at], w_a[at], p_a[at], row, rest], axis=0)
+        back[PLACE[x]] = jnp.concatenate([z_a[at], q_a[at], w_a[at], p_a[at], row, rest], axis=0)
 
 
 def share_kernel(back, out):
@@ -186,46 +240,29 @@
     return call
 
 
-def column_part(values, centre, cz, upper_z):
-    below = jnp.concatenate([jnp.zeros_like(values[:, :1]), values[:, :-1]], axis=-1)
-    above = jnp.concatenate([values[:, 1:], jnp.zeros_like(values[:, :1])], axis=-1)
-    return centre * values - cz * below - upper_z * above
-
-
-def lower(values):
-    return jnp.concatenate([jnp.zeros_like(values[:1]), values[:-1]], axis=0)
-
-
-def upper(values):
-    return jnp.concatenate([values[1:], jnp.zeros_like(values[:1])], axis=0)
-
-
 def on_device(right_side, coupling_x, coupling_y, coupling_z, inverse):
     packed, own = pack(inverse, right_side, coupling_z, coupling_x, coupling_y)
-    columns = lax.all_to_all(packed, WAVE, split_axis=0, concat_axis=0, tiled=True)
-    r, cz, cx, cy = (columns[:, i] for i in (R, CZ, CX, CY))
-    upper_z = jnp.concatenate([cz[:, 1:], cz[:, :1]], axis=-1)
-    centre = 2.0 * cx + 2.0 * cy + cz + upper_z
-
-    def before(source, half):
-        return source - column_part(half, centre, cz, upper_z) + cx * lower(half)
+    columns = exchanged(packed, WAVE_GROUPS)
+    field = on_chip(NW, B)
 
     def image_part(values):
-        return column_part(values, centre, cz, upper_z) - cx * (lower(values) + upper(values))
-
-    field = on_chip(NW, B)
+        return local(image_part_kernel, field, "image_part")(values, faces)
+
     half = local(first_kernel, field, "first")(columns)
     far, near = neighbours(half)
-    z = local(backward_kernel, field, "backward")(columns, before(r, half), near, far, cy, half)
+    parts = (field, field, on_chip(4, NW, B), field)
+    base, r, faces, cy = local(settle_first_kernel, parts, "settle_first")(columns, half)
+    z = local(backward_kernel, field, "backward")(columns, base, near, far, cy, half)
     far, near = neighbours(z)
-    q, half = local(image_kernel, (field, field), "image")(columns, image_part(z), far, near, cy)
+    q, half = local(image_kernel, (field, field), "image")(columns, image_part(z), near, far, cy)
     far, near = neighbours(half)
-    w = local(backward_kernel, field, "backward")(columns, before(q, half), near, far, cy, half)
+    base = local(settle_kernel, field, "settle")(q, half, faces)
+    w = local(backward_kernel, field, "backward")(columns, base, near, far, cy, half)
     far, near = neighbours(w)
-    back = local(sums_kernel, on_chip(NW, 8, B), "sums")(r, z, q, w, image_part(w), far, near, cy)
-    back = lax.all_to_all(back, WAVE, split_axis=0, concat_axis=0, tiled=True)
+    back = local(sums_kernel, on_chip(NW, 8, B), "sums")(r, z, q, w, image_part(w), near, far, cy)
+    back = exchanged(back, WAVE_GROUPS)
     share = local(share_kernel, on_chip(NP, 1, B), "share")(back)
-    everyone = lax.all_to_all(share, PLANE, split_axis=0, concat_axis=0, tiled=True)
+    everyone = exchanged(share, PLANE_GROUPS)
     out = f32(1, NW, B)
     return local(final_kernel, (out, out), "final")(everyone, back, own)
 

time: 86.6 us -> 79 us (0.912)
  blocking collectives: 55.5 us -> 46.8 us
  starting transfers between devices: 20.9 us -> 21.9 us
    all_to_all x3, blocking collectives: 55.5 us -> 46.8 us  [exchanged(): lax.all_to_all(values, ALL, split_axis=0, concat_axis=0, tiled=True, axis...]
    ppermute x4, starting transfers between devices: 11.7 us -> 13.4 us  [neighbours(): near = lax.ppermute(values, ALL, NEAR)]
    pallas_call x7 -> x11, Pallas kernels: 4.21 us -> 4.53 us  [call(): pl.pallas_call(kernel, out_shape=out, in_specs=[VMEM] * len(args), out_sp...]
where the time goes in v9:
time: 79 us; the launch traced here: 78.1 us
  blocking collectives  46.8 us (59%)
  starting transfers between devices  21.9 us (28%)
  Pallas kernels  5.75 us (7%)
  waiting for transfers between devices  2.88 us (4%)
    all_to_all x3, blocking collectives, exchanged(): lax.all_to_all(values, ALL, split_axis=0, concat_axis=0, tiled=True, axis...  46.8 us
    ppermute x4, starting transfers between devices, neighbours(): near = lax.ppermute(values, ALL, NEAR)  13.4 us
    ppermute x4, starting transfers between devices, neighbours(): far = lax.ppermute(values, ALL, FAR)  8.56 us
    pallas_call x11, Pallas kernels, call(): pl.pallas_call(kernel, out_shape=out, in_specs=[VMEM] * len(args), out_sp...  4.53 us
    ppermute x4, waiting for transfers between devices, neighbours(): near = lax.ppermute(values, ALL, NEAR)  2.87 us
  transfers between devices with their start and end apart: 8, of which 4 were waited for; matrix products, arithmetic and copies ran while one was open for 0% of the time, Pallas kernels for 0%

profile of v9, /device:TPU:1, one launch (start us, length us, event | category | flops | bytes accessed | tf_op | source)
XLA Modules:
  0.0 78.1 jit_solution(1983897059375804366)
XLA Ops:
  0.6 1.2 %pack.1 = (f32[8,136,128]{2,1,0:T(8,128)S(1)}, f32[8,128]{1,0:T(8,128)S(1)}) custom-call(f32[1,8,128,128]{3,2,1,0:T(8,128)} %inverse.1, f32[1,8,128]{2,1,0:T(8,128)} %right.1, f32[1,8,128]{2,1,0:T(8,128)} %cz.1, f32[8,128]{1,0:T(8,128)} %cx.1, f32[1,128]{1,0:T(1,128)} %cy.1), custom_call_target="tpu_custom_call" | custom-call | tf_op jit(solution)/shard_map/pack/pallas_call | solution.py:102
  1.9 18.1 %all_to_all.15.columns = f32[8,136,128]{2,1,0:T(8,128)S(1)} all-to-all(f32[8,136,128]{2,1,0:T(8,128)S(1)} %get-tuple-element.10), channel_id=1, replica_groups={{320,384,448,0,64,128,192,256},{321,385,449,1,65,129,193,257},{322,386,..., dimensions={0} | all-to-all | bytes 1114112 | tf_op jit(solution)/shard_map/all_to_all | solution.py:56
  19.9 0.8 first.1.half
  20.7 1.9 %collective-permute-start.1 = (f32[8,128]{1,0:T(8,128)S(1)}, f32[8,128]{1,0:T(8,128)S(1)}, u32[]{:S(2)}, u32[]{:S(2)}) collective-permute-start(f32[8,128]{1,0:T(8,128)S(1)} %first.1.half), channel_id=1, source_target_pairs={{384,320},{320,384},{256,192},{192,256},{128,0},{0,128},{64,65},{6... | collective-permute-start | bytes 12296 | tf_op jit(solution)/shard_map/ppermute | solution.py:50
  22.6 4.2 %collective-permute-start = (f32[8,128]{1,0:T(8,128)S(1)}, f32[8,128]{1,0:T(8,128)S(1)}, u32[]{:S(2)}, u32[]{:S(2)}) collective-permute-start(f32[8,128]{1,0:T(8,128)S(1)} %first.1.half), channel_id=1, source_target_pairs={{448,384},{384,448},{320,256},{256,320},{192,128},{128,192},{0,64}... | collective-permute-start | bytes 12296 | tf_op jit(solution)/shard_map/ppermute | solution.py:51
  26.8 0.1 settle_first.1
  26.9 0.7 collective-permute-done.near
  27.6 0.8 %backward.2.values.z = f32[8,128]{1,0:T(8,128)S(1)} custom-call(f32[8,136,128]{2,1,0:T(8,128)S(1)} %all_to_all.15.columns, f32[8,128]{1,0:T(8,128)S(1)} %get-tuple-element.12.base, f32[8,128]{1,0:T(8,128)S(1)} %collective-permute-done.near, f32[8,128]{1,0:T(8,128)S(1)} %collective-permute-done.1.far, f32[8,128]{1,0:T(8,128)S(1)} %get-tuple-element.13.cy, ...), custom_call_target="tpu_custom_call" | custom-call | tf_op jit(solution)/shard_map/backward/pallas_call | solution.py:236
  28.4 1.9 %collective-permute-start.3 = (f32[8,128]{1,0:T(8,128)S(1)}, f32[8,128]{1,0:T(8,128)S(1)}, u32[]{:S(2)}, u32[]{:S(2)}) collective-permute-start(f32[8,128]{1,0:T(8,128)S(1)} %backward.2.values.z), channel_id=1, source_target_pairs={{384,320},{320,384},{256,192},{192,256},{128,0},{0,128},{64,65},{6... | collective-permute-start | bytes 12296 | tf_op jit(solution)/shard_map/ppermute | solution.py:50
  30.3 3.6 %collective-permute-start.2 = (f32[8,128]{1,0:T(8,128)S(1)}, f32[8,128]{1,0:T(8,128)S(1)}, u32[]{:S(2)}, u32[]{:S(2)}) collective-permute-start(f32[8,128]{1,0:T(8,128)S(1)} %backward.2.values.z), channel_id=1, source_target_pairs={{448,384},{384,448},{320,256},{256,320},{192,128},{128,192},{0,64}... | collective-permute-start | bytes 12296 | tf_op jit(solution)/shard_map/ppermute | solution.py:51
  34.0 0.7 collective-permute-done.2.near
  34.7 0.8 %image.1 = (f32[8,128]{1,0:T(8,128)S(1)}, f32[8,128]{1,0:T(8,128)S(1)}) custom-call(f32[8,136,128]{2,1,0:T(8,128)S(1)} %all_to_all.15.columns, f32[8,128]{1,0:T(8,128)S(1)} %image_part.2.local, f32[8,128]{1,0:T(8,128)S(1)} %collective-permute-done.2.near, f32[8,128]{1,0:T(8,128)S(1)} %collective-permute-done.3.far, f32[8,128]{1,0:T(8,128)S(1)} %get-tuple-element.13.cy), custom_call_target="tpu_custom_call" | custom-call | tf_op jit(solution)/shard_map/image/pallas_call | solution.py:236
  35.5 2.1 %collective-permute-start.5 = (f32[8,128]{1,0:T(8,128)S(1)}, f32[8,128]{1,0:T(8,128)S(1)}, u32[]{:S(2)}, u32[]{:S(2)}) collective-permute-start(f32[8,128]{1,0:T(8,128)S(1)} %get-tuple-element.16.half), channel_id=1, source_target_pairs={{384,320},{320,384},{256,192},{192,256},{128,0},{0,128},{64,65},{6... | collective-permute-start | bytes 12296 | tf_op jit(solution)/shard_map/ppermute | solution.py:50
  37.6 2.8 %collective-permute-start.4 = (f32[8,128]{1,0:T(8,128)S(1)}, f32[8,128]{1,0:T(8,128)S(1)}, u32[]{:S(2)}, u32[]{:S(2)}) collective-permute-start(f32[8,128]{1,0:T(8,128)S(1)} %get-tuple-element.16.half), channel_id=1, source_target_pairs={{448,384},{384,448},{320,256},{256,320},{192,128},{128,192},{0,64}... | collective-permute-start | bytes 12296 | tf_op jit(solution)/shard_map/ppermute | solution.py:51
  40.4 0.1 settle.1.base
  40.5 0.7 collective-permute-done.4.near
  41.2 0.8 %backward.3.values.w = f32[8,128]{1,0:T(8,128)S(1)} custom-call(f32[8,136,128]{2,1,0:T(8,128)S(1)} %all_to_all.15.columns, f32[8,128]{1,0:T(8,128)S(1)} %settle.1.base, f32[8,128]{1,0:T(8,128)S(1)} %collective-permute-done.4.near, f32[8,128]{1,0:T(8,128)S(1)} %collective-permute-done.5.far, f32[8,128]{1,0:T(8,128)S(1)} %get-tuple-element.13.cy, ...), custom_call_target="tpu_custom_call" | custom-call | tf_op jit(solution)/shard_map/backward/pallas_call | solution.py:236
  42.0 2.7 %collective-permute-start.7 = (f32[8,128]{1,0:T(8,128)S(1)}, f32[8,128]{1,0:T(8,128)S(1)}, u32[]{:S(2)}, u32[]{:S(2)}) collective-permute-start(f32[8,128]{1,0:T(8,128)S(1)} %backward.3.values.w), channel_id=1, source_target_pairs={{384,320},{320,384},{256,192},{192,256},{128,0},{0,128},{64,65},{6... | collective-permute-start | bytes 12296 | tf_op jit(solution)/shard_map/ppermute | solution.py:50
  44.7 2.8 %collective-permute-start.6 = (f32[8,128]{1,0:T(8,128)S(1)}, f32[8,128]{1,0:T(8,128)S(1)}, u32[]{:S(2)}, u32[]{:S(2)}) collective-permute-start(f32[8,128]{1,0:T(8,128)S(1)} %backward.3.values.w), channel_id=1, source_target_pairs={{448,384},{384,448},{320,256},{256,320},{192,128},{128,192},{0,64}... | collective-permute-start | bytes 12296 | tf_op jit(solution)/shard_map/ppermute | solution.py:51
  47.6 0.7 collective-permute-done.6.near
  48.3 0.1 sums.1
  48.4 6.6 %all_to_all.16.back = f32[8,8,128]{2,1,0:T(8,128)S(1)} all-to-all(f32[8,8,128]{2,1,0:T(8,128)S(1)} %sums.1), channel_id=1, replica_groups={{320,384,448,0,64,128,192,256},{321,385,449,1,65,129,193,257},{322,386,..., dimensions={0} | all-to-all | bytes 65536 | tf_op jit(solution)/shard_map/all_to_all | solution.py:56
  55.0 22.1 %all_to_all.17.everyone = f32[64,1,128]{2,1,0:T(1,128)S(1)} all-to-all(f32[64,1,128]{2,1,0:T(1,128)S(1)} %share.1), channel_id=1, replica_groups={{40,41,42,43,44,45,46,47,48,49,50,51,52,53,54,55,56,57,58,59,60,61,62,6..., dimensions={0} | all-to-all | bytes 65536 | tf_op jit(solution)/shard_map/all_to_all | solution.py:56
  77.1 1.0 %final.1 = (f32[1,8,128]{2,1,0:T(8,128)}, f32[1,8,128]{2,1,0:T(8,128)}) custom-call(f32[64,1,128]{2,1,0:T(1,128)S(1)} %all_to_all.17.everyone, f32[8,8,128]{2,1,0:T(8,128)S(1)} %all_to_all.16.back, f32[8,128]{1,0:T(8,128)S(1)} %get-tuple-element.17.r), custom_call_target="tpu_custom_call" | custom-call | tf_op jit(solution)/shard_map/final/pallas_call | solution.py:236
  (7 shorter events, 0.2 us)
Async XLA Ops:
  20.7 6.2 %collective-permute-start.1 = (f32[8,128]{1,0:T(8,128)S(1)}, f32[8,128]{1,0:T(8,128)S(1)}, u32[]{:S(2)}, u32[]{:S(2)}) collective-permute-start(f32[8,128]{1,0:T(8,128)S(1)} %first.1.half), channel_id=1, source_target_pairs={{384,320},{320,384},{256,192},{192,256},{128,0},{0,128},{64,65},{6... | collective-permute-start | bytes 12296 | tf_op jit(solution)/shard_map/ppermute | solution.py:50
  22.6 5.0 %collective-permute-start = (f32[8,128]{1,0:T(8,128)S(1)}, f32[8,128]{1,0:T(8,128)S(1)}, u32[]{:S(2)}, u32[]{:S(2)}) collective-permute-start(f32[8,128]{1,0:T(8,128)S(1)} %first.1.half), channel_id=1, source_target_pairs={{448,384},{384,448},{320,256},{256,320},{192,128},{128,192},{0,64}... | collective-permute-start | bytes 12296 | tf_op jit(solution)/shard_map/ppermute | solution.py:51
  28.4 5.6 %collective-permute-start.3 = (f32[8,128]{1,0:T(8,128)S(1)}, f32[8,128]{1,0:T(8,128)S(1)}, u32[]{:S(2)}, u32[]{:S(2)}) collective-permute-start(f32[8,128]{1,0:T(8,128)S(1)} %backward.2.values.z), channel_id=1, source_target_pairs={{384,320},{320,384},{256,192},{192,256},{128,0},{0,128},{64,65},{6... | collective-permute-start | bytes 12296 | tf_op jit(solution)/shard_map/ppermute | solution.py:50
  30.3 4.4 %collective-permute-start.2 = (f32[8,128]{1,0:T(8,128)S(1)}, f32[8,128]{1,0:T(8,128)S(1)}, u32[]{:S(2)}, u32[]{:S(2)}) collective-permute-start(f32[8,128]{1,0:T(8,128)S(1)} %backward.2.values.z), channel_id=1, source_target_pairs={{448,384},{384,448},{320,256},{256,320},{192,128},{128,192},{0,64}... | collective-permute-start | bytes 12296 | tf_op jit(solution)/shard_map/ppermute | solution.py:51
  35.5 5.0 %collective-permute-start.5 = (f32[8,128]{1,0:T(8,128)S(1)}, f32[8,128]{1,0:T(8,128)S(1)}, u32[]{:S(2)}, u32[]{:S(2)}) collective-permute-start(f32[8,128]{1,0:T(8,128)S(1)} %get-tuple-element.16.half), channel_id=1, source_target_pairs={{384,320},{320,384},{256,192},{192,256},{128,0},{0,128},{64,65},{6... | collective-permute-start | bytes 12296 | tf_op jit(solution)/shard_map/ppermute | solution.py:50
  37.6 3.6 %collective-permute-start.4 = (f32[8,128]{1,0:T(8,128)S(1)}, f32[8,128]{1,0:T(8,128)S(1)}, u32[]{:S(2)}, u32[]{:S(2)}) collective-permute-start(f32[8,128]{1,0:T(8,128)S(1)} %get-tuple-element.16.half), channel_id=1, source_target_pairs={{448,384},{384,448},{320,256},{256,320},{192,128},{128,192},{0,64}... | collective-permute-start | bytes 12296 | tf_op jit(solution)/shard_map/ppermute | solution.py:51
  42.0 5.6 %collective-permute-start.7 = (f32[8,128]{1,0:T(8,128)S(1)}, f32[8,128]{1,0:T(8,128)S(1)}, u32[]{:S(2)}, u32[]{:S(2)}) collective-permute-start(f32[8,128]{1,0:T(8,128)S(1)} %backward.3.values.w), channel_id=1, source_target_pairs={{384,320},{320,384},{256,192},{192,256},{128,0},{0,128},{64,65},{6... | collective-permute-start | bytes 12296 | tf_op jit(solution)/shard_map/ppermute | solution.py:50
  44.7 3.6 %collective-permute-start.6 = (f32[8,128]{1,0:T(8,128)S(1)}, f32[8,128]{1,0:T(8,128)S(1)}, u32[]{:S(2)}, u32[]{:S(2)}) collective-permute-start(f32[8,128]{1,0:T(8,128)S(1)} %backward.3.values.w), channel_id=1, source_target_pairs={{448,384},{384,448},{320,256},{256,320},{192,128},{128,192},{0,64}... | collective-permute-start | bytes 12296 | tf_op jit(solution)/shard_map/ppermute | solution.py:51

commit v10 on v9

--- a/solution.py
+++ b/solution.py
@@ -39,10 +39,17 @@
 
 
 NEAR = swap_pairs(0)
-PLANE_GROUPS = [[w * NP + (p + 40) % NP for p in range(NP)] for w in range(NW)]
 ORDER = (5, 6, 7, 0, 1, 2, 3, 4)
 WAVE_GROUPS = [[w * NP + p for w in ORDER] for p in range(NP)]
 PLACE = tuple(ORDER.index(w) for w in range(NW))
+NY = 4
+NZ = NP // NY
+SLAB_GROUPS = [
+    [w * NP + (y + 2) % NY * NZ + z for y in range(NY) for w in ORDER] for z in range(NZ)
+]
+RING_GROUPS = [
+    [w * NP + y * NZ + (z + 8) % NZ for z in range(NZ)] for w in range(NW) for y in range(NY)
+]
 FAR = swap_pairs(1)
 
 
@@ -206,14 +213,16 @@
     rest = jnp.zeros((3, B), jnp.float32)
     for x in range(NW):
         at = slice(x, x + 1)
-        back[PLACE[x]] = jnp.concatenate([z_a[at], q_a[at], w_a[at], p_a[at], row, rest], axis=0)
+        tile = jnp.concatenate([z_a[at], q_a[at], w_a[at], p_a[at], row, rest], axis=0)
+        for y in range(NY):
+            back[y * NW + PLACE[x]] = tile
 
 
 def share_kernel(back, out):
     part = back[0, 4:5, :]
-    for x in range(1, NW):
+    for x in range(1, NY * NW):
         part = part + back[x, 4:5, :]
-    out[...] = jnp.broadcast_to(part[None], (NP, 1, B))
+    out[...] = jnp.broadcast_to(part[None], (NZ, 1, B))
 
 
 def final_kernel(everyone, back, r, solution_out, residual_out):
@@ -223,8 +232,9 @@
     ratio = wq / zq
     second = (first * wq - wr) / (wp - ratio * wq)
     lead = first + second * ratio
+    slab = (lax.axis_index("plane_0") + NY - 2) % NY * NW
     for j in range(NW):
-        field = back[turned(j)]
+        field = back[slab + turned(j)]
         solution_out[0, j : j + 1, :] = lead * field[0:1] - second * field[2:3]
         residual_out[0, j : j + 1, :] = r[j : j + 1] - lead * field[1:2] + second * field[3:4]
 
@@ -259,10 +269,10 @@
     base = local(settle_kernel, field, "settle")(q, half, faces)
     w = local(backward_kernel, field, "backward")(columns, base, near, far, cy, half)
     far, near = neighbours(w)
-    back = local(sums_kernel, on_chip(NW, 8, B), "sums")(r, z, q, w, image_part(w), near, far, cy)
-    back = exchanged(back, WAVE_GROUPS)
-    share = local(share_kernel, on_chip(NP, 1, B), "share")(back)
-    everyone = exchanged(share, PLANE_GROUPS)
+    back = local(sums_kernel, on_chip(NY * NW, 8, B), "sums")(r, z, q, w, image_part(w), near, far, cy)
+    back = exchanged(back, SLAB_GROUPS)
+    share = local(share_kernel, on_chip(NZ, 1, B), "share")(back)
+    everyone = exchanged(share, RING_GROUPS)
     out = f32(1, NW, B)
     return local(final_kernel, (out, out), "final")(everyone, back, own)
 

time: 79 us -> 78.6 us (level)
  no operation moved by 1% of the time
where the time goes in v10:
time: 78.6 us; the launch traced here: 77.7 us
  blocking collectives  46.5 us (59%)
  starting transfers between devices  21.9 us (28%)
  Pallas kernels  5.72 us (7%)
  waiting for transfers between devices  2.88 us (4%)
    all_to_all x3, blocking collectives, exchanged(): lax.all_to_all(values, ALL, split_axis=0, concat_axis=0, tiled=True, axis...  46.5 us
    ppermute x4, starting transfers between devices, neighbours(): near = lax.ppermute(values, ALL, NEAR)  13.4 us
    ppermute x4, starting transfers between devices, neighbours(): far = lax.ppermute(values, ALL, FAR)  8.56 us
    pallas_call x11, Pallas kernels, call(): pl.pallas_call(kernel, out_shape=out, in_specs=[VMEM] * len(args), out_sp...  4.49 us
    ppermute x4, waiting for transfers between devices, neighbours(): near = lax.ppermute(values, ALL, NEAR)  2.87 us
  transfers between devices with their start and end apart: 8, of which 4 were waited for; matrix products, arithmetic and copies ran while one was open for 0% of the time, Pallas kernels for 0%

profile of v10, /device:TPU:1, one launch (start us, length us, event | category | flops | bytes accessed | tf_op | source)
XLA Modules:
  0.0 77.7 jit_solution(9229672176035664194)
XLA Ops:
  0.6 1.2 %pack.1 = (f32[8,136,128]{2,1,0:T(8,128)S(1)}, f32[8,128]{1,0:T(8,128)S(1)}) custom-call(f32[1,8,128,128]{3,2,1,0:T(8,128)} %inverse.1, f32[1,8,128]{2,1,0:T(8,128)} %right.1, f32[1,8,128]{2,1,0:T(8,128)} %cz.1, f32[8,128]{1,0:T(8,128)} %cx.1, f32[1,128]{1,0:T(1,128)} %cy.1), custom_call_target="tpu_custom_call" | custom-call | tf_op jit(solution)/shard_map/pack/pallas_call | solution.py:109
  1.9 18.1 %all_to_all.15.columns = f32[8,136,128]{2,1,0:T(8,128)S(1)} all-to-all(f32[8,136,128]{2,1,0:T(8,128)S(1)} %get-tuple-element.10), channel_id=1, replica_groups={{320,384,448,0,64,128,192,256},{321,385,449,1,65,129,193,257},{322,386,..., dimensions={0} | all-to-all | bytes 1114112 | tf_op jit(solution)/shard_map/all_to_all | solution.py:63
  19.9 0.8 first.1.half
  20.7 1.9 %collective-permute-start.1 = (f32[8,128]{1,0:T(8,128)S(1)}, f32[8,128]{1,0:T(8,128)S(1)}, u32[]{:S(2)}, u32[]{:S(2)}) collective-permute-start(f32[8,128]{1,0:T(8,128)S(1)} %first.1.half), channel_id=1, source_target_pairs={{384,320},{320,384},{256,192},{192,256},{128,0},{0,128},{64,65},{6... | collective-permute-start | bytes 12296 | tf_op jit(solution)/shard_map/ppermute | solution.py:57
  22.6 4.2 %collective-permute-start = (f32[8,128]{1,0:T(8,128)S(1)}, f32[8,128]{1,0:T(8,128)S(1)}, u32[]{:S(2)}, u32[]{:S(2)}) collective-permute-start(f32[8,128]{1,0:T(8,128)S(1)} %first.1.half), channel_id=1, source_target_pairs={{448,384},{384,448},{320,256},{256,320},{192,128},{128,192},{0,64}... | collective-permute-start | bytes 12296 | tf_op jit(solution)/shard_map/ppermute | solution.py:58
  26.8 0.1 settle_first.1
  26.9 0.7 collective-permute-done.near
  27.6 0.8 %backward.2.values.z = f32[8,128]{1,0:T(8,128)S(1)} custom-call(f32[8,136,128]{2,1,0:T(8,128)S(1)} %all_to_all.15.columns, f32[8,128]{1,0:T(8,128)S(1)} %get-tuple-element.12.base, f32[8,128]{1,0:T(8,128)S(1)} %collective-permute-done.near, f32[8,128]{1,0:T(8,128)S(1)} %collective-permute-done.1.far, f32[8,128]{1,0:T(8,128)S(1)} %get-tuple-element.13.cy, ...), custom_call_target="tpu_custom_call" | custom-call | tf_op jit(solution)/shard_map/backward/pallas_call | solution.py:246
  28.4 1.9 %collective-permute-start.3 = (f32[8,128]{1,0:T(8,128)S(1)}, f32[8,128]{1,0:T(8,128)S(1)}, u32[]{:S(2)}, u32[]{:S(2)}) collective-permute-start(f32[8,128]{1,0:T(8,128)S(1)} %backward.2.values.z), channel_id=1, source_target_pairs={{384,320},{320,384},{256,192},{192,256},{128,0},{0,128},{64,65},{6... | collective-permute-start | bytes 12296 | tf_op jit(solution)/shard_map/ppermute | solution.py:57
  30.3 3.6 %collective-permute-start.2 = (f32[8,128]{1,0:T(8,128)S(1)}, f32[8,128]{1,0:T(8,128)S(1)}, u32[]{:S(2)}, u32[]{:S(2)}) collective-permute-start(f32[8,128]{1,0:T(8,128)S(1)} %backward.2.values.z), channel_id=1, source_target_pairs={{448,384},{384,448},{320,256},{256,320},{192,128},{128,192},{0,64}... | collective-permute-start | bytes 12296 | tf_op jit(solution)/shard_map/ppermute | solution.py:58
  34.0 0.7 collective-permute-done.2.near
  34.7 0.8 %image.1 = (f32[8,128]{1,0:T(8,128)S(1)}, f32[8,128]{1,0:T(8,128)S(1)}) custom-call(f32[8,136,128]{2,1,0:T(8,128)S(1)} %all_to_all.15.columns, f32[8,128]{1,0:T(8,128)S(1)} %image_part.2.local, f32[8,128]{1,0:T(8,128)S(1)} %collective-permute-done.2.near, f32[8,128]{1,0:T(8,128)S(1)} %collective-permute-done.3.far, f32[8,128]{1,0:T(8,128)S(1)} %get-tuple-element.13.cy), custom_call_target="tpu_custom_call" | custom-call | tf_op jit(solution)/shard_map/image/pallas_call | solution.py:246
  35.5 2.1 %collective-permute-start.5 = (f32[8,128]{1,0:T(8,128)S(1)}, f32[8,128]{1,0:T(8,128)S(1)}, u32[]{:S(2)}, u32[]{:S(2)}) collective-permute-start(f32[8,128]{1,0:T(8,128)S(1)} %get-tuple-element.16.half), channel_id=1, source_target_pairs={{384,320},{320,384},{256,192},{192,256},{128,0},{0,128},{64,65},{6... | collective-permute-start | bytes 12296 | tf_op jit(solution)/shard_map/ppermute | solution.py:57
  37.6 2.8 %collective-permute-start.4 = (f32[8,128]{1,0:T(8,128)S(1)}, f32[8,128]{1,0:T(8,128)S(1)}, u32[]{:S(2)}, u32[]{:S(2)}) collective-permute-start(f32[8,128]{1,0:T(8,128)S(1)} %get-tuple-element.16.half), channel_id=1, source_target_pairs={{448,384},{384,448},{320,256},{256,320},{192,128},{128,192},{0,64}... | collective-permute-start | bytes 12296 | tf_op jit(solution)/shard_map/ppermute | solution.py:58
  40.4 0.1 settle.1.base
  40.5 0.7 collective-permute-done.4.near
  41.2 0.8 %backward.3.values.w = f32[8,128]{1,0:T(8,128)S(1)} custom-call(f32[8,136,128]{2,1,0:T(8,128)S(1)} %all_to_all.15.columns, f32[8,128]{1,0:T(8,128)S(1)} %settle.1.base, f32[8,128]{1,0:T(8,128)S(1)} %collective-permute-done.4.near, f32[8,128]{1,0:T(8,128)S(1)} %collective-permute-done.5.far, f32[8,128]{1,0:T(8,128)S(1)} %get-tuple-element.13.cy, ...), custom_call_target="tpu_custom_call" | custom-call | tf_op jit(solution)/shard_map/backward/pallas_call | solution.py:246
  42.0 2.7 %collective-permute-start.7 = (f32[8,128]{1,0:T(8,128)S(1)}, f32[8,128]{1,0:T(8,128)S(1)}, u32[]{:S(2)}, u32[]{:S(2)}) collective-permute-start(f32[8,128]{1,0:T(8,128)S(1)} %backward.3.values.w), channel_id=1, source_target_pairs={{384,320},{320,384},{256,192},{192,256},{128,0},{0,128},{64,65},{6... | collective-permute-start | bytes 12296 | tf_op jit(solution)/shard_map/ppermute | solution.py:57
  44.7 2.8 %collective-permute-start.6 = (f32[8,128]{1,0:T(8,128)S(1)}, f32[8,128]{1,0:T(8,128)S(1)}, u32[]{:S(2)}, u32[]{:S(2)}) collective-permute-start(f32[8,128]{1,0:T(8,128)S(1)} %backward.3.values.w), channel_id=1, source_target_pairs={{448,384},{384,448},{320,256},{256,320},{192,128},{128,192},{0,64}... | collective-permute-start | bytes 12296 | tf_op jit(solution)/shard_map/ppermute | solution.py:58
  47.6 0.7 collective-permute-done.6.near
  48.3 0.1 sums.1
  48.4 15.6 %all_to_all.16.back = f32[32,8,128]{2,1,0:T(8,128)S(1)} all-to-all(f32[32,8,128]{2,1,0:T(8,128)S(1)} %sums.1), channel_id=1, replica_groups={{352,416,480,32,96,160,224,288,368,432,496,48,112,176,240,304,320,384,4..., dimensions={0} | all-to-all | bytes 262144 | tf_op jit(solution)/shard_map/all_to_all | solution.py:63
  64.0 12.8 %all_to_all.17.everyone = f32[16,1,128]{2,1,0:T(1,128)S(1)} all-to-all(f32[16,1,128]{2,1,0:T(1,128)S(1)} %share.1), channel_id=1, replica_groups={{8,9,10,11,12,13,14,15,0,1,2,3,4,5,6,7},{24,25,26,27,28,29,30,31,16,17,..., dimensions={0} | all-to-all | bytes 16384 | tf_op jit(solution)/shard_map/all_to_all | solution.py:63
  76.8 0.9 %final.1 = (f32[1,8,128]{2,1,0:T(8,128)}, f32[1,8,128]{2,1,0:T(8,128)}) custom-call(f32[16,1,128]{2,1,0:T(1,128)S(1)} %all_to_all.17.everyone, f32[32,8,128]{2,1,0:T(8,128)S(1)} %all_to_all.16.back, f32[8,128]{1,0:T(8,128)S(1)} %get-tuple-element.17.r), custom_call_target="tpu_custom_call" | custom-call | tf_op jit(solution)/shard_map/final/pallas_call | solution.py:246
  (7 shorter events, 0.2 us)
Async XLA Ops:
  20.7 6.2 %collective-permute-start.1 = (f32[8,128]{1,0:T(8,128)S(1)}, f32[8,128]{1,0:T(8,128)S(1)}, u32[]{:S(2)}, u32[]{:S(2)}) collective-permute-start(f32[8,128]{1,0:T(8,128)S(1)} %first.1.half), channel_id=1, source_target_pairs={{384,320},{320,384},{256,192},{192,256},{128,0},{0,128},{64,65},{6... | collective-permute-start | bytes 12296 | tf_op jit(solution)/shard_map/ppermute | solution.py:57
  22.6 5.0 %collective-permute-start = (f32[8,128]{1,0:T(8,128)S(1)}, f32[8,128]{1,0:T(8,128)S(1)}, u32[]{:S(2)}, u32[]{:S(2)}) collective-permute-start(f32[8,128]{1,0:T(8,128)S(1)} %first.1.half), channel_id=1, source_target_pairs={{448,384},{384,448},{320,256},{256,320},{192,128},{128,192},{0,64}... | collective-permute-start | bytes 12296 | tf_op jit(solution)/shard_map/ppermute | solution.py:58
  28.4 5.6 %collective-permute-start.3 = (f32[8,128]{1,0:T(8,128)S(1)}, f32[8,128]{1,0:T(8,128)S(1)}, u32[]{:S(2)}, u32[]{:S(2)}) collective-permute-start(f32[8,128]{1,0:T(8,128)S(1)} %backward.2.values.z), channel_id=1, source_target_pairs={{384,320},{320,384},{256,192},{192,256},{128,0},{0,128},{64,65},{6... | collective-permute-start | bytes 12296 | tf_op jit(solution)/shard_map/ppermute | solution.py:57
  30.3 4.4 %collective-permute-start.2 = (f32[8,128]{1,0:T(8,128)S(1)}, f32[8,128]{1,0:T(8,128)S(1)}, u32[]{:S(2)}, u32[]{:S(2)}) collective-permute-start(f32[8,128]{1,0:T(8,128)S(1)} %backward.2.values.z), channel_id=1, source_target_pairs={{448,384},{384,448},{320,256},{256,320},{192,128},{128,192},{0,64}... | collective-permute-start | bytes 12296 | tf_op jit(solution)/shard_map/ppermute | solution.py:58
  35.5 5.0 %collective-permute-start.5 = (f32[8,128]{1,0:T(8,128)S(1)}, f32[8,128]{1,0:T(8,128)S(1)}, u32[]{:S(2)}, u32[]{:S(2)}) collective-permute-start(f32[8,128]{1,0:T(8,128)S(1)} %get-tuple-element.16.half), channel_id=1, source_target_pairs={{384,320},{320,384},{256,192},{192,256},{128,0},{0,128},{64,65},{6... | collective-permute-start | bytes 12296 | tf_op jit(solution)/shard_map/ppermute | solution.py:57
  37.6 3.6 %collective-permute-start.4 = (f32[8,128]{1,0:T(8,128)S(1)}, f32[8,128]{1,0:T(8,128)S(1)}, u32[]{:S(2)}, u32[]{:S(2)}) collective-permute-start(f32[8,128]{1,0:T(8,128)S(1)} %get-tuple-element.16.half), channel_id=1, source_target_pairs={{448,384},{384,448},{320,256},{256,320},{192,128},{128,192},{0,64}... | collective-permute-start | bytes 12296 | tf_op jit(solution)/shard_map/ppermute | solution.py:58
  42.0 5.6 %collective-permute-start.7 = (f32[8,128]{1,0:T(8,128)S(1)}, f32[8,128]{1,0:T(8,128)S(1)}, u32[]{:S(2)}, u32[]{:S(2)}) collective-permute-start(f32[8,128]{1,0:T(8,128)S(1)} %backward.3.values.w), channel_id=1, source_target_pairs={{384,320},{320,384},{256,192},{192,256},{128,0},{0,128},{64,65},{6... | collective-permute-start | bytes 12296 | tf_op jit(solution)/shard_map/ppermute | solution.py:57
  44.7 3.6 %collective-permute-start.6 = (f32[8,128]{1,0:T(8,128)S(1)}, f32[8,128]{1,0:T(8,128)S(1)}, u32[]{:S(2)}, u32[]{:S(2)}) collective-permute-start(f32[8,128]{1,0:T(8,128)S(1)} %backward.3.values.w), channel_id=1, source_target_pairs={{448,384},{384,448},{320,256},{256,320},{192,128},{128,192},{0,64}... | collective-permute-start | bytes 12296 | tf_op jit(solution)/shard_map/ppermute | solution.py:58

commit v11 on v10

--- a/solution.py
+++ b/solution.py
@@ -38,7 +38,6 @@
     return pairs
 
 
-NEAR = swap_pairs(0)
 ORDER = (5, 6, 7, 0, 1, 2, 3, 4)
 WAVE_GROUPS = [[w * NP + p for w in ORDER] for p in range(NP)]
 PLACE = tuple(ORDER.index(w) for w in range(NW))
@@ -55,7 +54,7 @@
 
 def neighbours(values):
     far = lax.ppermute(values, ALL, FAR)
-    near = lax.ppermute(values, ALL, NEAR)
+    near = lax.psum(values, "wave_1") - values
     return far, near
 
 

time: 78.6 us -> 77.5 us (0.986)
  blocking collectives: 46.5 us -> 62 us
  starting transfers between devices: 21.9 us -> 8.24 us
  waiting for transfers between devices: 2.88 us -> 0.01 us
    psum x0 -> x4, blocking collectives: none -> 14.6 us  [neighbours(): near = lax.psum(values, 'wave_1') - values]
    ppermute x4 -> x0, starting transfers between devices: 13.4 us -> none  [neighbours(): near = lax.ppermute(values, ALL, NEAR)]
    ppermute x4 -> x0, waiting for transfers between devices: 2.87 us -> none  [neighbours(): near = lax.ppermute(values, ALL, NEAR)]
    all_to_all x3, blocking collectives: 46.5 us -> 47.4 us  [exchanged(): lax.all_to_all(values, ALL, split_axis=0, concat_axis=0, tiled=True, axis...]
  transfers between devices with their start and end apart: 8 -> 4, of which waited for: 4 -> 0; matrix products, arithmetic and copies ran while one was open for 0% -> 0% of each run, Pallas kernels for 0% -> 0%
where the time goes in v11:
time: 77.5 us; the launch traced here: 76.7 us
  blocking collectives  62 us (80%)
  starting transfers between devices  8.24 us (11%)
  Pallas kernels  5.72 us (7%)
    all_to_all x3, blocking collectives, exchanged(): lax.all_to_all(values, ALL, split_axis=0, concat_axis=0, tiled=True, axis...  47.4 us
    psum x4, blocking collectives, neighbours(): near = lax.psum(values, 'wave_1') - values  14.6 us
    ppermute x4, starting transfers between devices, neighbours(): far = lax.ppermute(values, ALL, FAR)  8.24 us
    pallas_call x11, Pallas kernels, call(): pl.pallas_call(kernel, out_shape=out, in_specs=[VMEM] * len(args), out_sp...  4.49 us
  transfers between devices with their start and end apart: 4, of which 0 were waited for; matrix products, arithmetic and copies ran while one was open for 0% of the time, Pallas kernels for 0%

profile of v11, /device:TPU:1, one launch (start us, length us, event | category | flops | bytes accessed | tf_op | source)
XLA Modules:
  0.0 76.7 jit_solution(3787863657514739951)
XLA Ops:
  0.6 1.2 %pack.1 = (f32[8,136,128]{2,1,0:T(8,128)S(1)}, f32[8,128]{1,0:T(8,128)S(1)}) custom-call(f32[1,8,128,128]{3,2,1,0:T(8,128)} %inverse.1, f32[1,8,128]{2,1,0:T(8,128)} %right.1, f32[1,8,128]{2,1,0:T(8,128)} %cz.1, f32[8,128]{1,0:T(8,128)} %cx.1, f32[1,128]{1,0:T(1,128)} %cy.1), custom_call_target="tpu_custom_call" | custom-call | tf_op jit(solution)/shard_map/pack/pallas_call | solution.py:108
  1.9 18.1 %all_to_all.15.columns = f32[8,136,128]{2,1,0:T(8,128)S(1)} all-to-all(f32[8,136,128]{2,1,0:T(8,128)S(1)} %get-tuple-element.10), channel_id=1, replica_groups={{320,384,448,0,64,128,192,256},{321,385,449,1,65,129,193,257},{322,386,..., dimensions={0} | all-to-all | bytes 1114112 | tf_op jit(solution)/shard_map/all_to_all | solution.py:62
  19.9 0.8 %first.1.half = f32[8,128]{1,0:T(8,128)S(1)} custom-call(f32[8,136,128]{2,1,0:T(8,128)S(1)} %all_to_all.15.columns), custom_call_target="tpu_custom_call" | custom-call | tf_op jit(solution)/shard_map/first/pallas_call | solution.py:245
  20.7 1.9 %collective-permute-start = (f32[8,128]{1,0:T(8,128)S(1)}, f32[8,128]{1,0:T(8,128)S(1)}, u32[]{:S(2)}, u32[]{:S(2)}) collective-permute-start(f32[8,128]{1,0:T(8,128)S(1)} %first.1.half), channel_id=1, source_target_pairs={{384,320},{320,384},{256,192},{192,256},{128,0},{0,128},{64,65},{6... | collective-permute-start | bytes 12296 | tf_op jit(solution)/shard_map/ppermute | solution.py:56
  22.6 4.4 %psum.28 = f32[8,128]{1,0:T(8,128)S(1)} all-reduce(f32[8,128]{1,0:T(8,128)S(1)} %first.1.half), channel_id=1, replica_groups=mesh['wave_0'=4,'wave_1'=2,'plane_0'=4,'plane_1'=16] {'wave_1'}, use_global_device_ids=true, to_apply=%region_0.0 | all-reduce | flops 1024 | bytes 8192 | tf_op jit(solution)/shard_map/psum | solution.py:57
  27.0 0.1 settle_first.1
  27.1 0.0 collective-permute-done.far
  27.1 0.8 %backward.2.values.z = f32[8,128]{1,0:T(8,128)S(1)} custom-call(f32[8,136,128]{2,1,0:T(8,128)S(1)} %all_to_all.15.columns, f32[8,128]{1,0:T(8,128)S(1)} %get-tuple-element.12.base, f32[8,128]{1,0:T(8,128)S(1)} %sub.12.near, f32[8,128]{1,0:T(8,128)S(1)} %collective-permute-done.far, f32[8,128]{1,0:T(8,128)S(1)} %get-tuple-element.13.cy, f32[8,128]{1,0:T(8,128)S(1)} %first.1.half), custom_call_target="tpu_custom_call" | custom-call | tf_op jit(solution)/shard_map/backward/pallas_call | solution.py:245
  27.9 1.9 %collective-permute-start.1 = (f32[8,128]{1,0:T(8,128)S(1)}, f32[8,128]{1,0:T(8,128)S(1)}, u32[]{:S(2)}, u32[]{:S(2)}) collective-permute-start(f32[8,128]{1,0:T(8,128)S(1)} %backward.2.values.z), channel_id=1, source_target_pairs={{384,320},{320,384},{256,192},{192,256},{128,0},{0,128},{64,65},{6... | collective-permute-start | bytes 12296 | tf_op jit(solution)/shard_map/ppermute | solution.py:56
  29.8 3.8 %psum.29 = f32[8,128]{1,0:T(8,128)S(1)} all-reduce(f32[8,128]{1,0:T(8,128)S(1)} %backward.2.values.z), channel_id=1, replica_groups=mesh['wave_0'=4,'wave_1'=2,'plane_0'=4,'plane_1'=16] {'wave_1'}, use_global_device_ids=true, to_apply=%region_1.0 | all-reduce | flops 1024 | bytes 8192 | tf_op jit(solution)/shard_map/psum | solution.py:57
  33.6 0.1 image_part.2.local
  33.7 0.8 %image.1 = (f32[8,128]{1,0:T(8,128)S(1)}, f32[8,128]{1,0:T(8,128)S(1)}) custom-call(f32[8,136,128]{2,1,0:T(8,128)S(1)} %all_to_all.15.columns, f32[8,128]{1,0:T(8,128)S(1)} %image_part.2.local, f32[8,128]{1,0:T(8,128)S(1)} %sub.13.near, f32[8,128]{1,0:T(8,128)S(1)} %collective-permute-done.1.far, f32[8,128]{1,0:T(8,128)S(1)} %get-tuple-element.13.cy), custom_call_target="tpu_custom_call" | custom-call | tf_op jit(solution)/shard_map/image/pallas_call | solution.py:245
  34.5 2.1 %collective-permute-start.2 = (f32[8,128]{1,0:T(8,128)S(1)}, f32[8,128]{1,0:T(8,128)S(1)}, u32[]{:S(2)}, u32[]{:S(2)}) collective-permute-start(f32[8,128]{1,0:T(8,128)S(1)} %get-tuple-element.16.half), channel_id=1, source_target_pairs={{384,320},{320,384},{256,192},{192,256},{128,0},{0,128},{64,65},{6... | collective-permute-start | bytes 12296 | tf_op jit(solution)/shard_map/ppermute | solution.py:56
  36.6 0.1 settle.1.base
  36.7 3.3 %psum.30 = f32[8,128]{1,0:T(8,128)S(1)} all-reduce(f32[8,128]{1,0:T(8,128)S(1)} %get-tuple-element.16.half), channel_id=1, replica_groups=mesh['wave_0'=4,'wave_1'=2,'plane_0'=4,'plane_1'=16] {'wave_1'}, use_global_device_ids=true, to_apply=%region_2.0 | all-reduce | flops 1024 | bytes 8192 | tf_op jit(solution)/shard_map/psum | solution.py:57
  40.0 0.8 %backward.3.values.w = f32[8,128]{1,0:T(8,128)S(1)} custom-call(f32[8,136,128]{2,1,0:T(8,128)S(1)} %all_to_all.15.columns, f32[8,128]{1,0:T(8,128)S(1)} %settle.1.base, f32[8,128]{1,0:T(8,128)S(1)} %sub.14.near, f32[8,128]{1,0:T(8,128)S(1)} %collective-permute-done.2.far, f32[8,128]{1,0:T(8,128)S(1)} %get-tuple-element.13.cy, ...), custom_call_target="tpu_custom_call" | custom-call | tf_op jit(solution)/shard_map/backward/pallas_call | solution.py:245
  40.8 0.1 image_part.3.local
  40.9 2.3 %collective-permute-start.3 = (f32[8,128]{1,0:T(8,128)S(1)}, f32[8,128]{1,0:T(8,128)S(1)}, u32[]{:S(2)}, u32[]{:S(2)}) collective-permute-start(f32[8,128]{1,0:T(8,128)S(1)} %backward.3.values.w), channel_id=1, source_target_pairs={{384,320},{320,384},{256,192},{192,256},{128,0},{0,128},{64,65},{6... | collective-permute-start | bytes 12296 | tf_op jit(solution)/shard_map/ppermute | solution.py:56
  43.2 3.1 %psum.31 = f32[8,128]{1,0:T(8,128)S(1)} all-reduce(f32[8,128]{1,0:T(8,128)S(1)} %backward.3.values.w), channel_id=1, replica_groups=mesh['wave_0'=4,'wave_1'=2,'plane_0'=4,'plane_1'=16] {'wave_1'}, use_global_device_ids=true, to_apply=%region_3.0 | all-reduce | flops 1024 | bytes 8192 | tf_op jit(solution)/shard_map/psum | solution.py:57
  46.3 0.0 collective-permute-done.3.far
  46.3 0.1 sums.1
  46.4 16.5 %all_to_all.16.back = f32[32,8,128]{2,1,0:T(8,128)S(1)} all-to-all(f32[32,8,128]{2,1,0:T(8,128)S(1)} %sums.1), channel_id=1, replica_groups={{352,416,480,32,96,160,224,288,368,432,496,48,112,176,240,304,320,384,4..., dimensions={0} | all-to-all | bytes 262144 | tf_op jit(solution)/shard_map/all_to_all | solution.py:62
  63.0 12.8 %all_to_all.17.everyone = f32[16,1,128]{2,1,0:T(1,128)S(1)} all-to-all(f32[16,1,128]{2,1,0:T(1,128)S(1)} %share.1), channel_id=1, replica_groups={{8,9,10,11,12,13,14,15,0,1,2,3,4,5,6,7},{24,25,26,27,28,29,30,31,16,17,..., dimensions={0} | all-to-all | bytes 16384 | tf_op jit(solution)/shard_map/all_to_all | solution.py:62
  75.8 0.9 %final.1 = (f32[1,8,128]{2,1,0:T(8,128)}, f32[1,8,128]{2,1,0:T(8,128)}) custom-call(f32[16,1,128]{2,1,0:T(1,128)S(1)} %all_to_all.17.everyone, f32[32,8,128]{2,1,0:T(8,128)S(1)} %all_to_all.16.back, f32[8,128]{1,0:T(8,128)S(1)} %get-tuple-element.17.r), custom_call_target="tpu_custom_call" | custom-call | tf_op jit(solution)/shard_map/final/pallas_call | solution.py:245
  (7 shorter events, 0.1 us)
Async XLA Ops:
  20.7 6.4 %collective-permute-start = (f32[8,128]{1,0:T(8,128)S(1)}, f32[8,128]{1,0:T(8,128)S(1)}, u32[]{:S(2)}, u32[]{:S(2)}) collective-permute-start(f32[8,128]{1,0:T(8,128)S(1)} %first.1.half), channel_id=1, source_target_pairs={{384,320},{320,384},{256,192},{192,256},{128,0},{0,128},{64,65},{6... | collective-permute-start | bytes 12296 | tf_op jit(solution)/shard_map/ppermute | solution.py:56
  27.9 5.8 %collective-permute-start.1 = (f32[8,128]{1,0:T(8,128)S(1)}, f32[8,128]{1,0:T(8,128)S(1)}, u32[]{:S(2)}, u32[]{:S(2)}) collective-permute-start(f32[8,128]{1,0:T(8,128)S(1)} %backward.2.values.z), channel_id=1, source_target_pairs={{384,320},{320,384},{256,192},{192,256},{128,0},{0,128},{64,65},{6... | collective-permute-start | bytes 12296 | tf_op jit(solution)/shard_map/ppermute | solution.py:56
  34.5 5.5 %collective-permute-start.2 = (f32[8,128]{1,0:T(8,128)S(1)}, f32[8,128]{1,0:T(8,128)S(1)}, u32[]{:S(2)}, u32[]{:S(2)}) collective-permute-start(f32[8,128]{1,0:T(8,128)S(1)} %get-tuple-element.16.half), channel_id=1, source_target_pairs={{384,320},{320,384},{256,192},{192,256},{128,0},{0,128},{64,65},{6... | collective-permute-start | bytes 12296 | tf_op jit(solution)/shard_map/ppermute | solution.py:56
  40.9 5.4 %collective-permute-start.3 = (f32[8,128]{1,0:T(8,128)S(1)}, f32[8,128]{1,0:T(8,128)S(1)}, u32[]{:S(2)}, u32[]{:S(2)}) collective-permute-start(f32[8,128]{1,0:T(8,128)S(1)} %backward.3.values.w), channel_id=1, source_target_pairs={{384,320},{320,384},{256,192},{192,256},{128,0},{0,128},{64,65},{6... | collective-permute-start | bytes 12296 | tf_op jit(solution)/shard_map/ppermute | solution.py:56

commit v12 on v11

--- a/solution.py
+++ b/solution.py
@@ -53,9 +53,7 @@
 
 
 def neighbours(values):
-    far = lax.ppermute(values, ALL, FAR)
-    near = lax.psum(values, "wave_1") - values
-    return far, near
+    return lax.ppermute(values, ALL, FAR), lax.psum(values, "wave_1")
 
 
 def exchanged(values, groups):
@@ -141,8 +139,8 @@
     forward(columns, lambda x: columns[PLACE[x], R : R + 1, :], half)
 
 
-def image_kernel(columns, local, near, far, cy, image, half):
-    image[...] = local[...] - cy[...] * (far[...] + near[...])
+def image_kernel(columns, local, both, far, cy, own, image, half):
+    image[...] = local[...] - cy[...] * (far[...] + (both[...] - own[...]))
     value = image[...]
     forward(columns, lambda x: value[x : x + 1], half)
 
@@ -189,8 +187,8 @@
     out[...] = column_part(v, faces[3], faces[1], faces[2]) - faces[0] * (lower(v) + upper(v))
 
 
-def backward_kernel(columns, base, near, far, cy, half, out):
-    source = base[...] + cy[...] * (far[...] + near[...])
+def backward_kernel(columns, base, both, far, cy, half, out):
+    source = base[...] + cy[...] * (far[...] + (both[...] - half[...]))
     cx = columns[0, CX : CX + 1, :]
     previous = None
     for x in reversed(range(NW)):
@@ -201,9 +199,9 @@
         out[x : x + 1, :] = previous
 
 
-def sums_kernel(r, z, q, w, local, near, far, cy, back):
+def sums_kernel(r, z, q, w, local, both, far, cy, back):
     z_a, q_a, w_a = z[...], q[...], w[...]
-    p_a = local[...] - cy[...] * (far[...] + near[...])
+    p_a = local[...] - cy[...] * (far[...] + (both[...] - w_a))
     lane = lax.broadcasted_iota(jnp.int32, (1, B), 1)
     row = jnp.zeros((1, B), jnp.float32)
     for k, product in enumerate((z_a * r[...], z_a * q_a, w_a * r[...], w_a * q_a, w_a * p_a)):
@@ -258,17 +256,17 @@
         return local(image_part_kernel, field, "image_part")(values, faces)
 
     half = local(first_kernel, field, "first")(columns)
-    far, near = neighbours(half)
+    far, both = neighbours(half)
     parts = (field, field, on_chip(4, NW, B), field)
     base, r, faces, cy = local(settle_first_kernel, parts, "settle_first")(columns, half)
-    z = local(backward_kernel, field, "backward")(columns, base, near, far, cy, half)
-    far, near = neighbours(z)
-    q, half = local(image_kernel, (field, field), "image")(columns, image_part(z), near, far, cy)
-    far, near = neighbours(half)
+    z = local(backward_kernel, field, "backward")(columns, base, both, far, cy, half)
+    far, both = neighbours(z)
+    q, half = local(image_kernel, (field, field), "image")(columns, image_part(z), both, far, cy, z)
+    far, both = neighbours(half)
     base = local(settle_kernel, field, "settle")(q, half, faces)
-    w = local(backward_kernel, field, "backward")(columns, base, near, far, cy, half)
-    far, near = neighbours(w)
-    back = local(sums_kernel, on_chip(NY * NW, 8, B), "sums")(r, z, q, w, image_part(w), near, far, cy)
+    w = local(backward_kernel, field, "backward")(columns, base, both, far, cy, half)
+    far, both = neighbours(w)
+    back = local(sums_kernel, on_chip(NY * NW, 8, B), "sums")(r, z, q, w, image_part(w), both, far, cy)
     back = exchanged(back, SLAB_GROUPS)
     share = local(share_kernel, on_chip(NZ, 1, B), "share")(back)
     everyone = exchanged(share, RING_GROUPS)

time: 77.5 us -> 77.4 us (level)
  no operation moved by 1% of the time
where the time goes in v12:
time: 77.4 us; the launch traced here: 76.7 us
  blocking collectives  62 us (80%)
  starting transfers between devices  8.2 us (11%)
  Pallas kernels  5.73 us (7%)
    all_to_all x3, blocking collectives, exchanged(): lax.all_to_all(values, ALL, split_axis=0, concat_axis=0, tiled=True, axis...  47.4 us
    psum x4, blocking collectives, neighbours(): return (lax.ppermute(values, ALL, FAR), lax.psum(values, 'wave_1'))  14.6 us
    ppermute x4, starting transfers between devices, neighbours(): return (lax.ppermute(values, ALL, FAR), lax.psum(values, 'wave_1'))  8.2 us
    pallas_call x11, Pallas kernels, call(): pl.pallas_call(kernel, out_shape=out, in_specs=[VMEM] * len(args), out_sp...  4.5 us
  transfers between devices with their start and end apart: 4, of which 0 were waited for; matrix products, arithmetic and copies ran while one was open for 0% of the time, Pallas kernels for 0%

profile of v12, /device:TPU:1, one launch (start us, length us, event | category | flops | bytes accessed | tf_op | source)
XLA Modules:
  0.0 76.7 jit_solution(3495676916292515375)
XLA Ops:
  0.6 1.2 %pack.1 = (f32[8,136,128]{2,1,0:T(8,128)S(1)}, f32[8,128]{1,0:T(8,128)S(1)}) custom-call(f32[1,8,128,128]{3,2,1,0:T(8,128)} %inverse.1, f32[1,8,128]{2,1,0:T(8,128)} %right.1, f32[1,8,128]{2,1,0:T(8,128)} %cz.1, f32[8,128]{1,0:T(8,128)} %cx.1, f32[1,128]{1,0:T(1,128)} %cy.1), custom_call_target="tpu_custom_call" | custom-call | tf_op jit(solution)/shard_map/pack/pallas_call | solution.py:106
  1.9 18.1 %all_to_all.15.columns = f32[8,136,128]{2,1,0:T(8,128)S(1)} all-to-all(f32[8,136,128]{2,1,0:T(8,128)S(1)} %get-tuple-element.10), channel_id=1, replica_groups={{320,384,448,0,64,128,192,256},{321,385,449,1,65,129,193,257},{322,386,..., dimensions={0} | all-to-all | bytes 1114112 | tf_op jit(solution)/shard_map/all_to_all | solution.py:60
  19.9 0.8 %first.1.half = f32[8,128]{1,0:T(8,128)S(1)} custom-call(f32[8,136,128]{2,1,0:T(8,128)S(1)} %all_to_all.15.columns), custom_call_target="tpu_custom_call" | custom-call | tf_op jit(solution)/shard_map/first/pallas_call | solution.py:243
  20.7 1.9 %collective-permute-start = (f32[8,128]{1,0:T(8,128)S(1)}, f32[8,128]{1,0:T(8,128)S(1)}, u32[]{:S(2)}, u32[]{:S(2)}) collective-permute-start(f32[8,128]{1,0:T(8,128)S(1)} %first.1.half), channel_id=1, source_target_pairs={{384,320},{320,384},{256,192},{192,256},{128,0},{0,128},{64,65},{6... | collective-permute-start | bytes 12296 | tf_op jit(solution)/shard_map/ppermute | solution.py:56
  22.6 0.1 settle_first.1
  22.7 4.4 %psum.28.both = f32[8,128]{1,0:T(8,128)S(1)} all-reduce(f32[8,128]{1,0:T(8,128)S(1)} %first.1.half), channel_id=1, replica_groups=mesh['wave_0'=4,'wave_1'=2,'plane_0'=4,'plane_1'=16] {'wave_1'}, use_global_device_ids=true, to_apply=%region_0.0 | all-reduce | flops 1024 | bytes 8192 | tf_op jit(solution)/shard_map/psum | solution.py:56
  27.1 0.0 collective-permute-done.far
  27.1 0.8 %backward.2.values.own.z = f32[8,128]{1,0:T(8,128)S(1)} custom-call(f32[8,136,128]{2,1,0:T(8,128)S(1)} %all_to_all.15.columns, f32[8,128]{1,0:T(8,128)S(1)} %get-tuple-element.12.base, f32[8,128]{1,0:T(8,128)S(1)} %psum.28.both, f32[8,128]{1,0:T(8,128)S(1)} %collective-permute-done.far, f32[8,128]{1,0:T(8,128)S(1)} %get-tuple-element.13.cy, ...), custom_call_target="tpu_custom_call" | custom-call | tf_op jit(solution)/shard_map/backward/pallas_call | solution.py:243
  27.9 1.9 %collective-permute-start.1 = (f32[8,128]{1,0:T(8,128)S(1)}, f32[8,128]{1,0:T(8,128)S(1)}, u32[]{:S(2)}, u32[]{:S(2)}) collective-permute-start(f32[8,128]{1,0:T(8,128)S(1)} %backward.2.values.own.z), channel_id=1, source_target_pairs={{384,320},{320,384},{256,192},{192,256},{128,0},{0,128},{64,65},{6... | collective-permute-start | bytes 12296 | tf_op jit(solution)/shard_map/ppermute | solution.py:56
  29.8 0.1 image_part.2.local
  29.9 3.8 %psum.29.both = f32[8,128]{1,0:T(8,128)S(1)} all-reduce(f32[8,128]{1,0:T(8,128)S(1)} %backward.2.values.own.z), channel_id=1, replica_groups=mesh['wave_0'=4,'wave_1'=2,'plane_0'=4,'plane_1'=16] {'wave_1'}, use_global_device_ids=true, to_apply=%region_1.0 | all-reduce | flops 1024 | bytes 8192 | tf_op jit(solution)/shard_map/psum | solution.py:56
  33.6 0.0 collective-permute-done.1.far
  33.7 0.8 %image.1 = (f32[8,128]{1,0:T(8,128)S(1)}, f32[8,128]{1,0:T(8,128)S(1)}) custom-call(f32[8,136,128]{2,1,0:T(8,128)S(1)} %all_to_all.15.columns, f32[8,128]{1,0:T(8,128)S(1)} %image_part.2.local, f32[8,128]{1,0:T(8,128)S(1)} %psum.29.both, f32[8,128]{1,0:T(8,128)S(1)} %collective-permute-done.1.far, f32[8,128]{1,0:T(8,128)S(1)} %get-tuple-element.13.cy, ...), custom_call_target="tpu_custom_call" | custom-call | tf_op jit(solution)/shard_map/image/pallas_call | solution.py:243
  34.4 2.1 %collective-permute-start.2 = (f32[8,128]{1,0:T(8,128)S(1)}, f32[8,128]{1,0:T(8,128)S(1)}, u32[]{:S(2)}, u32[]{:S(2)}) collective-permute-start(f32[8,128]{1,0:T(8,128)S(1)} %get-tuple-element.16.half), channel_id=1, source_target_pairs={{384,320},{320,384},{256,192},{192,256},{128,0},{0,128},{64,65},{6... | collective-permute-start | bytes 12296 | tf_op jit(solution)/shard_map/ppermute | solution.py:56
  36.5 0.1 settle.1.base
  36.6 3.4 %psum.30.both = f32[8,128]{1,0:T(8,128)S(1)} all-reduce(f32[8,128]{1,0:T(8,128)S(1)} %get-tuple-element.16.half), channel_id=1, replica_groups=mesh['wave_0'=4,'wave_1'=2,'plane_0'=4,'plane_1'=16] {'wave_1'}, use_global_device_ids=true, to_apply=%region_2.0 | all-reduce | flops 1024 | bytes 8192 | tf_op jit(solution)/shard_map/psum | solution.py:56
  39.9 0.8 %backward.3.values.w = f32[8,128]{1,0:T(8,128)S(1)} custom-call(f32[8,136,128]{2,1,0:T(8,128)S(1)} %all_to_all.15.columns, f32[8,128]{1,0:T(8,128)S(1)} %settle.1.base, f32[8,128]{1,0:T(8,128)S(1)} %psum.30.both, f32[8,128]{1,0:T(8,128)S(1)} %collective-permute-done.2.far, f32[8,128]{1,0:T(8,128)S(1)} %get-tuple-element.13.cy, ...), custom_call_target="tpu_custom_call" | custom-call | tf_op jit(solution)/shard_map/backward/pallas_call | solution.py:243
  40.7 0.1 image_part.3.local
  40.8 2.3 %collective-permute-start.3 = (f32[8,128]{1,0:T(8,128)S(1)}, f32[8,128]{1,0:T(8,128)S(1)}, u32[]{:S(2)}, u32[]{:S(2)}) collective-permute-start(f32[8,128]{1,0:T(8,128)S(1)} %backward.3.values.w), channel_id=1, source_target_pairs={{384,320},{320,384},{256,192},{192,256},{128,0},{0,128},{64,65},{6... | collective-permute-start | bytes 12296 | tf_op jit(solution)/shard_map/ppermute | solution.py:56
  43.1 3.1 %psum.31.both = f32[8,128]{1,0:T(8,128)S(1)} all-reduce(f32[8,128]{1,0:T(8,128)S(1)} %backward.3.values.w), channel_id=1, replica_groups=mesh['wave_0'=4,'wave_1'=2,'plane_0'=4,'plane_1'=16] {'wave_1'}, use_global_device_ids=true, to_apply=%region_3.0 | all-reduce | flops 1024 | bytes 8192 | tf_op jit(solution)/shard_map/psum | solution.py:56
  46.3 0.1 sums.1
  46.4 16.5 %all_to_all.16.back = f32[32,8,128]{2,1,0:T(8,128)S(1)} all-to-all(f32[32,8,128]{2,1,0:T(8,128)S(1)} %sums.1), channel_id=1, replica_groups={{352,416,480,32,96,160,224,288,368,432,496,48,112,176,240,304,320,384,4..., dimensions={0} | all-to-all | bytes 262144 | tf_op jit(solution)/shard_map/all_to_all | solution.py:60
  62.9 12.8 %all_to_all.17.everyone = f32[16,1,128]{2,1,0:T(1,128)S(1)} all-to-all(f32[16,1,128]{2,1,0:T(1,128)S(1)} %share.1), channel_id=1, replica_groups={{8,9,10,11,12,13,14,15,0,1,2,3,4,5,6,7},{24,25,26,27,28,29,30,31,16,17,..., dimensions={0} | all-to-all | bytes 16384 | tf_op jit(solution)/shard_map/all_to_all | solution.py:60
  75.8 0.9 %final.1 = (f32[1,8,128]{2,1,0:T(8,128)}, f32[1,8,128]{2,1,0:T(8,128)}) custom-call(f32[16,1,128]{2,1,0:T(1,128)S(1)} %all_to_all.17.everyone, f32[32,8,128]{2,1,0:T(8,128)S(1)} %all_to_all.16.back, f32[8,128]{1,0:T(8,128)S(1)} %get-tuple-element.17.r), custom_call_target="tpu_custom_call" | custom-call | tf_op jit(solution)/shard_map/final/pallas_call | solution.py:243
  (3 shorter events, 0.0 us)
Async XLA Ops:
  20.7 6.4 %collective-permute-start = (f32[8,128]{1,0:T(8,128)S(1)}, f32[8,128]{1,0:T(8,128)S(1)}, u32[]{:S(2)}, u32[]{:S(2)}) collective-permute-start(f32[8,128]{1,0:T(8,128)S(1)} %first.1.half), channel_id=1, source_target_pairs={{384,320},{320,384},{256,192},{192,256},{128,0},{0,128},{64,65},{6... | collective-permute-start | bytes 12296 | tf_op jit(solution)/shard_map/ppermute | solution.py:56
  27.9 5.8 %collective-permute-start.1 = (f32[8,128]{1,0:T(8,128)S(1)}, f32[8,128]{1,0:T(8,128)S(1)}, u32[]{:S(2)}, u32[]{:S(2)}) collective-permute-start(f32[8,128]{1,0:T(8,128)S(1)} %backward.2.values.own.z), channel_id=1, source_target_pairs={{384,320},{320,384},{256,192},{192,256},{128,0},{0,128},{64,65},{6... | collective-permute-start | bytes 12296 | tf_op jit(solution)/shard_map/ppermute | solution.py:56
  34.4 5.5 %collective-permute-start.2 = (f32[8,128]{1,0:T(8,128)S(1)}, f32[8,128]{1,0:T(8,128)S(1)}, u32[]{:S(2)}, u32[]{:S(2)}) collective-permute-start(f32[8,128]{1,0:T(8,128)S(1)} %get-tuple-element.16.half), channel_id=1, source_target_pairs={{384,320},{320,384},{256,192},{192,256},{128,0},{0,128},{64,65},{6... | collective-permute-start | bytes 12296 | tf_op jit(solution)/shard_map/ppermute | solution.py:56
  40.8 5.4 %collective-permute-start.3 = (f32[8,128]{1,0:T(8,128)S(1)}, f32[8,128]{1,0:T(8,128)S(1)}, u32[]{:S(2)}, u32[]{:S(2)}) collective-permute-start(f32[8,128]{1,0:T(8,128)S(1)} %backward.3.values.w), channel_id=1, source_target_pairs={{384,320},{320,384},{256,192},{192,256},{128,0},{0,128},{64,65},{6... | collective-permute-start | bytes 12296 | tf_op jit(solution)/shard_map/ppermute | solution.py:56

commit v13 on v12

--- a/solution.py
+++ b/solution.py
@@ -21,7 +21,7 @@
 HBM = pl.BlockSpec(memory_space=pl.ANY)
 
 
-EVEN = (7, 6, 5, 4, 3, 2, 0, 1)
+EVEN = (1, 0, 2, 3, 4, 5, 6, 7)
 ODD = EVEN[::-1]
 
 

time: 77.4 us -> 76.8 us (level)
  starting transfers between devices: 8.2 us -> 2.63 us
  blocking collectives: 62 us -> 66.9 us
    psum x4, blocking collectives: 14.6 us -> 20.2 us  [neighbours(): return (lax.ppermute(values, ALL, FAR), lax.psum(values, 'wave_1'))]
    ppermute x4, starting transfers between devices: 8.2 us -> 2.63 us  [neighbours(): return (lax.ppermute(values, ALL, FAR), lax.psum(values, 'wave_1'))]
where the time goes in v13:
time: 76.8 us; the launch traced here: 76 us
  blocking collectives  66.9 us (87%)
  Pallas kernels  5.73 us (7%)
  starting transfers between devices  2.63 us (3%)
    all_to_all x3, blocking collectives, exchanged(): lax.all_to_all(values, ALL, split_axis=0, concat_axis=0, tiled=True, axis...  46.7 us
    psum x4, blocking collectives, neighbours(): return (lax.ppermute(values, ALL, FAR), lax.psum(values, 'wave_1'))  20.2 us
    pallas_call x11, Pallas kernels, call(): pl.pallas_call(kernel, out_shape=out, in_specs=[VMEM] * len(args), out_sp...  4.5 us
    ppermute x4, starting transfers between devices, neighbours(): return (lax.ppermute(values, ALL, FAR), lax.psum(values, 'wave_1'))  2.63 us
  transfers between devices with their start and end apart: 4, of which 0 were waited for; matrix products, arithmetic and copies ran while one was open for 0% of the time, Pallas kernels for 0%

profile of v13, /device:TPU:1, one launch (start us, length us, event | category | flops | bytes accessed | tf_op | source)
XLA Modules:
  0.0 76.0 jit_solution(9280991842200762384)
XLA Ops:
  0.6 1.2 %pack.1 = (f32[8,136,128]{2,1,0:T(8,128)S(1)}, f32[8,128]{1,0:T(8,128)S(1)}) custom-call(f32[1,8,128,128]{3,2,1,0:T(8,128)} %inverse.1, f32[1,8,128]{2,1,0:T(8,128)} %right.1, f32[1,8,128]{2,1,0:T(8,128)} %cz.1, f32[8,128]{1,0:T(8,128)} %cx.1, f32[1,128]{1,0:T(1,128)} %cy.1), custom_call_target="tpu_custom_call" | custom-call | tf_op jit(solution)/shard_map/pack/pallas_call | solution.py:106
  1.9 18.1 %all_to_all.15.columns = f32[8,136,128]{2,1,0:T(8,128)S(1)} all-to-all(f32[8,136,128]{2,1,0:T(8,128)S(1)} %get-tuple-element.10), channel_id=1, replica_groups={{320,384,448,0,64,128,192,256},{321,385,449,1,65,129,193,257},{322,386,..., dimensions={0} | all-to-all | bytes 1114112 | tf_op jit(solution)/shard_map/all_to_all | solution.py:60
  19.9 0.8 %first.1.half = f32[8,128]{1,0:T(8,128)S(1)} custom-call(f32[8,136,128]{2,1,0:T(8,128)S(1)} %all_to_all.15.columns), custom_call_target="tpu_custom_call" | custom-call | tf_op jit(solution)/shard_map/first/pallas_call | solution.py:243
  20.7 0.7 collective-permute-start
  21.4 0.1 settle_first.1
  21.5 5.6 %psum.28.both = f32[8,128]{1,0:T(8,128)S(1)} all-reduce(f32[8,128]{1,0:T(8,128)S(1)} %first.1.half), channel_id=1, replica_groups=mesh['wave_0'=4,'wave_1'=2,'plane_0'=4,'plane_1'=16] {'wave_1'}, use_global_device_ids=true, to_apply=%region_0.0 | all-reduce | flops 1024 | bytes 8192 | tf_op jit(solution)/shard_map/psum | solution.py:56
  27.1 0.0 collective-permute-done.far
  27.1 0.8 %backward.2.values.own.z = f32[8,128]{1,0:T(8,128)S(1)} custom-call(f32[8,136,128]{2,1,0:T(8,128)S(1)} %all_to_all.15.columns, f32[8,128]{1,0:T(8,128)S(1)} %get-tuple-element.12.base, f32[8,128]{1,0:T(8,128)S(1)} %psum.28.both, f32[8,128]{1,0:T(8,128)S(1)} %collective-permute-done.far, f32[8,128]{1,0:T(8,128)S(1)} %get-tuple-element.13.cy, ...), custom_call_target="tpu_custom_call" | custom-call | tf_op jit(solution)/shard_map/backward/pallas_call | solution.py:243
  27.9 0.7 collective-permute-start.1
  28.6 0.1 image_part.2.local
  28.6 5.0 %psum.29.both = f32[8,128]{1,0:T(8,128)S(1)} all-reduce(f32[8,128]{1,0:T(8,128)S(1)} %backward.2.values.own.z), channel_id=1, replica_groups=mesh['wave_0'=4,'wave_1'=2,'plane_0'=4,'plane_1'=16] {'wave_1'}, use_global_device_ids=true, to_apply=%region_1.0 | all-reduce | flops 1024 | bytes 8192 | tf_op jit(solution)/shard_map/psum | solution.py:56
  33.6 0.0 collective-permute-done.1.far
  33.7 0.8 %image.1 = (f32[8,128]{1,0:T(8,128)S(1)}, f32[8,128]{1,0:T(8,128)S(1)}) custom-call(f32[8,136,128]{2,1,0:T(8,128)S(1)} %all_to_all.15.columns, f32[8,128]{1,0:T(8,128)S(1)} %image_part.2.local, f32[8,128]{1,0:T(8,128)S(1)} %psum.29.both, f32[8,128]{1,0:T(8,128)S(1)} %collective-permute-done.1.far, f32[8,128]{1,0:T(8,128)S(1)} %get-tuple-element.13.cy, ...), custom_call_target="tpu_custom_call" | custom-call | tf_op jit(solution)/shard_map/image/pallas_call | solution.py:243
  34.4 0.7 collective-permute-start.2
  35.1 0.1 settle.1.base
  35.2 4.8 %psum.30.both = f32[8,128]{1,0:T(8,128)S(1)} all-reduce(f32[8,128]{1,0:T(8,128)S(1)} %get-tuple-element.16.half), channel_id=1, replica_groups=mesh['wave_0'=4,'wave_1'=2,'plane_0'=4,'plane_1'=16] {'wave_1'}, use_global_device_ids=true, to_apply=%region_2.0 | all-reduce | flops 1024 | bytes 8192 | tf_op jit(solution)/shard_map/psum | solution.py:56
  39.9 0.8 %backward.3.values.w = f32[8,128]{1,0:T(8,128)S(1)} custom-call(f32[8,136,128]{2,1,0:T(8,128)S(1)} %all_to_all.15.columns, f32[8,128]{1,0:T(8,128)S(1)} %settle.1.base, f32[8,128]{1,0:T(8,128)S(1)} %psum.30.both, f32[8,128]{1,0:T(8,128)S(1)} %collective-permute-done.2.far, f32[8,128]{1,0:T(8,128)S(1)} %get-tuple-element.13.cy, ...), custom_call_target="tpu_custom_call" | custom-call | tf_op jit(solution)/shard_map/backward/pallas_call | solution.py:243
  40.7 0.1 image_part.3.local
  40.8 0.7 collective-permute-start.3
  41.5 4.8 %psum.31.both = f32[8,128]{1,0:T(8,128)S(1)} all-reduce(f32[8,128]{1,0:T(8,128)S(1)} %backward.3.values.w), channel_id=1, replica_groups=mesh['wave_0'=4,'wave_1'=2,'plane_0'=4,'plane_1'=16] {'wave_1'}, use_global_device_ids=true, to_apply=%region_3.0 | all-reduce | flops 1024 | bytes 8192 | tf_op jit(solution)/shard_map/psum | solution.py:56
  46.3 0.1 sums.1
  46.4 15.9 %all_to_all.16.back = f32[32,8,128]{2,1,0:T(8,128)S(1)} all-to-all(f32[32,8,128]{2,1,0:T(8,128)S(1)} %sums.1), channel_id=1, replica_groups={{352,416,480,32,96,160,224,288,368,432,496,48,112,176,240,304,320,384,4..., dimensions={0} | all-to-all | bytes 262144 | tf_op jit(solution)/shard_map/all_to_all | solution.py:60
  62.3 12.8 %all_to_all.17.everyone = f32[16,1,128]{2,1,0:T(1,128)S(1)} all-to-all(f32[16,1,128]{2,1,0:T(1,128)S(1)} %share.1), channel_id=1, replica_groups={{8,9,10,11,12,13,14,15,0,1,2,3,4,5,6,7},{24,25,26,27,28,29,30,31,16,17,..., dimensions={0} | all-to-all | bytes 16384 | tf_op jit(solution)/shard_map/all_to_all | solution.py:60
  75.1 0.9 %final.1 = (f32[1,8,128]{2,1,0:T(8,128)}, f32[1,8,128]{2,1,0:T(8,128)}) custom-call(f32[16,1,128]{2,1,0:T(1,128)S(1)} %all_to_all.17.everyone, f32[32,8,128]{2,1,0:T(8,128)S(1)} %all_to_all.16.back, f32[8,128]{1,0:T(8,128)S(1)} %get-tuple-element.17.r), custom_call_target="tpu_custom_call" | custom-call | tf_op jit(solution)/shard_map/final/pallas_call | solution.py:243
  (3 shorter events, 0.0 us)
Async XLA Ops:
  20.7 6.4 %collective-permute-start = (f32[8,128]{1,0:T(8,128)S(1)}, f32[8,128]{1,0:T(8,128)S(1)}, u32[]{:S(2)}, u32[]{:S(2)}) collective-permute-start(f32[8,128]{1,0:T(8,128)S(1)} %first.1.half), channel_id=1, source_target_pairs={{0,128},{128,0},{192,256},{256,192},{320,384},{384,320},{448,449},... | collective-permute-start | bytes 12296 | tf_op jit(solution)/shard_map/ppermute | solution.py:56
  27.9 5.8 %collective-permute-start.1 = (f32[8,128]{1,0:T(8,128)S(1)}, f32[8,128]{1,0:T(8,128)S(1)}, u32[]{:S(2)}, u32[]{:S(2)}) collective-permute-start(f32[8,128]{1,0:T(8,128)S(1)} %backward.2.values.own.z), channel_id=1, source_target_pairs={{0,128},{128,0},{192,256},{256,192},{320,384},{384,320},{448,449},... | collective-permute-start | bytes 12296 | tf_op jit(solution)/shard_map/ppermute | solution.py:56
  34.4 5.5 %collective-permute-start.2 = (f32[8,128]{1,0:T(8,128)S(1)}, f32[8,128]{1,0:T(8,128)S(1)}, u32[]{:S(2)}, u32[]{:S(2)}) collective-permute-start(f32[8,128]{1,0:T(8,128)S(1)} %get-tuple-element.16.half), channel_id=1, source_target_pairs={{0,128},{128,0},{192,256},{256,192},{320,384},{384,320},{448,449},... | collective-permute-start | bytes 12296 | tf_op jit(solution)/shard_map/ppermute | solution.py:56
  40.8 5.4 %collective-permute-start.3 = (f32[8,128]{1,0:T(8,128)S(1)}, f32[8,128]{1,0:T(8,128)S(1)}, u32[]{:S(2)}, u32[]{:S(2)}) collective-permute-start(f32[8,128]{1,0:T(8,128)S(1)} %backward.3.values.w), channel_id=1, source_target_pairs={{0,128},{128,0},{192,256},{256,192},{320,384},{384,320},{448,449},... | collective-permute-start | bytes 12296 | tf_op jit(solution)/shard_map/ppermute | solution.py:56

commit v14 on v13

--- a/solution.py
+++ b/solution.py
@@ -125,13 +125,13 @@
 
 
 def forward(columns, source, out):
-    cx = columns[0, CX : CX + 1, :]
+    cx = relax * columns[0, CX : CX + 1, :]
     previous = None
     for x in range(NW):
-        s = source(x)
+        s = relax * source(x)
         if previous is not None:
             s = s + cx * previous
-        previous = relax * times_block(columns, x, s)
+        previous = times_block(columns, x, s)
         out[x : x + 1, :] = previous
 
 
@@ -188,14 +188,14 @@
 
 
 def backward_kernel(columns, base, both, far, cy, half, out):
-    source = base[...] + cy[...] * (far[...] + (both[...] - half[...]))
-    cx = columns[0, CX : CX + 1, :]
+    source = relax * (base[...] + cy[...] * (far[...] + (both[...] - half[...])))
+    cx = relax * columns[0, CX : CX + 1, :]
     previous = None
     for x in reversed(range(NW)):
         s = source[x : x + 1]
         if previous is not None:
             s = s + cx * previous
-        previous = half[x : x + 1, :] + relax * times_block(columns, x, s)
+        previous = half[x : x + 1, :] + times_block(columns, x, s)
         out[x : x + 1, :] = previous
 
 

time: 76.8 us -> 76.8 us (level)
  no operation moved by 1% of the time
where the time goes in v14:
time: 76.8 us; the launch traced here: 76 us
  blocking collectives  66.9 us (87%)
  Pallas kernels  5.69 us (7%)
  starting transfers between devices  2.64 us (3%)
    all_to_all x3, blocking collectives, exchanged(): lax.all_to_all(values, ALL, split_axis=0, concat_axis=0, tiled=True, axis...  46.7 us
    psum x4, blocking collectives, neighbours(): return (lax.ppermute(values, ALL, FAR), lax.psum(values, 'wave_1'))  20.2 us
    pallas_call x11, Pallas kernels, call(): pl.pallas_call(kernel, out_shape=out, in_specs=[VMEM] * len(args), out_sp...  4.46 us
    ppermute x4, starting transfers between devices, neighbours(): return (lax.ppermute(values, ALL, FAR), lax.psum(values, 'wave_1'))  2.64 us
  transfers between devices with their start and end apart: 4, of which 0 were waited for; matrix products, arithmetic and copies ran while one was open for 0% of the time, Pallas kernels for 0%

profile of v14, /device:TPU:1, one launch (start us, length us, event | category | flops | bytes accessed | tf_op | source)
XLA Modules:
  0.0 76.0 jit_solution(10135835949956290953)
XLA Ops:
  0.6 1.2 %pack.1 = (f32[8,136,128]{2,1,0:T(8,128)S(1)}, f32[8,128]{1,0:T(8,128)S(1)}) custom-call(f32[1,8,128,128]{3,2,1,0:T(8,128)} %inverse.1, f32[1,8,128]{2,1,0:T(8,128)} %right.1, f32[1,8,128]{2,1,0:T(8,128)} %cz.1, f32[8,128]{1,0:T(8,128)} %cx.1, f32[1,128]{1,0:T(1,128)} %cy.1), custom_call_target="tpu_custom_call" | custom-call | tf_op jit(solution)/shard_map/pack/pallas_call | solution.py:106
  1.9 18.1 %all_to_all.15.columns = f32[8,136,128]{2,1,0:T(8,128)S(1)} all-to-all(f32[8,136,128]{2,1,0:T(8,128)S(1)} %get-tuple-element.10), channel_id=1, replica_groups={{320,384,448,0,64,128,192,256},{321,385,449,1,65,129,193,257},{322,386,..., dimensions={0} | all-to-all | bytes 1114112 | tf_op jit(solution)/shard_map/all_to_all | solution.py:60
  19.9 0.8 %first.1.half = f32[8,128]{1,0:T(8,128)S(1)} custom-call(f32[8,136,128]{2,1,0:T(8,128)S(1)} %all_to_all.15.columns), custom_call_target="tpu_custom_call" | custom-call | tf_op jit(solution)/shard_map/first/pallas_call | solution.py:243
  20.7 0.7 collective-permute-start
  21.4 0.1 settle_first.1
  21.4 5.6 %psum.28.both = f32[8,128]{1,0:T(8,128)S(1)} all-reduce(f32[8,128]{1,0:T(8,128)S(1)} %first.1.half), channel_id=1, replica_groups=mesh['wave_0'=4,'wave_1'=2,'plane_0'=4,'plane_1'=16] {'wave_1'}, use_global_device_ids=true, to_apply=%region_0.0 | all-reduce | flops 1024 | bytes 8192 | tf_op jit(solution)/shard_map/psum | solution.py:56
  27.1 0.0 collective-permute-done.far
  27.1 0.8 %backward.2.values.own.z = f32[8,128]{1,0:T(8,128)S(1)} custom-call(f32[8,136,128]{2,1,0:T(8,128)S(1)} %all_to_all.15.columns, f32[8,128]{1,0:T(8,128)S(1)} %get-tuple-element.12.base, f32[8,128]{1,0:T(8,128)S(1)} %psum.28.both, f32[8,128]{1,0:T(8,128)S(1)} %collective-permute-done.far, f32[8,128]{1,0:T(8,128)S(1)} %get-tuple-element.13.cy, ...), custom_call_target="tpu_custom_call" | custom-call | tf_op jit(solution)/shard_map/backward/pallas_call | solution.py:243
  27.9 0.7 collective-permute-start.1
  28.5 0.1 image_part.2.local
  28.6 5.0 %psum.29.both = f32[8,128]{1,0:T(8,128)S(1)} all-reduce(f32[8,128]{1,0:T(8,128)S(1)} %backward.2.values.own.z), channel_id=1, replica_groups=mesh['wave_0'=4,'wave_1'=2,'plane_0'=4,'plane_1'=16] {'wave_1'}, use_global_device_ids=true, to_apply=%region_1.0 | all-reduce | flops 1024 | bytes 8192 | tf_op jit(solution)/shard_map/psum | solution.py:56
  33.6 0.0 collective-permute-done.1.far
  33.6 0.8 %image.1 = (f32[8,128]{1,0:T(8,128)S(1)}, f32[8,128]{1,0:T(8,128)S(1)}) custom-call(f32[8,136,128]{2,1,0:T(8,128)S(1)} %all_to_all.15.columns, f32[8,128]{1,0:T(8,128)S(1)} %image_part.2.local, f32[8,128]{1,0:T(8,128)S(1)} %psum.29.both, f32[8,128]{1,0:T(8,128)S(1)} %collective-permute-done.1.far, f32[8,128]{1,0:T(8,128)S(1)} %get-tuple-element.13.cy, ...), custom_call_target="tpu_custom_call" | custom-call | tf_op jit(solution)/shard_map/image/pallas_call | solution.py:243
  34.4 0.7 collective-permute-start.2
  35.1 0.1 settle.1.base
  35.2 4.8 %psum.30.both = f32[8,128]{1,0:T(8,128)S(1)} all-reduce(f32[8,128]{1,0:T(8,128)S(1)} %get-tuple-element.16.half), channel_id=1, replica_groups=mesh['wave_0'=4,'wave_1'=2,'plane_0'=4,'plane_1'=16] {'wave_1'}, use_global_device_ids=true, to_apply=%region_2.0 | all-reduce | flops 1024 | bytes 8192 | tf_op jit(solution)/shard_map/psum | solution.py:56
  39.9 0.8 %backward.3.values.w = f32[8,128]{1,0:T(8,128)S(1)} custom-call(f32[8,136,128]{2,1,0:T(8,128)S(1)} %all_to_all.15.columns, f32[8,128]{1,0:T(8,128)S(1)} %settle.1.base, f32[8,128]{1,0:T(8,128)S(1)} %psum.30.both, f32[8,128]{1,0:T(8,128)S(1)} %collective-permute-done.2.far, f32[8,128]{1,0:T(8,128)S(1)} %get-tuple-element.13.cy, ...), custom_call_target="tpu_custom_call" | custom-call | tf_op jit(solution)/shard_map/backward/pallas_call | solution.py:243
  40.7 0.1 image_part.3.local
  40.8 0.7 collective-permute-start.3
  41.4 4.8 %psum.31.both = f32[8,128]{1,0:T(8,128)S(1)} all-reduce(f32[8,128]{1,0:T(8,128)S(1)} %backward.3.values.w), channel_id=1, replica_groups=mesh['wave_0'=4,'wave_1'=2,'plane_0'=4,'plane_1'=16] {'wave_1'}, use_global_device_ids=true, to_apply=%region_3.0 | all-reduce | flops 1024 | bytes 8192 | tf_op jit(solution)/shard_map/psum | solution.py:56
  46.2 0.1 sums.1
  46.3 15.9 %all_to_all.16.back = f32[32,8,128]{2,1,0:T(8,128)S(1)} all-to-all(f32[32,8,128]{2,1,0:T(8,128)S(1)} %sums.1), channel_id=1, replica_groups={{352,416,480,32,96,160,224,288,368,432,496,48,112,176,240,304,320,384,4..., dimensions={0} | all-to-all | bytes 262144 | tf_op jit(solution)/shard_map/all_to_all | solution.py:60
  62.2 12.8 %all_to_all.17.everyone = f32[16,1,128]{2,1,0:T(1,128)S(1)} all-to-all(f32[16,1,128]{2,1,0:T(1,128)S(1)} %share.1), channel_id=1, replica_groups={{8,9,10,11,12,13,14,15,0,1,2,3,4,5,6,7},{24,25,26,27,28,29,30,31,16,17,..., dimensions={0} | all-to-all | bytes 16384 | tf_op jit(solution)/shard_map/all_to_all | solution.py:60
  75.1 0.9 %final.1 = (f32[1,8,128]{2,1,0:T(8,128)}, f32[1,8,128]{2,1,0:T(8,128)}) custom-call(f32[16,1,128]{2,1,0:T(1,128)S(1)} %all_to_all.17.everyone, f32[32,8,128]{2,1,0:T(8,128)S(1)} %all_to_all.16.back, f32[8,128]{1,0:T(8,128)S(1)} %get-tuple-element.17.r), custom_call_target="tpu_custom_call" | custom-call | tf_op jit(solution)/shard_map/final/pallas_call | solution.py:243
  (3 shorter events, 0.0 us)
Async XLA Ops:
  20.7 6.4 %collective-permute-start = (f32[8,128]{1,0:T(8,128)S(1)}, f32[8,128]{1,0:T(8,128)S(1)}, u32[]{:S(2)}, u32[]{:S(2)}) collective-permute-start(f32[8,128]{1,0:T(8,128)S(1)} %first.1.half), channel_id=1, source_target_pairs={{0,128},{128,0},{192,256},{256,192},{320,384},{384,320},{448,449},... | collective-permute-start | bytes 12296 | tf_op jit(solution)/shard_map/ppermute | solution.py:56
  27.9 5.8 %collective-permute-start.1 = (f32[8,128]{1,0:T(8,128)S(1)}, f32[8,128]{1,0:T(8,128)S(1)}, u32[]{:S(2)}, u32[]{:S(2)}) collective-permute-start(f32[8,128]{1,0:T(8,128)S(1)} %backward.2.values.own.z), channel_id=1, source_target_pairs={{0,128},{128,0},{192,256},{256,192},{320,384},{384,320},{448,449},... | collective-permute-start | bytes 12296 | tf_op jit(solution)/shard_map/ppermute | solution.py:56
  34.4 5.5 %collective-permute-start.2 = (f32[8,128]{1,0:T(8,128)S(1)}, f32[8,128]{1,0:T(8,128)S(1)}, u32[]{:S(2)}, u32[]{:S(2)}) collective-permute-start(f32[8,128]{1,0:T(8,128)S(1)} %get-tuple-element.16.half), channel_id=1, source_target_pairs={{0,128},{128,0},{192,256},{256,192},{320,384},{384,320},{448,449},... | collective-permute-start | bytes 12296 | tf_op jit(solution)/shard_map/ppermute | solution.py:56
  40.8 5.4 %collective-permute-start.3 = (f32[8,128]{1,0:T(8,128)S(1)}, f32[8,128]{1,0:T(8,128)S(1)}, u32[]{:S(2)}, u32[]{:S(2)}) collective-permute-start(f32[8,128]{1,0:T(8,128)S(1)} %backward.3.values.w), channel_id=1, source_target_pairs={{0,128},{128,0},{192,256},{256,192},{320,384},{384,320},{448,449},... | collective-permute-start | bytes 12296 | tf_op jit(solution)/shard_map/ppermute | solution.py:56
